TPU v7x, 128 devices: a whole 4x4x4 slice. The times are simulated.
128 devices in a mesh: seq: 16 (over z, y_lo, core), tensor: 8 (over y_hi, x).
Axes of the slice: x: 4, y: 4 (y_hi: 2, y_lo: 2; y = y_hi * 2 + y_lo), z: 4, core: 2. Of those that a mesh axis runs over, the one named last changes fastest.
Arguments:
- queries: bfloat16 [12288, 4096], P('seq', 'tensor'), may hold values from -12 to 12
- keys: bfloat16 [12288, 1024], P('seq', 'tensor'), may hold values from -12 to 12
- values: bfloat16 [12288, 1024], P('seq', 'tensor'), may hold values from -6 to 6
- out_weight: bfloat16 [4096, 4096], P('tensor'), may hold values from -0.09375 to 0.09375
- out_grad: bfloat16 [12288, 4096], P('seq', 'tensor'), may hold values from -6 to 6
- doc_ids: int32 [12288], P('seq'), may hold values from 0 to 7, never falling along the last dimension, each value on 1 to 3072 neighbouring positions
Outputs:
- grad_queries: bfloat16 [12288, 4096], P('seq', 'tensor')
- grad_keys: bfloat16 [12288, 1024], P('seq', 'tensor')
- grad_values: bfloat16 [12288, 1024], P('seq', 'tensor')
- grad_out_weight: bfloat16 [4096, 4096], P('tensor', 'seq')
Inputs may be any that keep to these rules, and one draw needn't show every extreme that they name: `doc_ids`: document numbers never fall along the sequence; a document holds 1 to 3072 tokens and one holds exactly that many.
All inputs are finite; a program needn't handle non-finite values.
Results may differ from a plain program's by a relative error of at most 0.015.
Values may be sent and summed in bfloat16 or wider, within the bound.
No kernel may reach another device: no remote copies, remote signals or barrier semaphores. Data moves between devices by JAX's collectives and lax.ppermute only.
A program may use at most 128 MiB of HBM per device.

v0:
```python
import math

import jax
import jax.numpy as jnp
from jax import lax
from jax.experimental import pallas as pl
from jax.experimental.pallas import tpu as pltpu
from jax.sharding import PartitionSpec as P

HEAD_SIZE = 128
NEG_BIG = -1e30
ROWS = 256


def shifted(value, axis, steps):
    count = lax.axis_size(axis)
    initial, last = (max(0, -steps), min(count, count - steps))
    return lax.ppermute(value, axis, [(source, source + steps) for source in range(initial, last)])


def contract_rows(left, right):
    return lax.dot_general(
        left, right, (((0,), (0,)), ((), ())), preferred_element_type=jnp.float32
    )


def contract_last(left, right):
    return lax.dot_general(
        left, right, (((1,), (1,)), ((), ())), preferred_element_type=jnp.float32
    )


def gather_keys(parts, key_all, value_all, tok):
    for index, part in enumerate(parts):
        rows = pl.ds(index * tok, tok)
        key_all[rows, :] = part[pl.ds(0, tok), :]
        value_all[rows, :] = part[pl.ds(tok, tok), :]


def first_step():
    return (pl.program_id(0) == 0) & (pl.program_id(1) == 0)


def forward_kernel(tok, span, low_ref, q_ref, far_ref, near_ref, own_ref, probs_ref, attn_ref, key_all, value_all):
    @pl.when(first_step())
    def _():
        gather_keys((far_ref, near_ref, own_ref), key_all, value_all, tok)

    block = pl.program_id(0)
    begin = pl.multiple_of(block * ROWS, ROWS)
    keys = key_all[pl.ds(begin, span), :]
    values = value_all[pl.ds(begin, span), :]
    raw = contract_last(q_ref[...], keys)
    key_at = lax.broadcasted_iota(jnp.int32, (ROWS, span), 1)
    row_at = lax.broadcasted_iota(jnp.int32, (ROWS, 1), 0)
    visible = (key_at >= low_ref[...] - begin) & (key_at <= row_at + 2 * tok)
    masked = jnp.where(visible, raw, NEG_BIG)
    top = jnp.max(masked, axis=1, keepdims=True)
    expo = jnp.exp2((masked - top) * (math.log2(math.e) / math.sqrt(HEAD_SIZE)))
    total = jnp.sum(expo, axis=1, keepdims=True)
    probs_low = (expo * (1.0 / total)).astype(jnp.bfloat16)
    probs_ref[0] = probs_low
    attn_ref[...] = jnp.dot(probs_low, values, preferred_element_type=jnp.float32).astype(jnp.bfloat16)


def backward_kernel(
    tok, span, q_ref, grad_ref, attn_ref, probs_ref, far_ref, near_ref, own_ref,
    gq_ref, far_out, near_out, own_out, key_all, value_all, key_sum, value_sum,
):
    scale = 1.0 / math.sqrt(HEAD_SIZE)

    @pl.when(first_step())
    def _():
        gather_keys((far_ref, near_ref, own_ref), key_all, value_all, tok)
        key_sum[...] = jnp.zeros_like(key_sum)
        value_sum[...] = jnp.zeros_like(value_sum)

    begin = pl.multiple_of(pl.program_id(0) * ROWS, ROWS)
    window = pl.ds(begin, span)
    grad = grad_ref[...]
    delta = jnp.sum(grad.astype(jnp.float32) * attn_ref[...].astype(jnp.float32), axis=1, keepdims=True)
    d_prob = contract_last(grad, value_all[window, :])
    probs = probs_ref[0]
    d_score = (probs.astype(jnp.float32) * (d_prob - delta)).astype(jnp.bfloat16)
    gq = jnp.dot(d_score, key_all[window, :], preferred_element_type=jnp.float32)
    gq_ref[...] = (gq * scale).astype(jnp.bfloat16)
    key_sum[window, :] += contract_rows(d_score, q_ref[...])
    value_sum[window, :] += contract_rows(probs, grad)

    @pl.when((pl.program_id(0) == pl.num_programs(0) - 1) & (pl.program_id(1) == pl.num_programs(1) - 1))
    def _():
        for index, out in enumerate((far_out, near_out, own_out)):
            rows = pl.ds(index * tok, tok)
            out[pl.ds(0, tok), :] = (key_sum[rows, :] * scale).astype(out.dtype)
            out[pl.ds(tok, tok), :] = value_sum[rows, :].astype(out.dtype)


def whole():
    return pl.BlockSpec(memory_space=pltpu.VMEM)


def local(queries, keys, values, out_weight, out_grad, doc_ids):
    tok = queries.shape[0]
    heads = queries.shape[1] // HEAD_SIZE
    blocks = tok // ROWS
    span = 2 * tok + ROWS
    shard = lax.axis_index("seq")
    docs = jnp.pad(doc_ids.astype(jnp.bfloat16).reshape(tok // HEAD_SIZE, HEAD_SIZE), ((0, 16 - tok // HEAD_SIZE), (0, 0)))
    own = jnp.concatenate([keys, values, docs], axis=0)
    far, near = shifted(own, "seq", 2), shifted(own, "seq", 1)
    doc_of = lambda part: part[2 * tok : 2 * tok + tok // HEAD_SIZE].reshape(tok).astype(jnp.int32)
    doc_keys = jnp.concatenate([
        jnp.where(shard >= 2, doc_of(far), -1), jnp.where(shard >= 1, doc_of(near), -1), doc_ids
    ])
    earlier = jnp.sum((doc_keys[None, :] < doc_ids[:, None]).astype(jnp.int32), axis=1)
    low = jnp.maximum(earlier, jnp.arange(tok, dtype=jnp.int32) + 1)[:, None]

    head_block = pl.BlockSpec((ROWS, HEAD_SIZE), lambda b, h: (b, h))
    probs_block = pl.BlockSpec((1, ROWS, span), lambda b, h: (h, b, 0))
    held = [pltpu.VMEM((3 * tok, HEAD_SIZE), jnp.bfloat16)] * 2
    work = heads * tok * span * HEAD_SIZE * 2
    probs, attn = pl.pallas_call(
        lambda *refs: forward_kernel(tok, span, *refs),
        grid=(blocks, heads),
        in_specs=[pl.BlockSpec((ROWS, 1), lambda b, h: (b, 0)), head_block, whole(), whole(), whole()],
        out_specs=[probs_block, head_block],
        out_shape=[
            jax.ShapeDtypeStruct((heads, tok, span), jnp.bfloat16),
            jax.ShapeDtypeStruct((tok, heads * HEAD_SIZE), jnp.bfloat16),
        ],
        scratch_shapes=held,
        compiler_params=pltpu.CompilerParams(vmem_limit_bytes=40 << 20),
        cost_estimate=pl.CostEstimate(flops=2 * work, bytes_accessed=14 << 20, transcendentals=heads * tok * span),
        name="forward",
    )(low, queries, far, near, own)

    grad_full = lax.all_gather(out_grad, "tensor", axis=1, tiled=True)
    weight_part = contract_rows(grad_full, attn)
    summed = lax.psum_scatter(weight_part.astype(jnp.bfloat16), "seq", scatter_dimension=0, tiled=True)
    weight_grad = summed.T
    attention_gradient = contract_last(grad_full, out_weight).astype(jnp.bfloat16)

    pair = lambda dtype: jax.ShapeDtypeStruct((2 * tok, HEAD_SIZE), dtype)
    grad_queries, far_sum, near_sum, own_sum = pl.pallas_call(
        lambda *refs: backward_kernel(tok, span, *refs),
        grid=(blocks, heads),
        in_specs=[head_block, head_block, head_block, probs_block, whole(), whole(), whole()],
        out_specs=[head_block, whole(), whole(), whole()],
        out_shape=[
            jax.ShapeDtypeStruct((tok, heads * HEAD_SIZE), jnp.bfloat16),
            pair(jnp.bfloat16), pair(jnp.bfloat16), pair(jnp.float32),
        ],
        scratch_shapes=held + [pltpu.VMEM((3 * tok, HEAD_SIZE), jnp.float32)] * 2,
        compiler_params=pltpu.CompilerParams(vmem_limit_bytes=40 << 20),
        cost_estimate=pl.CostEstimate(flops=4 * work, bytes_accessed=14 << 20, transcendentals=0),
        name="backward",
    )(queries, attention_gradient, attn, probs, far, near, own)
    total = own_sum + shifted(far_sum, "seq", -2).astype(jnp.float32) + shifted(near_sum, "seq", -1).astype(jnp.float32)
    total = total.astype(jnp.bfloat16)
    return (grad_queries, total[:tok], total[tok:], weight_grad)


def solution(mesh):
    placed = (
        P("seq", "tensor"),
        P("seq", "tensor"),
        P("seq", "tensor"),
        P("tensor", None),
        P("seq", "tensor"),
        P("seq"),
    )
    return jax.shard_map(
        local,
        mesh=mesh,
        in_specs=placed,
        out_specs=(P("seq", "tensor"), P("seq", "tensor"), P("seq", "tensor"), P("tensor", "seq")),
        check_vma=False,
    )
```

profile of v0, /device:TPU:0, one launch (start us, length us, event | category | flops | bytes accessed | tf_op | source)
XLA Modules:
  0.0 202.7 jit_solution(3542333868800539788)
XLA Ops:
  7.2 0.0 all-gather.2.cloned.1.call-start
  7.2 0.7 all-gather.2.cloned.1.call-update
  7.9 0.0 reduce-scatter.2.cloned.1.call-start
  7.9 0.7 convert_bitcast_fusion
  8.6 1.0 fusion.2.refs_4_.refs_6_
  9.7 1.3 collective-permute-start.1
  11.0 4.2 %collective-permute-start = (bf16[1552,128]{1,0:T(8,128)(2,1)S(1)}, bf16[1552,128]{1,0:T(8,128)(2,1)S(1)}, u32[]{:S(2)}, u32[]{:S(2)}) collective-permute-start(bf16[1552,128]{1,0:T(8,128)(2,1)S(1)} %fusion.2.refs_4_.refs_6_), channel_id=1, source_target_pairs={{0,16},{8,24},{16,32},{24,40},{32,48},{40,56},{48,64},{56,72},{64,... | collective-permute-start | bytes 1191944 | tf_op jit(solution)/shard_map/ppermute | solution.py:18
  15.2 0.0 collective-permute-done.1.refs_3_.refs_5_
  15.2 10.5 %collective-permute-done.refs_2_.refs_4_ = bf16[1552,128]{1,0:T(8,128)(2,1)S(1)} collective-permute-done((bf16[1552,128]{1,0:T(8,128)(2,1)S(1)}, bf16[1552,128]{1,0:T(8,128)(2,1)S(1)}, u32[]{:S(2)}, u32[]{:S(2)}) %collective-permute-start) | collective-permute-done | bytes 397344 | tf_op jit(solution)/shard_map/ppermute | solution.py:18
  25.8 0.7 pad_add_fusion
  26.5 1.5 convert_reduce_fusion
  28.0 0.2 reshape_maximum_fusion.refs_0_
  28.2 0.0 copy-start
  28.2 1.1 copy-done
  29.3 17.1 %forward.1 = (bf16[4,768,1792]{2,1,0:T(8,128)(2,1)S(1)}, bf16[768,512]{1,0:T(8,128)(2,1)S(1)}) custom-call(s32[768,1]{1,0:T(8,128)S(1)} %reshape_maximum_fusion.refs_0_, bf16[768,512]{1,0:T(8,128)(2,1)S(1)} %copy-done, bf16[1552,128]{1,0:T(8,128)(2,1)S(1)} %collective-permute-done.refs_2_.refs_4_, ...), custom_call_target="tpu_custom_call" | custom-call | flops 2818572288 | bytes 14680064 | tf_op jit(solution)/shard_map/forward/pallas_call | solution.py:122
  46.5 0.0 copy-start.2
  46.5 4.2 %copy-done.2 = bf16[4,768,1792]{2,1,0:T(8,128)(2,1)} copy-done((bf16[4,768,1792]{2,1,0:T(8,128)(2,1)}, bf16[4,768,1792]{2,1,0:T(8,128)(2,1)S(1)}, u32[]{:S(2)}) %copy-start.2) | copy-done | bytes 11010072
  50.6 62.6 %all-gather.2.cloned.1.call-done = bf16[768,4096]{1,0:T(8,128)(2,1)} async-done(((bf16[768,512]{1,0:T(8,128)(2,1)}), bf16[768,4096]{1,0:T(8,128)(2,1)}) %all-gather.2.cloned.1.call-update) | async-done | bytes 6291472 | tf_op jit(solution)/shard_map/all_gather | solution.py:137
  113.2 7.8 %fusion = bf16[4096,512]{0,1:T(8,128)(2,1)} fusion(bf16[768,512]{1,0:T(8,128)(2,1)S(1)} %get-tuple-element.10.refs_2_, bf16[768,4096]{1,0:T(8,128)(2,1)} %all-gather.2.cloned.1.call-done), kind=kOutput, calls=%fused_computation.2 | convolution fusion | flops 3223322624 | bytes 11272192 | tf_op jit(solution)/shard_map/dot_general | solution.py:22
  121.0 0.0 reduce-scatter.2.cloned.1.call-update
  121.1 0.0 copy-start.1
  121.1 7.5 %convolution_convert_fusion.1.refs_1_ = bf16[768,512]{1,0:T(8,128)(2,1)S(1)} fusion(bf16[768,4096]{1,0:T(8,128)(2,1)} %all-gather.2.cloned.1.call-done, bf16[512,4096]{1,0:T(8,128)(2,1)} %param.9), kind=kOutput, calls=%fused_computation.3 | convolution fusion | flops 3221618688 | bytes 11272192 | tf_op jit(solution)/shard_map/dot_general | solution.py:28
  128.6 0.0 copy-done.1
  128.6 16.9 %backward.1 = (bf16[768,512]{1,0:T(8,128)(2,1)}, bf16[1536,128]{1,0:T(8,128)(2,1)S(1)}, bf16[1536,128]{1,0:T(8,128)(2,1)S(1)}, f32[1536,128]{1,0:T(8,128)S(1)}) custom-call(bf16[768,512]{1,0:T(8,128)(2,1)S(1)} %copy-done.1, bf16[768,512]{1,0:T(8,128)(2,1)S(1)} %convolution_convert_fusion.1.refs_1_, bf16[768,512]{1,0:T(8,128)(2,1)S(1)} %get-tuple-element.10.refs_2_, ...), custom_call_target="tpu_custom_call" | custom-call | flops 5637144576 | bytes 14680064 | tf_op jit(solution)/shard_map/backward/pallas_call | solution.py:144
  145.5 1.3 collective-permute-start.2
  146.8 1.3 collective-permute-start.3
  148.1 19.1 %collective-permute-done.2 = bf16[1536,128]{1,0:T(8,128)(2,1)S(1)} collective-permute-done((bf16[1536,128]{1,0:T(8,128)(2,1)S(1)}, bf16[1536,128]{1,0:T(8,128)(2,1)S(1)}, u32[]{:S(2)}, u32[]{:S(2)}) %collective-permute-start.2) | collective-permute-done | bytes 393248 | tf_op jit(solution)/shard_map/ppermute | solution.py:18
  167.2 0.0 collective-permute-done.3
  167.2 0.1 add_convert_fusion
  167.3 0.8 fusion.3
  168.1 27.8 %reduce-scatter.2.cloned.1.call-done = bf16[256,512]{0,1:T(8,128)(2,1)} async-done(((bf16[4096,512]{0,1:T(8,128)(2,1)}), bf16[256,512]{0,1:T(8,128)(2,1)}) %reduce-scatter.2.cloned.1.call-update) | async-done | bytes 262160 | tf_op jit(solution)/shard_map/reduce_scatter | solution.py:139
  (2 shorter events, 0.0 us)
Async XLA Ops:
  7.2 106.1 %all-gather.2.cloned.1.call-start = ((), (), s32[]{:S(2)}) async-start(), calls=%async_computation.1 | async-start | bytes 7077888 | tf_op jit(solution)/shard_map/all_gather | solution.py:137
  7.9 188.0 %reduce-scatter.2.cloned.1.call-start = ((), (), s32[]{:S(2)}) async-start(), calls=%async_computation.2 | async-start | bytes 4456448 | tf_op jit(solution)/shard_map/reduce_scatter | solution.py:139
  9.7 5.5 %collective-permute-start.1 = (bf16[1552,128]{1,0:T(8,128)(2,1)S(1)}, bf16[1552,128]{1,0:T(8,128)(2,1)S(1)}, u32[]{:S(2)}, u32[]{:S(2)}) collective-permute-start(bf16[1552,128]{1,0:T(8,128)(2,1)S(1)} %fusion.2.refs_4_.refs_6_), channel_id=1, source_target_pairs={{0,8},{8,16},{16,24},{24,32},{32,40},{40,48},{48,56},{56,64},{64,7... | collective-permute-start | bytes 1191944 | tf_op jit(solution)/shard_map/ppermute | solution.py:18
  11.0 14.8 %collective-permute-start = (bf16[1552,128]{1,0:T(8,128)(2,1)S(1)}, bf16[1552,128]{1,0:T(8,128)(2,1)S(1)}, u32[]{:S(2)}, u32[]{:S(2)}) collective-permute-start(bf16[1552,128]{1,0:T(8,128)(2,1)S(1)} %fusion.2.refs_4_.refs_6_), channel_id=1, source_target_pairs={{0,16},{8,24},{16,32},{24,40},{32,48},{40,56},{48,64},{56,72},{64,... | collective-permute-start | bytes 1191944 | tf_op jit(solution)/shard_map/ppermute | solution.py:18
  28.2 1.1 copy-start
  46.5 4.2 %copy-start.2 = (bf16[4,768,1792]{2,1,0:T(8,128)(2,1)}, bf16[4,768,1792]{2,1,0:T(8,128)(2,1)S(1)}, u32[]{:S(2)}) copy-start(bf16[4,768,1792]{2,1,0:T(8,128)(2,1)S(1)} %get-tuple-element.11.refs_3_) | copy-start | bytes 33030148
  121.1 7.5 %copy-start.1 = (bf16[768,512]{1,0:T(8,128)(2,1)S(1)}, bf16[768,512]{1,0:T(8,128)(2,1)}, u32[]{:S(2)}) copy-start(bf16[768,512]{1,0:T(8,128)(2,1)} %refs_0_.1) | copy-start | bytes 2359300
  145.5 21.7 %collective-permute-start.2 = (bf16[1536,128]{1,0:T(8,128)(2,1)S(1)}, bf16[1536,128]{1,0:T(8,128)(2,1)S(1)}, u32[]{:S(2)}, u32[]{:S(2)}) collective-permute-start(bf16[1536,128]{1,0:T(8,128)(2,1)S(1)} %get-tuple-element.14), channel_id=1, source_target_pairs={{16,0},{24,8},{32,16},{40,24},{48,32},{56,40},{64,48},{72,56},{80,... | collective-permute-start | bytes 1179656 | tf_op jit(solution)/shard_map/ppermute | solution.py:18
  146.8 20.4 %collective-permute-start.3 = (bf16[1536,128]{1,0:T(8,128)(2,1)S(1)}, bf16[1536,128]{1,0:T(8,128)(2,1)S(1)}, u32[]{:S(2)}, u32[]{:S(2)}) collective-permute-start(bf16[1536,128]{1,0:T(8,128)(2,1)S(1)} %get-tuple-element.15), channel_id=1, source_target_pairs={{8,0},{16,8},{24,16},{32,24},{40,32},{48,40},{56,48},{64,56},{72,6... | collective-permute-start | bytes 1179656 | tf_op jit(solution)/shard_map/ppermute | solution.py:18
Sparse Core Ops, SparseCore 0:
  10.2 102.9 all-gather.1
  121.2 74.6 reduce-scatter.1
where the time goes:
time: 204 us; the launch traced here: 203 us
  waiting for transfers between devices  121 us (59%)
  Pallas kernels  34 us (17%)
  matrix products  15.3 us (8%)
  between operations  14.2 us (7%)
  starting transfers between devices  8.16 us (4%)
  local copies, waits for them, and re-layouts  6.08 us (3%)
  other arithmetic  4.27 us (2%)
    all_gather x1, waiting for transfers between devices, local(): grad_full = lax.all_gather(out_grad, 'tensor', axis=1, tiled=True)  62.6 us
    ppermute x4, waiting for transfers between devices, shifted(): lax.ppermute(value, axis, [(source, source + steps) for source in range(i...  29.6 us
    reduce_scatter x1, waiting for transfers between devices, local(): lax.psum_scatter(weight_part.astype(jnp.bfloat16), 'seq', scatter_dimensi...  27.8 us
    pallas_call x1, Pallas kernels, local(): pl.pallas_call(lambda *refs: forward_kernel(tok, span, *refs), grid=(bloc...  17.1 us
    pallas_call x1, Pallas kernels, local(): pl.pallas_call(lambda *refs: backward_kernel(tok, span, *refs), grid=(blo...  16.9 us
    ppermute x4, starting transfers between devices, shifted(): lax.ppermute(value, axis, [(source, source + steps) for source in range(i...  8.08 us
    dot_general x1, matrix products, contract_rows(): lax.dot_general(left, right, (((0,), (0,)), ((), ())), preferred_element_...  7.8 us
    dot_general x1, matrix products, contract_last(): lax.dot_general(left, right, (((1,), (1,)), ((), ())), preferred_element_...  7.51 us
  transfers between devices with their start and end apart: 6, of which 4 were waited for; matrix products, arithmetic and copies ran while one was open for 6% of the time, Pallas kernels for 17%

commit v1 on v0

v1 whole, which is shorter than its diff:
```python
import math

import jax
import jax.numpy as jnp
from jax import lax
from jax.experimental import pallas as pl
from jax.experimental.pallas import tpu as pltpu
from jax.sharding import PartitionSpec as P

HEAD_SIZE = 128
NEG_BIG = -1e30
ROWS = 256
VMEM_BYTES = 24 << 20


def shifted(value, axis, steps):
    count = lax.axis_size(axis)
    initial, last = (max(0, -steps), min(count, count - steps))
    return lax.ppermute(value, axis, [(source, source + steps) for source in range(initial, last)])


def step_x(value, step):
    pairs = [(t, t // 4 * 4 + (t + step) % 4) for t in range(8)]
    return lax.ppermute(value, "tensor", pairs)


def step_y(value):
    return lax.ppermute(value, "tensor", [(t, t ^ 4) for t in range(8)])


def step_core(value):
    return lax.ppermute(value, "seq", [(s, s ^ 1) for s in range(16)])


def contract_rows(left, right):
    return lax.dot_general(
        left, right, (((0,), (0,)), ((), ())), preferred_element_type=jnp.float32
    )


def contract_last(left, right):
    return lax.dot_general(
        left, right, (((1,), (1,)), ((), ())), preferred_element_type=jnp.float32
    )


def gather_keys(parts, key_all, value_all, tok):
    for index, part in enumerate(parts):
        rows = pl.ds(index * tok, tok)
        key_all[rows, :] = part[pl.ds(0, tok), :]
        value_all[rows, :] = part[pl.ds(tok, tok), :]


def forward_kernel(
    tok, span, heads, low_ref, q_ref, far_ref, near_ref, own_ref,
    expo_ref, attn_ref, turned_ref, inverse_ref, key_all, value_all, bias,
):
    @pl.when(pl.program_id(0) == 0)
    def _():
        gather_keys((far_ref, near_ref, own_ref), key_all, value_all, tok)

    begin = pl.multiple_of(pl.program_id(0) * ROWS, ROWS)
    window = pl.ds(begin, span)
    key_at = lax.broadcasted_iota(jnp.int32, (ROWS, span), 1)
    row_at = lax.broadcasted_iota(jnp.int32, (ROWS, 1), 0)
    visible = (key_at >= low_ref[...] - begin) & (key_at <= row_at + 2 * tok)
    bias[...] = jnp.where(visible, 0.0, NEG_BIG)
    for head in range(heads):
        columns = slice(head * HEAD_SIZE, (head + 1) * HEAD_SIZE)
        raw = contract_last(q_ref[:, columns], key_all[window, :]) + bias[...]
        top = jnp.max(raw, axis=1, keepdims=True)
        expo = jnp.exp2((raw - top) * (math.log2(math.e) / math.sqrt(HEAD_SIZE)))
        inverse = 1.0 / jnp.sum(expo, axis=1, keepdims=True)
        expo_low = expo.astype(jnp.bfloat16)
        expo_ref[head] = expo_low
        inverse_ref[:, columns] = jnp.broadcast_to(inverse, (ROWS, HEAD_SIZE))
        attn = jnp.dot(expo_low, value_all[window, :], preferred_element_type=jnp.float32) * inverse
        attn = attn.astype(jnp.bfloat16)
        attn_ref[:, columns] = attn
        turned_ref[columns, :] = attn.T


def backward_rows(heads, width, first, q_ref, grad_ref, attn_ref, inverse_ref, probs_of, keys, values, gq_of, key_sum, value_sum):
    at = slice(first, first + width)
    for head in range(heads):
        columns = slice(head * HEAD_SIZE, (head + 1) * HEAD_SIZE)
        grad = (grad_ref[:, columns].astype(jnp.float32) * inverse_ref[:, columns]).astype(jnp.bfloat16)
        delta = jnp.sum(grad.astype(jnp.float32) * attn_ref[:, columns].astype(jnp.float32), axis=1, keepdims=True)
        d_prob = contract_last(grad, values[at, :])
        probs = probs_of(head)
        d_score = (probs.astype(jnp.float32) * (d_prob - delta)).astype(jnp.bfloat16)
        gq_of(columns, jnp.dot(d_score, keys[at, :], preferred_element_type=jnp.float32))
        key_sum[:, at] += jnp.dot(q_ref[:, columns].T, d_score, preferred_element_type=jnp.float32)
        value_sum[:, at] += jnp.dot(grad.T, probs, preferred_element_type=jnp.float32)


def backward_past_kernel(
    tok, heads, q_ref, grad_ref, attn_ref, inverse_ref, expo_ref, far_ref, near_ref,
    gq_ref, far_out, near_out, key_all, value_all, key_sum, value_sum,
):
    scale = 1.0 / math.sqrt(HEAD_SIZE)

    @pl.when(pl.program_id(0) == 0)
    def _():
        gather_keys((far_ref, near_ref), key_all, value_all, tok)
        key_sum[...] = jnp.zeros_like(key_sum)
        value_sum[...] = jnp.zeros_like(value_sum)

    def put(columns, value):
        gq_ref[:, columns] = value

    for block in range(tok // ROWS):
        @pl.when(pl.program_id(0) == block)
        def _(block=block):
            first = block * ROWS
            width = 2 * tok - first
            backward_rows(
                heads, width, first, q_ref, grad_ref, attn_ref, inverse_ref,
                lambda head: expo_ref[head, :, :width], key_all, value_all, put, key_sum, value_sum,
            )

    @pl.when(pl.program_id(0) == pl.num_programs(0) - 1)
    def _():
        for index, out in enumerate((far_out, near_out)):
            rows = pl.ds(index * tok, tok)
            out[pl.ds(0, tok), :] = (key_sum[:, rows].T * scale).astype(out.dtype)
            out[pl.ds(tok, tok), :] = value_sum[:, rows].T.astype(out.dtype)


def backward_own_kernel(
    tok, heads, q_ref, grad_ref, attn_ref, inverse_ref, expo_a, expo_b, expo_c, own_ref, past_ref,
    gq_ref, own_out, key_all, value_all, key_sum, value_sum,
):
    scale = 1.0 / math.sqrt(HEAD_SIZE)
    blocks = tok // ROWS
    expos = (expo_a, expo_b, expo_c)

    @pl.when(pl.program_id(0) == 0)
    def _():
        gather_keys((own_ref,), key_all, value_all, tok)
        key_sum[...] = jnp.zeros_like(key_sum)
        value_sum[...] = jnp.zeros_like(value_sum)

    def put(columns, value):
        gq_ref[:, columns] = ((past_ref[:, columns] + value) * scale).astype(gq_ref.dtype)

    for block in range(blocks):
        @pl.when(pl.program_id(0) == block)
        def _(block=block):
            width = (block + 1) * ROWS
            probs_of = lambda head: jnp.concatenate([expo[head] for expo in expos[blocks - 1 - block :]], axis=1)
            backward_rows(
                heads, width, 0, q_ref, grad_ref, attn_ref, inverse_ref,
                probs_of, key_all, value_all, put, key_sum, value_sum,
            )

    @pl.when(pl.program_id(0) == pl.num_programs(0) - 1)
    def _():
        own_out[pl.ds(0, tok), :] = key_sum[...].T * scale
        own_out[pl.ds(tok, tok), :] = value_sum[...].T


def project_kernel(sources, shapes, where_ref, weight_ref, turned_ref, *refs):
    count = len(shapes)
    pieces, refs = refs[:count], refs[count:]
    sems, turned, weights, *buffers = refs[-3 - count :]
    before, (total_ref, mine_ref, other_ref) = refs[: -6 - count], refs[-6 - count : -3 - count]
    width = weights.shape[1]
    cut = width // 2
    copies = []

    def fetch(source, target):
        copies.append(pltpu.make_async_copy(source, target, sems.at[len(copies)]))
        copies[-1].start()
        return copies[-1]

    pending = {}
    turned_copy = None
    for index, blocks in enumerate(sources):
        columns = pl.ds(pl.multiple_of(where_ref[1 + index] * width, width), width)
        pending["weight", index] = fetch(weight_ref.at[:, columns], weights.at[index])
        for operand, _, _, _ in blocks:
            if ("piece", operand) not in pending:
                pending["piece", operand] = fetch(pieces[operand], buffers[operand])
        if turned_copy is None:
            turned_copy = fetch(turned_ref, turned)
    pending["turned"] = turned_copy
    done = set()

    def ready(key):
        if key not in done:
            done.add(key)
            pending[key].wait()

    mine = pl.multiple_of(where_ref[0] * cut, cut)
    other = pl.multiple_of((1 - where_ref[0]) * cut, cut)
    total = before[0] if before else total_ref
    for index, blocks in enumerate(sources):
        ready(("weight", index))
        for operand, _, _, _ in blocks:
            ready(("piece", operand))
        weight = weights[index]
        for operand, there, row, rows in blocks:
            term = contract_last(buffers[operand][pl.ds(there, rows), :], weight)
            at = pl.ds(row, rows)
            if before or index:
                term = total[at, :] + term
            total_ref[at, :] = term.astype(total_ref.dtype)
        total = total_ref
        ready("turned")
        for out, begin in ((mine_ref, mine), (other_ref, other)):
            part = None
            for operand, there, row, rows in blocks:
                term = jnp.dot(
                    turned[:, pl.ds(row, rows)],
                    buffers[operand][pl.ds(there, rows), pl.ds(begin, cut)],
                    preferred_element_type=jnp.float32,
                )
                part = term if part is None else part + term
            out[index] = part.astype(out.dtype)


def in_hbm(value):
    return pltpu.with_memory_space_constraint(value, pltpu.HBM)


def hbm():
    return pl.BlockSpec(memory_space=pltpu.HBM)


def project(sources, last, flops, where, weight, turned, pieces, before):
    width, tok = turned.shape
    count = len(sources)
    parts = jax.ShapeDtypeStruct((count, width, width // 2), jnp.bfloat16)
    pieces = [in_hbm(piece) for piece in pieces]
    shapes = [piece.shape for piece in pieces]
    return pl.pallas_call(
        lambda *refs: project_kernel(sources, shapes, *refs),
        in_specs=[pl.BlockSpec(memory_space=pltpu.SMEM)] + [hbm()] * (2 + len(pieces)) + [whole()] * len(before),
        out_specs=[whole()] * 3,
        scratch_shapes=[
            pltpu.SemaphoreType.DMA((count + len(pieces) + 1,)), pltpu.VMEM((width, tok), jnp.bfloat16),
            pltpu.VMEM((count, width, width), jnp.bfloat16),
        ] + [pltpu.VMEM(shape, jnp.bfloat16) for shape in shapes],
        out_shape=[jax.ShapeDtypeStruct((tok, width), jnp.bfloat16 if last else jnp.float32), parts, parts],
        compiler_params=pltpu.CompilerParams(vmem_limit_bytes=VMEM_BYTES),
        cost_estimate=pl.CostEstimate(flops=flops, bytes_accessed=1 << 20, transcendentals=0),
        name="project",
    )(where, weight, turned, *pieces, *before)


def place_kernel(counts, where_ref, *refs):
    sems, mine, come = refs[-3:]
    out_ref, refs = refs[-4], refs[:-4]
    copies, index = [], 0
    for i, count in enumerate(counts):
        rows = pl.ds(index, count)
        for source, target, sem in ((refs[2 * i], mine, 2 * i), (refs[2 * i + 1], come, 2 * i + 1)):
            copies.append(pltpu.make_async_copy(source, target.at[rows], sems.at[sem]))
            copies[-1].start()
        index += count
    index = 0
    for i, count in enumerate(counts):
        copies[2 * i].wait()
        copies[2 * i + 1].wait()
        for _ in range(count):
            both = mine[index].astype(jnp.float32) + come[index].astype(jnp.float32)
            out_ref[where_ref[index]] = both.astype(out_ref.dtype)
            index += 1


def whole():
    return pl.BlockSpec(memory_space=pltpu.VMEM)


def local(queries, keys, values, out_weight, out_grad, doc_ids):
    tok = queries.shape[0]
    heads = queries.shape[1] // HEAD_SIZE
    blocks = tok // ROWS
    span = 2 * tok + ROWS
    shard = lax.axis_index("seq")
    docs = jnp.pad(doc_ids.astype(jnp.bfloat16).reshape(tok // HEAD_SIZE, HEAD_SIZE), ((0, 16 - tok // HEAD_SIZE), (0, 0)))
    own = jnp.concatenate([keys, values, docs], axis=0)
    far, near = shifted(own, "seq", 2), shifted(own, "seq", 1)
    doc_of = lambda part: part[2 * tok : 2 * tok + tok // HEAD_SIZE].reshape(tok).astype(jnp.int32)
    doc_keys = jnp.concatenate([
        jnp.where(shard >= 2, doc_of(far), -1), jnp.where(shard >= 1, doc_of(near), -1), doc_ids
    ])
    earlier = jnp.sum((doc_keys[None, :] < doc_ids[:, None]).astype(jnp.int32), axis=1)
    low = jnp.maximum(earlier, jnp.arange(tok, dtype=jnp.int32) + 1)[:, None]

    all_heads = heads * HEAD_SIZE
    row_block = pl.BlockSpec((ROWS, all_heads), lambda b: (b, 0))
    held = [pltpu.VMEM((3 * tok, HEAD_SIZE), jnp.bfloat16)] * 2
    work = heads * tok * span * HEAD_SIZE * 2
    rows_of = lambda dtype: jax.ShapeDtypeStruct((tok, all_heads), dtype)
    expo, attn, turned, inverse = pl.pallas_call(
        lambda *refs: forward_kernel(tok, span, heads, *refs),
        grid=(blocks,),
        in_specs=[pl.BlockSpec((ROWS, 1), lambda b: (b, 0)), row_block, whole(), whole(), whole()],
        out_specs=[
            pl.BlockSpec((heads, ROWS, span), lambda b: (0, b, 0)), row_block,
            pl.BlockSpec((all_heads, ROWS), lambda b: (0, b)), row_block,
        ],
        out_shape=[
            pltpu.HBM((heads, tok, span), jnp.bfloat16), rows_of(jnp.bfloat16),
            pltpu.HBM((all_heads, tok), jnp.bfloat16), rows_of(jnp.float32),
        ],
        scratch_shapes=held + [pltpu.VMEM((ROWS, span), jnp.float32)],
        compiler_params=pltpu.CompilerParams(vmem_limit_bytes=VMEM_BYTES),
        cost_estimate=pl.CostEstimate(flops=2 * work, bytes_accessed=14 << 20, transcendentals=heads * tok * span),
        name="forward",
    )(low, queries, far, near, own)
    expo = in_hbm(expo)

    tensor = lax.axis_index("tensor")
    row, column = tensor // 4, tensor % 4
    at = lambda flip, step: (row ^ flip) * 4 + (column + step) % 4
    core = shard % 2
    places = [at(0, 0), at(0, 3), at(0, 1), at(0, 2), at(1, 0), at(1, 3), at(1, 1), at(1, 2)]
    where = lambda some: jnp.stack([core, *some]).astype(jnp.int32)
    near_up, near_down, opposite = step_x(out_grad, 1), step_x(out_grad, -1), step_x(out_grad, 2)
    across = step_y(lax.optimization_barrier((out_grad, far, near))[0])
    across, turned = lax.optimization_barrier((across, turned))
    across_up, across_down = step_x(across, 1), step_x(across, -1)
    weight, turned = in_hbm(out_weight), in_hbm(turned)
    real = lambda count: 4 * count * tok * all_heads * all_heads
    total, mine_a, other_a = project(
        [((p, 0, 0, tok),) for p in range(4)], False, real(4),
        where(places[:4]), weight, turned, (out_grad, near_up, near_down, opposite), (),
    )
    last = step_y(opposite)
    total, mine_b, other_b = project(
        [((p, 0, 0, tok),) for p in range(3)], False, 4 * real(3),
        where(places[4:7]), weight, turned, (across, across_up, across_down), (total,),
    )
    attention_gradient, mine_c, other_c = project(
        [((0, 0, 0, tok),)], True, 1 << 20,
        where(places[7:]), weight, turned, (last,), (total,),
    )
    parts = [mine_a, step_core(other_a), mine_b, step_core(other_b), mine_c, step_core(other_c)]
    counts = [part.shape[0] for part in parts[::2]]
    both = pltpu.VMEM((8,) + mine_a.shape[1:], jnp.bfloat16)
    placed = pl.pallas_call(
        lambda *refs: place_kernel(counts, *refs),
        in_specs=[pl.BlockSpec(memory_space=pltpu.SMEM)] + [hbm()] * 6,
        out_specs=whole(),
        out_shape=jax.ShapeDtypeStruct((8,) + mine_a.shape[1:], jnp.bfloat16),
        scratch_shapes=[pltpu.SemaphoreType.DMA((6,)), both, both],
        compiler_params=pltpu.CompilerParams(vmem_limit_bytes=VMEM_BYTES),
        cost_estimate=pl.CostEstimate(flops=1 << 20, bytes_accessed=1 << 20, transcendentals=0),
        name="place",
    )(jnp.stack(places).astype(jnp.int32), *[in_hbm(part) for part in parts])
    placed, attention_gradient = lax.optimization_barrier((placed, attention_gradient))
    groups = [[2 * chip + c for chip in range(8)] for c in range(2)]
    arrived = lax.all_to_all(placed, "seq", 0, 0, axis_index_groups=groups)
    weight_grad = jnp.sum(arrived.astype(jnp.float32), axis=0).astype(jnp.bfloat16)

    pair = lambda dtype: jax.ShapeDtypeStruct((2 * tok, HEAD_SIZE), dtype)
    sums = lambda width: [pltpu.VMEM((width, HEAD_SIZE), jnp.bfloat16)] * 2 + [pltpu.VMEM((HEAD_SIZE, width), jnp.float32)] * 2
    past_queries, far_sum, near_sum = pl.pallas_call(
        lambda *refs: backward_past_kernel(tok, heads, *refs),
        grid=(blocks,),
        in_specs=[row_block] * 4 + [pl.BlockSpec((heads, ROWS, 2 * tok), lambda b: (0, b, 0)), whole(), whole()],
        out_specs=[row_block, whole(), whole()],
        out_shape=[rows_of(jnp.float32), pair(jnp.bfloat16), pair(jnp.bfloat16)],
        scratch_shapes=sums(2 * tok),
        compiler_params=pltpu.CompilerParams(vmem_limit_bytes=VMEM_BYTES),
        cost_estimate=pl.CostEstimate(flops=1 << 20, bytes_accessed=1 << 20, transcendentals=0),
        name="backward_past",
    )(queries, attention_gradient, attn, inverse, expo, far, near)
    far_come, near_come = shifted(far_sum, "seq", -2), shifted(near_sum, "seq", -1)
    last_blocks = [pl.BlockSpec((heads, ROWS, ROWS), lambda b, i=i: (0, b, span // ROWS - blocks + i)) for i in range(blocks)]
    grad_queries, own_sum = pl.pallas_call(
        lambda *refs: backward_own_kernel(tok, heads, *refs),
        grid=(blocks,),
        in_specs=[row_block] * 4 + last_blocks + [whole(), row_block],
        out_specs=[row_block, whole()],
        out_shape=[rows_of(jnp.bfloat16), pair(jnp.float32)],
        scratch_shapes=sums(tok),
        compiler_params=pltpu.CompilerParams(vmem_limit_bytes=VMEM_BYTES),
        cost_estimate=pl.CostEstimate(flops=1 << 20, bytes_accessed=1 << 20, transcendentals=0),
        name="backward_own",
    )(queries, attention_gradient, attn, inverse, *([expo] * blocks), own, past_queries)
    total = own_sum + near_come.astype(jnp.float32) + far_come.astype(jnp.float32)
    total = total.astype(jnp.bfloat16)
    return (grad_queries, total[:tok], total[tok:], weight_grad)


def solution(mesh):
    placed = (
        P("seq", "tensor"),
        P("seq", "tensor"),
        P("seq", "tensor"),
        P("tensor", None),
        P("seq", "tensor"),
        P("seq"),
    )
    return jax.shard_map(
        local,
        mesh=mesh,
        in_specs=placed,
        out_specs=(P("seq", "tensor"), P("seq", "tensor"), P("seq", "tensor"), P("tensor", "seq")),
        check_vma=False,
    )
```

time: 204 us -> 137 us (0.67)
  waiting for transfers between devices: 121 us -> 37 us
  starting transfers between devices: 8.16 us -> 29 us
  matrix products: 15.3 us -> 0 us
  Pallas kernels: 34 us -> 48.4 us
  between operations: 14.2 us -> 0.81 us
  local copies, waits for them, and re-layouts: 6.08 us -> 13.7 us
  other arithmetic: 4.27 us -> 7.07 us
    all_gather x1 -> x0, waiting for transfers between devices: 62.6 us -> none  [local(): grad_full = lax.all_gather(out_grad, 'tensor', axis=1, tiled=True)]
    reduce_scatter x1 -> x0, waiting for transfers between devices: 27.8 us -> none  [local(): lax.psum_scatter(weight_part.astype(jnp.bfloat16), 'seq', scatter_dimensi...]
    dot_general x2 -> x0, matrix products: 15.3 us -> none  [the longest x1 7.8 us: contract_rows(): lax.dot_general(left, right, (((0,), (0,)), ((), ())), preferred_element_...]
    ppermute x0 -> x10, waiting for transfers between devices: none -> 14.7 us  [the longest x5 12.8 us: step_x(): return lax.ppermute(value, 'tensor', pairs)]
    ppermute x0 -> x10, starting transfers between devices: none -> 14.6 us  [the longest x5 7.88 us: step_x(): return lax.ppermute(value, 'tensor', pairs)]
    pallas_call x2 -> x7, Pallas kernels: 34 us -> 48.4 us  [the longest x3 16.3 us: project(): pl.pallas_call(lambda *refs: project_kernel(sources, shapes, *refs), in_s...]
    unnamed x6 -> x30, local copies, waits for them, and re-layouts: 5.32 us -> 12.8 us
    ppermute x4, waiting for transfers between devices: 29.6 us -> 22.3 us  [shifted(): lax.ppermute(value, axis, [(source, source + steps) for source in range(i...]
  transfers between devices with their start and end apart: 6 -> 15, of which waited for: 4 -> 7; matrix products, arithmetic and copies ran while one was open for 6% -> 3% of each run, Pallas kernels for 17% -> 32%
where the time goes in v1:
time: 137 us; the launch traced here: 136 us
  Pallas kernels  48.4 us (35%)
  waiting for transfers between devices  37 us (27%)
  starting transfers between devices  29 us (21%)
  local copies, waits for them, and re-layouts  13.7 us (10%)
  other arithmetic  7.07 us (5%)
    ppermute x4, waiting for transfers between devices, shifted(): lax.ppermute(value, axis, [(source, source + steps) for source in range(i...  22.3 us
    pallas_call x3, Pallas kernels, project(): pl.pallas_call(lambda *refs: project_kernel(sources, shapes, *refs), in_s...  16.3 us
    ppermute x5, waiting for transfers between devices, step_x(): return lax.ppermute(value, 'tensor', pairs)  12.8 us
    unnamed x30, local copies, waits for them, and re-layouts  12.8 us
    pallas_call x1, Pallas kernels, local(): pl.pallas_call(lambda *refs: forward_kernel(tok, span, heads, *refs), gri...  12.6 us
    pallas_call x1, Pallas kernels, local(): pl.pallas_call(lambda *refs: backward_past_kernel(tok, heads, *refs), gri...  8.81 us
    ppermute x4, starting transfers between devices, shifted(): lax.ppermute(value, axis, [(source, source + steps) for source in range(i...  8.31 us
    ppermute x5, starting transfers between devices, step_x(): return lax.ppermute(value, 'tensor', pairs)  7.88 us
  transfers between devices with their start and end apart: 15, of which 7 were waited for; matrix products, arithmetic and copies ran while one was open for 3% of the time, Pallas kernels for 32%

profile of v1, /device:TPU:0, one launch (start us, length us, event | category | flops | bytes accessed | tf_op | source)
XLA Modules:
  0.0 136.0 jit_solution(4932256079051313329)
XLA Ops:
  1.3 1.0 fusion.1.refs_4_.refs_7_
  2.4 1.3 collective-permute-start.1
  3.7 4.2 %collective-permute-start = (bf16[1552,128]{1,0:T(8,128)(2,1)S(1)}, bf16[1552,128]{1,0:T(8,128)(2,1)S(1)}, u32[]{:S(2)}, u32[]{:S(2)}) collective-permute-start(bf16[1552,128]{1,0:T(8,128)(2,1)S(1)} %fusion.1.refs_4_.refs_7_), channel_id=1, source_target_pairs={{0,16},{8,24},{16,32},{24,40},{32,48},{40,56},{48,64},{56,72},{64,... | collective-permute-start | bytes 1191944 | tf_op jit(solution)/shard_map/ppermute | solution.py:19
  7.9 2.8 %collective-permute-start.4 = (bf16[768,512]{1,0:T(8,128)(2,1)}, bf16[768,512]{1,0:T(8,128)(2,1)}, u32[]{:S(2)}, u32[]{:S(2)}) collective-permute-start(bf16[768,512]{1,0:T(8,128)(2,1)} %refs_3_.1), channel_id=1, source_target_pairs={{0,3},{1,0},{2,1},{3,2},{4,7},{5,4},{6,5},{7,6},{8,11},{9,8},{10,9... | collective-permute-start | bytes 2359304 | tf_op jit(solution)/shard_map/ppermute | solution.py:24
  10.7 2.3 %collective-permute-start.5 = (bf16[768,512]{1,0:T(8,128)(2,1)}, bf16[768,512]{1,0:T(8,128)(2,1)}, u32[]{:S(2)}, u32[]{:S(2)}) collective-permute-start(bf16[768,512]{1,0:T(8,128)(2,1)} %refs_3_.1), channel_id=1, source_target_pairs={{0,2},{1,3},{2,0},{3,1},{4,6},{5,7},{6,4},{7,5},{8,10},{9,11},{10,... | collective-permute-start | bytes 2359304 | tf_op jit(solution)/shard_map/ppermute | solution.py:24
  13.0 4.5 %collective-permute-done.refs_2_.refs_5_ = bf16[1552,128]{1,0:T(8,128)(2,1)S(1)} collective-permute-done((bf16[1552,128]{1,0:T(8,128)(2,1)S(1)}, bf16[1552,128]{1,0:T(8,128)(2,1)S(1)}, u32[]{:S(2)}, u32[]{:S(2)}) %collective-permute-start) | collective-permute-done | bytes 397344 | tf_op jit(solution)/shard_map/ppermute | solution.py:19
  17.5 2.9 %collective-permute-start.2 = (bf16[768,512]{1,0:T(8,128)(2,1)}, bf16[768,512]{1,0:T(8,128)(2,1)}, u32[]{:S(2)}, u32[]{:S(2)}) collective-permute-start(bf16[768,512]{1,0:T(8,128)(2,1)} %refs_3_.1), channel_id=1, source_target_pairs={{0,4},{1,5},{2,6},{3,7},{4,0},{5,1},{6,2},{7,3},{8,12},{9,13},{10,... | collective-permute-start | bytes 2359304 | tf_op jit(solution)/shard_map/ppermute | solution.py:28
  21.9 1.5 %convert_reduce_fusion = s32[768]{0:T(1024)S(1)} fusion(s32[2304]{0:T(1024)S(1)} %pad_add_fusion, s32[768]{0:T(1024)} %param.11), kind=kLoop, calls=%fused_computation | loop fusion | flops 5307648 | bytes 15360 | tf_op jit(solution)/shard_map/reduce_sum | solution.py:289
  23.6 1.1 copy-done
  24.7 1.0 copy-done.11
  25.7 12.6 %forward.1 = (bf16[4,768,1792]{2,1,0:T(8,128)(2,1)}, bf16[768,512]{1,0:T(8,128)(2,1)S(1)}, bf16[512,768]{1,0:T(8,128)(2,1)}, f32[768,512]{1,0:T(8,128)S(1)}) custom-call(s32[768,1]{1,0:T(8,128)S(1)} %reshape_maximum_fusion.refs_0_, bf16[768,512]{1,0:T(8,128)(2,1)S(1)} %copy-done, bf16[1552,128]{1,0:T(8,128)(2,1)S(1)} %copy-done.11, ...), custom_call_target="tpu_custom_call" | custom-call | flops 2818572288 | bytes 14680064 | tf_op jit(solution)/shard_map/forward/pallas_call | solution.py:297
  38.9 2.8 %collective-permute-start.8 = (bf16[768,512]{1,0:T(8,128)(2,1)}, bf16[768,512]{1,0:T(8,128)(2,1)}, u32[]{:S(2)}, u32[]{:S(2)}) collective-permute-start(bf16[768,512]{1,0:T(8,128)(2,1)} %collective-permute-done.2.refs_3_), channel_id=1, source_target_pairs={{0,3},{1,0},{2,1},{3,2},{4,7},{5,4},{6,5},{7,6},{8,11},{9,8},{10,9... | collective-permute-start | bytes 2359304 | tf_op jit(solution)/shard_map/ppermute | solution.py:24
  41.9 6.5 %collective-permute-done.5.refs_6_ = bf16[768,512]{1,0:T(8,128)(2,1)} collective-permute-done((bf16[768,512]{1,0:T(8,128)(2,1)}, bf16[768,512]{1,0:T(8,128)(2,1)}, u32[]{:S(2)}, u32[]{:S(2)}) %collective-permute-start.5) | collective-permute-done | bytes 786464 | tf_op jit(solution)/shard_map/ppermute | solution.py:24
  48.4 2.6 %collective-permute-start.10 = (bf16[768,512]{1,0:T(8,128)(2,1)}, bf16[768,512]{1,0:T(8,128)(2,1)}, u32[]{:S(2)}, u32[]{:S(2)}) collective-permute-start(bf16[768,512]{1,0:T(8,128)(2,1)} %collective-permute-done.5.refs_6_), channel_id=1, source_target_pairs={{0,4},{1,5},{2,6},{3,7},{4,0},{5,1},{6,2},{7,3},{8,12},{9,13},{10,... | collective-permute-start | bytes 2359304 | tf_op jit(solution)/shard_map/ppermute | solution.py:28
  51.0 7.1 %project.3 = (f32[768,512]{1,0:T(8,128)S(1)}, bf16[4,512,256]{2,1,0:T(8,128)(2,1)S(1)}, bf16[4,512,256]{2,1,0:T(8,128)(2,1)}) custom-call(s32[5]{0:T(128)S(1)} %stack.59.refs_0_, bf16[512,4096]{1,0:T(8,128)(2,1)} %refs_1_.7, bf16[512,768]{1,0:T(8,128)(2,1)} %get-tuple-element.29.refs_2_, bf16[768,512]{1,0:T(8,128)(2,1)} %refs_3_.1, ...), custom_call_target="tpu_custom_call" | custom-call | flops 3221225472 | bytes 1048576 | tf_op jit(solution)/shard_map/project/pallas_call | solution.py:237
  59.8 2.2 %collective-permute-done.8.refs_5_ = bf16[768,512]{1,0:T(8,128)(2,1)} collective-permute-done((bf16[768,512]{1,0:T(8,128)(2,1)}, bf16[768,512]{1,0:T(8,128)(2,1)}, u32[]{:S(2)}, u32[]{:S(2)}) %collective-permute-start.8) | collective-permute-done | bytes 786464 | tf_op jit(solution)/shard_map/ppermute | solution.py:24
  62.1 4.0 %collective-permute-done.7.refs_4_ = bf16[768,512]{1,0:T(8,128)(2,1)} collective-permute-done((bf16[768,512]{1,0:T(8,128)(2,1)}, bf16[768,512]{1,0:T(8,128)(2,1)}, u32[]{:S(2)}, u32[]{:S(2)}) %collective-permute-start.7) | collective-permute-done | bytes 786464 | tf_op jit(solution)/shard_map/ppermute | solution.py:24
  66.1 6.1 %project.4 = (f32[768,512]{1,0:T(8,128)S(1)}, bf16[3,512,256]{2,1,0:T(8,128)(2,1)S(1)}, bf16[3,512,256]{2,1,0:T(8,128)(2,1)}) custom-call(s32[4]{0:T(128)S(1)} %pad_add_fusion.1.refs_0_, bf16[512,4096]{1,0:T(8,128)(2,1)} %refs_1_.7, bf16[512,768]{1,0:T(8,128)(2,1)} %get-tuple-element.29.refs_2_, bf16[768,512]{1,0:T(8,128)(2,1)} %collective-permute-done.2.refs_3_, ...), custom_call_target="tpu_custom_call" | custom-call | flops 9663676416 | bytes 1048576 | tf_op jit(solution)/shard_map/project/pallas_call | solution.py:237
  72.2 1.2 copy-done.4
  74.8 1.4 %copy-done.5 = f32[768,512]{1,0:T(8,128)S(1)} copy-done((f32[768,512]{1,0:T(8,128)S(1)}, f32[768,512]{1,0:T(8,128)}, u32[]{:S(2)}) %copy-start.5) | copy-done | bytes 1572888
  76.2 3.1 %project.5 = (bf16[768,512]{1,0:T(8,128)(2,1)S(1)}, bf16[1,512,256]{2,1,0:T(8,128)(2,1)S(1)}, bf16[1,512,256]{2,1,0:T(8,128)(2,1)S(1)}) custom-call(s32[2]{0:T(128)S(1)} %pad_add_fusion.2.refs_0_, bf16[512,4096]{1,0:T(8,128)(2,1)} %refs_1_.7, bf16[512,768]{1,0:T(8,128)(2,1)} %get-tuple-element.29.refs_2_, bf16[768,512]{1,0:T(8,128)(2,1)} %collective-permute-done.10.refs_3_, ...), custom_call_target="tpu_custom_call" | custom-call | flops 1048576 | bytes 1048576 | tf_op jit(solution)/shard_map/project/pallas_call | solution.py:237
  81.0 1.4 collective-permute-done.11.refs_6_
  83.1 4.3 %place.1 = bf16[8,512,256]{2,1,0:T(8,128)(2,1)} custom-call(s32[8]{0:T(128)S(1)} %stack.57.refs_0_, bf16[4,512,256]{2,1,0:T(8,128)(2,1)} %copy-done.6, bf16[4,512,256]{2,1,0:T(8,128)(2,1)} %collective-permute-done.6.refs_2_, bf16[3,512,256]{2,1,0:T(8,128)(2,1)} %copy-done.7, bf16[3,512,256]{2,1,0:T(8,128)(2,1)} %collective-permute-done.9.refs_4_, ...), custom_call_target="tpu_custom_call" | custom-call | flops 1048576 | bytes 1048576 | tf_op jit(solution)/shard_map/place/pallas_call | solution.py:344
  87.4 6.1 %all-to-all-start = ((bf16[8,512,256]{2,1,0:T(8,128)(2,1)}), bf16[8,512,256]{2,1,0:T(8,128)(2,1)}, u32[]{:S(2)}, u32[]{:S(2)}) async-start(bf16[8,512,256]{2,1,0:T(8,128)(2,1)} %place.1), calls=%async_computation | async-start | bytes 4194304 | tf_op jit(solution)/shard_map/all_to_all | solution.py:356
  93.5 1.1 copy-done.3
  94.6 1.0 copy-done.9
  96.6 8.8 %backward_past.1 = (f32[768,512]{1,0:T(8,128)S(1)}, bf16[1536,128]{1,0:T(8,128)(2,1)S(1)}, bf16[1536,128]{1,0:T(8,128)(2,1)S(1)}) custom-call(bf16[768,512]{1,0:T(8,128)(2,1)S(1)} %copy-done.1, bf16[768,512]{1,0:T(8,128)(2,1)S(1)} %copy-done.3, bf16[768,512]{1,0:T(8,128)(2,1)S(1)} %get-tuple-element.41.refs_2_, f32[768,512]{1,0:T(8,128)S(1)} %get-tuple-element.42.refs_3_, ...), custom_call_target="tpu_custom_call" | custom-call | flops 1048576 | bytes 1048576 | tf_op jit(solution)/shard_map/backward_past/pallas_call | solution.py:361
  105.4 1.3 collective-permute-start.12
  106.7 1.5 %collective-permute-start.13 = (bf16[1536,128]{1,0:T(8,128)(2,1)S(1)}, bf16[1536,128]{1,0:T(8,128)(2,1)S(1)}, u32[]{:S(2)}, u32[]{:S(2)}) collective-permute-start(bf16[1536,128]{1,0:T(8,128)(2,1)S(1)} %get-tuple-element.48), channel_id=1, source_target_pairs={{16,0},{24,8},{32,16},{40,24},{48,32},{56,40},{64,48},{72,56},{80,... | collective-permute-start | bytes 1179656 | tf_op jit(solution)/shard_map/ppermute | solution.py:19
  108.2 6.4 %backward_own.1 = (bf16[768,512]{1,0:T(8,128)(2,1)}, f32[1536,128]{1,0:T(8,128)S(1)}) custom-call(bf16[768,512]{1,0:T(8,128)(2,1)S(1)} %copy-done.1, bf16[768,512]{1,0:T(8,128)(2,1)S(1)} %copy-done.3, bf16[768,512]{1,0:T(8,128)(2,1)S(1)} %get-tuple-element.41.refs_2_, f32[768,512]{1,0:T(8,128)S(1)} %get-tuple-element.42.refs_3_, ...), custom_call_target="tpu_custom_call" | custom-call | flops 1048576 | bytes 1048576 | tf_op jit(solution)/shard_map/backward_own/pallas_call | solution.py:374
  114.6 17.8 %collective-permute-done.13 = bf16[1536,128]{1,0:T(8,128)(2,1)S(1)} collective-permute-done((bf16[1536,128]{1,0:T(8,128)(2,1)S(1)}, bf16[1536,128]{1,0:T(8,128)(2,1)S(1)}, u32[]{:S(2)}, u32[]{:S(2)}) %collective-permute-start.13) | collective-permute-done | bytes 393248 | tf_op jit(solution)/shard_map/ppermute | solution.py:19
  133.3 2.6 %reduce_sum.25 = bf16[512,256]{1,0:T(8,128)(2,1)} reduce(bf16[8,512,256]{2,1,0:T(8,128)(2,1)} %all-to-all-done, bf16[]{:T(256)} %constant.75.clone.1), dimensions={0}, to_apply=%region_1.2 | reduce | flops 917504 | bytes 2359298 | tf_op jit(solution)/shard_map/reduce_sum | solution.py:357
  (49 shorter events, 10.6 us)
Async XLA Ops:
  2.4 10.6 %collective-permute-start.1 = (bf16[1552,128]{1,0:T(8,128)(2,1)S(1)}, bf16[1552,128]{1,0:T(8,128)(2,1)S(1)}, u32[]{:S(2)}, u32[]{:S(2)}) collective-permute-start(bf16[1552,128]{1,0:T(8,128)(2,1)S(1)} %fusion.1.refs_4_.refs_7_), channel_id=1, source_target_pairs={{0,8},{8,16},{16,24},{24,32},{32,40},{40,48},{48,56},{56,64},{64,7... | collective-permute-start | bytes 1191944 | tf_op jit(solution)/shard_map/ppermute | solution.py:19
  3.7 13.8 %collective-permute-start = (bf16[1552,128]{1,0:T(8,128)(2,1)S(1)}, bf16[1552,128]{1,0:T(8,128)(2,1)S(1)}, u32[]{:S(2)}, u32[]{:S(2)}) collective-permute-start(bf16[1552,128]{1,0:T(8,128)(2,1)S(1)} %fusion.1.refs_4_.refs_7_), channel_id=1, source_target_pairs={{0,16},{8,24},{16,32},{24,40},{32,48},{40,56},{48,64},{56,72},{64,... | collective-permute-start | bytes 1191944 | tf_op jit(solution)/shard_map/ppermute | solution.py:19
  7.9 43.1 %collective-permute-start.4 = (bf16[768,512]{1,0:T(8,128)(2,1)}, bf16[768,512]{1,0:T(8,128)(2,1)}, u32[]{:S(2)}, u32[]{:S(2)}) collective-permute-start(bf16[768,512]{1,0:T(8,128)(2,1)} %refs_3_.1), channel_id=1, source_target_pairs={{0,3},{1,0},{2,1},{3,2},{4,7},{5,4},{6,5},{7,6},{8,11},{9,8},{10,9... | collective-permute-start | bytes 2359304 | tf_op jit(solution)/shard_map/ppermute | solution.py:24
  10.7 40.2 %collective-permute-start.3 = (bf16[768,512]{1,0:T(8,128)(2,1)}, bf16[768,512]{1,0:T(8,128)(2,1)}, u32[]{:S(2)}, u32[]{:S(2)}) collective-permute-start(bf16[768,512]{1,0:T(8,128)(2,1)} %refs_3_.1), channel_id=1, source_target_pairs={{0,1},{1,2},{2,3},{3,0},{4,5},{5,6},{6,7},{7,4},{8,9},{9,10},{10,1... | collective-permute-start | bytes 2359304 | tf_op jit(solution)/shard_map/ppermute | solution.py:24
  10.7 37.7 %collective-permute-start.5 = (bf16[768,512]{1,0:T(8,128)(2,1)}, bf16[768,512]{1,0:T(8,128)(2,1)}, u32[]{:S(2)}, u32[]{:S(2)}) collective-permute-start(bf16[768,512]{1,0:T(8,128)(2,1)} %refs_3_.1), channel_id=1, source_target_pairs={{0,2},{1,3},{2,0},{3,1},{4,6},{5,7},{6,4},{7,5},{8,10},{9,11},{10,... | collective-permute-start | bytes 2359304 | tf_op jit(solution)/shard_map/ppermute | solution.py:24
  13.0 25.3 %copy-start.8 = (bf16[1552,128]{1,0:T(8,128)(2,1)}, bf16[1552,128]{1,0:T(8,128)(2,1)S(1)}, u32[]{:S(2)}) copy-start(bf16[1552,128]{1,0:T(8,128)(2,1)S(1)} %collective-permute-done.1.refs_3_.refs_6_) | copy-start | bytes 1191940
  17.5 21.4 %collective-permute-start.2 = (bf16[768,512]{1,0:T(8,128)(2,1)}, bf16[768,512]{1,0:T(8,128)(2,1)}, u32[]{:S(2)}, u32[]{:S(2)}) collective-permute-start(bf16[768,512]{1,0:T(8,128)(2,1)} %refs_3_.1), channel_id=1, source_target_pairs={{0,4},{1,5},{2,6},{3,7},{4,0},{5,1},{6,2},{7,3},{8,12},{9,13},{10,... | collective-permute-start | bytes 2359304 | tf_op jit(solution)/shard_map/ppermute | solution.py:28
  20.4 0.8 copy-start.10
  23.6 1.1 copy-start
  24.7 1.0 copy-start.11
  38.9 23.1 %collective-permute-start.8 = (bf16[768,512]{1,0:T(8,128)(2,1)}, bf16[768,512]{1,0:T(8,128)(2,1)}, u32[]{:S(2)}, u32[]{:S(2)}) collective-permute-start(bf16[768,512]{1,0:T(8,128)(2,1)} %collective-permute-done.2.refs_3_), channel_id=1, source_target_pairs={{0,3},{1,0},{2,1},{3,2},{4,7},{5,4},{6,5},{7,6},{8,11},{9,8},{10,9... | collective-permute-start | bytes 2359304 | tf_op jit(solution)/shard_map/ppermute | solution.py:24
  41.7 24.4 %collective-permute-start.7 = (bf16[768,512]{1,0:T(8,128)(2,1)}, bf16[768,512]{1,0:T(8,128)(2,1)}, u32[]{:S(2)}, u32[]{:S(2)}) collective-permute-start(bf16[768,512]{1,0:T(8,128)(2,1)} %collective-permute-done.2.refs_3_), channel_id=1, source_target_pairs={{0,1},{1,2},{2,3},{3,0},{4,5},{5,6},{6,7},{7,4},{8,9},{9,10},{10,1... | collective-permute-start | bytes 2359304 | tf_op jit(solution)/shard_map/ppermute | solution.py:24
  48.4 26.4 %collective-permute-start.10 = (bf16[768,512]{1,0:T(8,128)(2,1)}, bf16[768,512]{1,0:T(8,128)(2,1)}, u32[]{:S(2)}, u32[]{:S(2)}) collective-permute-start(bf16[768,512]{1,0:T(8,128)(2,1)} %collective-permute-done.5.refs_6_), channel_id=1, source_target_pairs={{0,4},{1,5},{2,6},{3,7},{4,0},{5,1},{6,2},{7,3},{8,12},{9,13},{10,... | collective-permute-start | bytes 2359304 | tf_op jit(solution)/shard_map/ppermute | solution.py:28
  58.1 1.0 copy-start.6
  59.1 23.3 %collective-permute-start.6 = (bf16[4,512,256]{2,1,0:T(8,128)(2,1)}, bf16[4,512,256]{2,1,0:T(8,128)(2,1)}, u32[]{:S(2)}, u32[]{:S(2)}) collective-permute-start(bf16[4,512,256]{2,1,0:T(8,128)(2,1)} %get-tuple-element.31), channel_id=1, source_target_pairs={{0,8},{8,0},{16,24},{24,16},{32,40},{40,32},{48,56},{56,48},{64,72... | collective-permute-start | bytes 3145736 | tf_op jit(solution)/shard_map/ppermute | solution.py:32
  72.2 1.2 copy-start.4
  73.4 0.9 copy-start.7
  74.3 8.1 %collective-permute-start.9 = (bf16[3,512,256]{2,1,0:T(8,128)(2,1)}, bf16[3,512,256]{2,1,0:T(8,128)(2,1)}, u32[]{:S(2)}, u32[]{:S(2)}) collective-permute-start(bf16[3,512,256]{2,1,0:T(8,128)(2,1)} %get-tuple-element.35), channel_id=1, source_target_pairs={{0,8},{8,0},{16,24},{24,16},{32,40},{40,32},{48,56},{56,48},{64,72... | collective-permute-start | bytes 2359304 | tf_op jit(solution)/shard_map/ppermute | solution.py:32
  74.8 1.4 %copy-start.5 = (f32[768,512]{1,0:T(8,128)S(1)}, f32[768,512]{1,0:T(8,128)}, u32[]{:S(2)}) copy-start(f32[768,512]{1,0:T(8,128)} %copy-done.4) | copy-start | bytes 4718596
  79.3 0.9 copy-start.2
  80.1 0.7 copy-start.13
  80.8 1.5 %collective-permute-start.11 = (bf16[1,512,256]{2,1,0:T(8,128)(2,1)S(1)}, bf16[1,512,256]{2,1,0:T(8,128)(2,1)S(1)}, u32[]{:S(2)}, u32[]{:S(2)}) collective-permute-start(bf16[1,512,256]{2,1,0:T(8,128)(2,1)S(1)} %get-tuple-element.38), channel_id=1, source_target_pairs={{0,8},{8,0},{16,24},{24,16},{32,40},{40,32},{48,56},{56,48},{64,72... | collective-permute-start | bytes 786440 | tf_op jit(solution)/shard_map/ppermute | solution.py:32
  82.4 0.7 copy-start.14
  87.3 6.1 %copy-start.1 = (bf16[768,512]{1,0:T(8,128)(2,1)S(1)}, bf16[768,512]{1,0:T(8,128)(2,1)}, u32[]{:S(2)}) copy-start(bf16[768,512]{1,0:T(8,128)(2,1)} %refs_0_.3) | copy-start | bytes 2359300
  87.4 45.9 %all-to-all-start = ((bf16[8,512,256]{2,1,0:T(8,128)(2,1)}), bf16[8,512,256]{2,1,0:T(8,128)(2,1)}, u32[]{:S(2)}, u32[]{:S(2)}) async-start(bf16[8,512,256]{2,1,0:T(8,128)(2,1)} %place.1), calls=%async_computation | async-start | bytes 4194304 | tf_op jit(solution)/shard_map/all_to_all | solution.py:356
  93.5 1.1 copy-start.3
  94.6 1.0 copy-start.9
  95.6 1.0 copy-start.12
  105.4 9.2 %collective-permute-start.12 = (bf16[1536,128]{1,0:T(8,128)(2,1)S(1)}, bf16[1536,128]{1,0:T(8,128)(2,1)S(1)}, u32[]{:S(2)}, u32[]{:S(2)}) collective-permute-start(bf16[1536,128]{1,0:T(8,128)(2,1)S(1)} %get-tuple-element.47), channel_id=1, source_target_pairs={{8,0},{16,8},{24,16},{32,24},{40,32},{48,40},{56,48},{64,56},{72,6... | collective-permute-start | bytes 1179656 | tf_op jit(solution)/shard_map/ppermute | solution.py:19
  106.7 25.7 %collective-permute-start.13 = (bf16[1536,128]{1,0:T(8,128)(2,1)S(1)}, bf16[1536,128]{1,0:T(8,128)(2,1)S(1)}, u32[]{:S(2)}, u32[]{:S(2)}) collective-permute-start(bf16[1536,128]{1,0:T(8,128)(2,1)S(1)} %get-tuple-element.48), channel_id=1, source_target_pairs={{16,0},{24,8},{32,16},{40,24},{48,32},{56,40},{64,48},{72,56},{80,... | collective-permute-start | bytes 1179656 | tf_op jit(solution)/shard_map/ppermute | solution.py:19

commit v2 on v1

--- a/solution.py
+++ b/solution.py
@@ -10,7 +10,7 @@
 HEAD_SIZE = 128
 NEG_BIG = -1e30
 ROWS = 256
-VMEM_BYTES = 24 << 20
+VMEM_BYTES = 20 << 20
 
 
 def shifted(value, axis, steps):
@@ -160,11 +160,18 @@
         own_out[pl.ds(tok, tok), :] = value_sum[...].T
 
 
-def project_kernel(sources, shapes, where_ref, weight_ref, turned_ref, *refs):
+def project_kernel(sources, shapes, groups, where_ref, weight_ref, turned_ref, *refs):
     count = len(shapes)
     pieces, refs = refs[:count], refs[count:]
+    earlier, refs = refs[: 2 * len(groups)], refs[2 * len(groups) :]
+    if groups:
+        come, placed, placed_sems = refs[-3:]
+        refs = refs[:-3]
     sems, turned, weights, *buffers = refs[-3 - count :]
-    before, (total_ref, mine_ref, other_ref) = refs[: -6 - count], refs[-6 - count : -3 - count]
+    refs = refs[: -3 - count]
+    if groups:
+        placed_ref, refs = refs[-1], refs[:-1]
+    before, (total_ref, mine_ref, other_ref) = refs[:-3], refs[-3:]
     width = weights.shape[1]
     cut = width // 2
     copies = []
@@ -185,6 +192,12 @@
         if turned_copy is None:
             turned_copy = fetch(turned_ref, turned)
     pending["turned"] = turned_copy
+    at, loads = 0, []
+    for i, size in enumerate(groups):
+        for j, target in enumerate((placed, come)):
+            loads.append(pltpu.make_async_copy(earlier[2 * i + j], target.at[pl.ds(at, size)], placed_sems.at[2 * i + j]))
+            loads[-1].start()
+        at += size
     done = set()
 
     def ready(key):
@@ -218,6 +231,17 @@
                 )
                 part = term if part is None else part + term
             out[index] = part.astype(out.dtype)
+    for load in loads:
+        load.wait()
+    stores = []
+    for index in range(sum(groups)):
+        both = placed[index].astype(jnp.float32) + come[index].astype(jnp.float32)
+        placed[index] = both.astype(placed.dtype)
+        place = where_ref[1 + len(sources) + index]
+        stores.append(pltpu.make_async_copy(placed.at[index], placed_ref.at[place], placed_sems.at[2 * len(groups) + index]))
+        stores[-1].start()
+    for store in stores:
+        store.wait()
 
 
 def in_hbm(value):
@@ -228,45 +252,42 @@
     return pl.BlockSpec(memory_space=pltpu.HBM)
 
 
-def project(sources, last, flops, where, weight, turned, pieces, before):
+def project(sources, last, flops, where, weight, turned, pieces, before, earlier=()):
     width, tok = turned.shape
     count = len(sources)
     parts = jax.ShapeDtypeStruct((count, width, width // 2), jnp.bfloat16)
     pieces = [in_hbm(piece) for piece in pieces]
+    earlier = [in_hbm(part) for part in earlier]
     shapes = [piece.shape for piece in pieces]
+    groups = [part.shape[0] for part in earlier[::2]]
+    slots = (sum(groups), width, width // 2)
+    out_specs = [whole()] * 3
+    out_shape = [jax.ShapeDtypeStruct((tok, width), jnp.bfloat16 if last else jnp.float32), parts, parts]
+    scratch = [
+        pltpu.SemaphoreType.DMA((count + len(pieces) + 1,)), pltpu.VMEM((width, tok), jnp.bfloat16),
+        pltpu.VMEM((count, width, width), jnp.bfloat16),
+    ] + [pltpu.VMEM(shape, jnp.bfloat16) for shape in shapes]
+    if groups:
+        out_specs.append(hbm())
+        out_shape.append(pltpu.HBM((8,) + slots[1:], jnp.bfloat16))
+        scratch += [pltpu.VMEM(slots, jnp.bfloat16)] * 2 + [pltpu.SemaphoreType.DMA((2 * len(groups) + slots[0],))]
     return pl.pallas_call(
-        lambda *refs: project_kernel(sources, shapes, *refs),
-        in_specs=[pl.BlockSpec(memory_space=pltpu.SMEM)] + [hbm()] * (2 + len(pieces)) + [whole()] * len(before),
-        out_specs=[whole()] * 3,
-        scratch_shapes=[
-            pltpu.SemaphoreType.DMA((count + len(pieces) + 1,)), pltpu.VMEM((width, tok), jnp.bfloat16),
-            pltpu.VMEM((count, width, width), jnp.bfloat16),
-        ] + [pltpu.VMEM(shape, jnp.bfloat16) for shape in shapes],
-        out_shape=[jax.ShapeDtypeStruct((tok, width), jnp.bfloat16 if last else jnp.float32), parts, parts],
+        lambda *refs: project_kernel(sources, shapes, groups, *refs),
+        in_specs=[pl.BlockSpec(memory_space=pltpu.SMEM)] + [hbm()] * (2 + len(pieces) + len(earlier)) + [whole()] * len(before),
+        out_specs=out_specs,
+        scratch_shapes=scratch,
+        out_shape=out_shape,
         compiler_params=pltpu.CompilerParams(vmem_limit_bytes=VMEM_BYTES),
         cost_estimate=pl.CostEstimate(flops=flops, bytes_accessed=1 << 20, transcendentals=0),
         name="project",
-    )(where, weight, turned, *pieces, *before)
-
-
-def place_kernel(counts, where_ref, *refs):
-    sems, mine, come = refs[-3:]
-    out_ref, refs = refs[-4], refs[:-4]
-    copies, index = [], 0
-    for i, count in enumerate(counts):
-        rows = pl.ds(index, count)
-        for source, target, sem in ((refs[2 * i], mine, 2 * i), (refs[2 * i + 1], come, 2 * i + 1)):
-            copies.append(pltpu.make_async_copy(source, target.at[rows], sems.at[sem]))
-            copies[-1].start()
-        index += count
-    index = 0
-    for i, count in enumerate(counts):
-        copies[2 * i].wait()
-        copies[2 * i + 1].wait()
-        for _ in range(count):
-            both = mine[index].astype(jnp.float32) + come[index].astype(jnp.float32)
-            out_ref[where_ref[index]] = both.astype(out_ref.dtype)
-            index += 1
+    )(where, weight, turned, *pieces, *earlier, *before)
+
+
+def place_kernel(where_ref, mine_ref, come_ref, earlier_ref, out_ref, both, sem):
+    both[...] = (mine_ref[...].astype(jnp.float32) + come_ref[...].astype(jnp.float32)).astype(both.dtype)
+    copy = pltpu.make_async_copy(both, out_ref.at[pl.ds(where_ref[0], 1)], sem)
+    copy.start()
+    copy.wait()
 
 
 def whole():
@@ -303,15 +324,15 @@
             pl.BlockSpec((all_heads, ROWS), lambda b: (0, b)), row_block,
         ],
         out_shape=[
-            pltpu.HBM((heads, tok, span), jnp.bfloat16), rows_of(jnp.bfloat16),
-            pltpu.HBM((all_heads, tok), jnp.bfloat16), rows_of(jnp.float32),
+            pltpu.HBM((heads, tok, span), jnp.bfloat16), pltpu.HBM((tok, all_heads), jnp.bfloat16),
+            pltpu.HBM((all_heads, tok), jnp.bfloat16), pltpu.HBM((tok, all_heads), jnp.float32),
         ],
         scratch_shapes=held + [pltpu.VMEM((ROWS, span), jnp.float32)],
         compiler_params=pltpu.CompilerParams(vmem_limit_bytes=VMEM_BYTES),
         cost_estimate=pl.CostEstimate(flops=2 * work, bytes_accessed=14 << 20, transcendentals=heads * tok * span),
         name="forward",
     )(low, queries, far, near, own)
-    expo = in_hbm(expo)
+    expo, attn, inverse, queries = in_hbm(expo), in_hbm(attn), in_hbm(inverse), in_hbm(queries)
 
     tensor = lax.axis_index("tensor")
     row, column = tensor // 4, tensor % 4
@@ -325,32 +346,33 @@
     across_up, across_down = step_x(across, 1), step_x(across, -1)
     weight, turned = in_hbm(out_weight), in_hbm(turned)
     real = lambda count: 4 * count * tok * all_heads * all_heads
+    last = step_y(opposite)
     total, mine_a, other_a = project(
-        [((p, 0, 0, tok),) for p in range(4)], False, real(4),
-        where(places[:4]), weight, turned, (out_grad, near_up, near_down, opposite), (),
-    )
-    last = step_y(opposite)
+        [((p, 0, 0, tok),) for p in range(5)], False, real(5),
+        where(places[:5]), weight, turned, (out_grad, near_up, near_down, opposite, across), (),
+    )
+    come_a = step_core(other_a)
     total, mine_b, other_b = project(
-        [((p, 0, 0, tok),) for p in range(3)], False, 4 * real(3),
-        where(places[4:7]), weight, turned, (across, across_up, across_down), (total,),
-    )
-    attention_gradient, mine_c, other_c = project(
-        [((0, 0, 0, tok),)], True, 1 << 20,
-        where(places[7:]), weight, turned, (last,), (total,),
-    )
-    parts = [mine_a, step_core(other_a), mine_b, step_core(other_b), mine_c, step_core(other_c)]
-    counts = [part.shape[0] for part in parts[::2]]
-    both = pltpu.VMEM((8,) + mine_a.shape[1:], jnp.bfloat16)
+        [((p, 0, 0, tok),) for p in range(2)], False, 1 << 20,
+        where(places[5:7]), weight, turned, (across_up, across_down), (total,),
+    )
+    come_b = step_core(other_b)
+    attention_gradient, mine_c, other_c, placed = project(
+        [((0, 0, 0, tok),)], True, 1 << 20, where(places[7:] + places[:7]), weight, turned, (last,), (total,),
+        (mine_a, come_a, mine_b, come_b),
+    )
+    come_c = step_core(other_c)
     placed = pl.pallas_call(
-        lambda *refs: place_kernel(counts, *refs),
-        in_specs=[pl.BlockSpec(memory_space=pltpu.SMEM)] + [hbm()] * 6,
-        out_specs=whole(),
-        out_shape=jax.ShapeDtypeStruct((8,) + mine_a.shape[1:], jnp.bfloat16),
-        scratch_shapes=[pltpu.SemaphoreType.DMA((6,)), both, both],
+        place_kernel,
+        in_specs=[pl.BlockSpec(memory_space=pltpu.SMEM), whole(), whole(), hbm()],
+        out_specs=hbm(),
+        out_shape=pltpu.HBM(placed.shape, placed.dtype),
+        input_output_aliases={3: 0},
+        scratch_shapes=[pltpu.VMEM(mine_c.shape, mine_c.dtype), pltpu.SemaphoreType.DMA(())],
         compiler_params=pltpu.CompilerParams(vmem_limit_bytes=VMEM_BYTES),
         cost_estimate=pl.CostEstimate(flops=1 << 20, bytes_accessed=1 << 20, transcendentals=0),
         name="place",
-    )(jnp.stack(places).astype(jnp.int32), *[in_hbm(part) for part in parts])
+    )(jnp.stack(places[7:]).astype(jnp.int32), mine_c, come_c, placed)
     placed, attention_gradient = lax.optimization_barrier((placed, attention_gradient))
     groups = [[2 * chip + c for chip in range(8)] for c in range(2)]
     arrived = lax.all_to_all(placed, "seq", 0, 0, axis_index_groups=groups)
@@ -382,6 +404,7 @@
         cost_estimate=pl.CostEstimate(flops=1 << 20, bytes_accessed=1 << 20, transcendentals=0),
         name="backward_own",
     )(queries, attention_gradient, attn, inverse, *([expo] * blocks), own, past_queries)
+    own_sum, weight_grad = lax.optimization_barrier((own_sum, weight_grad))
     total = own_sum + near_come.astype(jnp.float32) + far_come.astype(jnp.float32)
     total = total.astype(jnp.bfloat16)
     return (grad_queries, total[:tok], total[tok:], weight_grad)

time: 137 us -> 135 us (0.985)
  local copies, waits for them, and re-layouts: 13.7 us -> 9.05 us
  waiting for transfers between devices: 37 us -> 39.1 us
  starting transfers between devices: 29 us -> 30.6 us
    ppermute x4, waiting for transfers between devices: 22.3 us -> 10.7 us  [shifted(): lax.ppermute(value, axis, [(source, source + steps) for source in range(i...]
    all_to_all x1, waiting for transfers between devices: 0.01 us -> 9.37 us  [local(): arrived = lax.all_to_all(placed, 'seq', 0, 0, axis_index_groups=groups)]
    ppermute x2, waiting for transfers between devices: 0.6 us -> 9.51 us  [step_y(): return lax.ppermute(value, 'tensor', [(t, t ^ 4) for t in range(8)])]
    ppermute x5, waiting for transfers between devices: 12.8 us -> 7.98 us  [step_x(): return lax.ppermute(value, 'tensor', pairs)]
    unnamed x30 -> x16, local copies, waits for them, and re-layouts: 12.8 us -> 8.12 us
    pallas_call x4, Pallas kernels: 20.5 us -> 18.5 us  [the longest x3 17.7 us: project(): pl.pallas_call(lambda *refs: project_kernel(sources, shapes, groups, *ref...]
    ppermute x5, starting transfers between devices: 7.88 us -> 9.58 us  [step_x(): return lax.ppermute(value, 'tensor', pairs)]
  transfers between devices with their start and end apart: 15 -> 15, of which waited for: 7 -> 8; matrix products, arithmetic and copies ran while one was open for 3% -> 4% of each run, Pallas kernels for 32% -> 31%
where the time goes in v2:
time: 135 us
  Pallas kernels  48.1 us (36%)
  waiting for transfers between devices  39.1 us (29%)
  starting transfers between devices  30.6 us (23%)
  local copies, waits for them, and re-layouts  9.05 us (7%)
  other arithmetic  6.99 us (5%)
    pallas_call x3, Pallas kernels, project(): pl.pallas_call(lambda *refs: project_kernel(sources, shapes, groups, *ref...  17.7 us
    pallas_call x1, Pallas kernels, local(): pl.pallas_call(lambda *refs: forward_kernel(tok, span, heads, *refs), gri...  13.3 us
    ppermute x4, waiting for transfers between devices, shifted(): lax.ppermute(value, axis, [(source, source + steps) for source in range(i...  10.7 us
    ppermute x5, starting transfers between devices, step_x(): return lax.ppermute(value, 'tensor', pairs)  9.58 us
    ppermute x2, waiting for transfers between devices, step_y(): return lax.ppermute(value, 'tensor', [(t, t ^ 4) for t in range(8)])  9.51 us
    all_to_all x1, waiting for transfers between devices, local(): arrived = lax.all_to_all(placed, 'seq', 0, 0, axis_index_groups=groups)  9.37 us
    pallas_call x1, Pallas kernels, local(): pl.pallas_call(lambda *refs: backward_past_kernel(tok, heads, *refs), gri...  9.24 us
    ppermute x4, starting transfers between devices, shifted(): lax.ppermute(value, axis, [(source, source + steps) for source in range(i...  8.31 us
  transfers between devices with their start and end apart: 15, of which 8 were waited for; matrix products, arithmetic and copies ran while one was open for 4% of the time, Pallas kernels for 31%

profile of v2, /device:TPU:0, one launch (start us, length us, event | category | flops | bytes accessed | tf_op | source)
XLA Modules:
  0.0 134.6 jit_solution(16370261063295946620)
XLA Ops:
  1.3 1.0 fusion.1.refs_4_.refs_7_
  2.4 1.3 collective-permute-start.1
  3.7 4.2 %collective-permute-start = (bf16[1552,128]{1,0:T(8,128)(2,1)S(1)}, bf16[1552,128]{1,0:T(8,128)(2,1)S(1)}, u32[]{:S(2)}, u32[]{:S(2)}) collective-permute-start(bf16[1552,128]{1,0:T(8,128)(2,1)S(1)} %fusion.1.refs_4_.refs_7_), channel_id=1, source_target_pairs={{0,16},{8,24},{16,32},{24,40},{32,48},{40,56},{48,64},{56,72},{64,... | collective-permute-start | bytes 1191944 | tf_op jit(solution)/shard_map/ppermute | solution.py:19
  7.9 3.1 %collective-permute-start.3 = (bf16[768,512]{1,0:T(8,128)(2,1)}, bf16[768,512]{1,0:T(8,128)(2,1)}, u32[]{:S(2)}, u32[]{:S(2)}) collective-permute-start(bf16[768,512]{1,0:T(8,128)(2,1)} %refs_3_.1), channel_id=1, source_target_pairs={{0,2},{1,3},{2,0},{3,1},{4,6},{5,7},{6,4},{7,5},{8,10},{9,11},{10,... | collective-permute-start | bytes 2359304 | tf_op jit(solution)/shard_map/ppermute | solution.py:24
  11.6 2.6 %collective-permute-start.6 = (bf16[768,512]{1,0:T(8,128)(2,1)}, bf16[768,512]{1,0:T(8,128)(2,1)}, u32[]{:S(2)}, u32[]{:S(2)}) collective-permute-start(bf16[768,512]{1,0:T(8,128)(2,1)} %refs_3_.1), channel_id=1, source_target_pairs={{0,3},{1,0},{2,1},{3,2},{4,7},{5,4},{6,5},{7,6},{8,11},{9,8},{10,9... | collective-permute-start | bytes 2359304 | tf_op jit(solution)/shard_map/ppermute | solution.py:24
  14.3 3.2 %collective-permute-done.refs_2_.refs_5_ = bf16[1552,128]{1,0:T(8,128)(2,1)S(1)} collective-permute-done((bf16[1552,128]{1,0:T(8,128)(2,1)S(1)}, bf16[1552,128]{1,0:T(8,128)(2,1)S(1)}, u32[]{:S(2)}, u32[]{:S(2)}) %collective-permute-start) | collective-permute-done | bytes 397344 | tf_op jit(solution)/shard_map/ppermute | solution.py:19
  17.5 2.9 %collective-permute-start.2 = (bf16[768,512]{1,0:T(8,128)(2,1)}, bf16[768,512]{1,0:T(8,128)(2,1)}, u32[]{:S(2)}, u32[]{:S(2)}) collective-permute-start(bf16[768,512]{1,0:T(8,128)(2,1)} %refs_3_.1), channel_id=1, source_target_pairs={{0,4},{1,5},{2,6},{3,7},{4,0},{5,1},{6,2},{7,3},{8,12},{9,13},{10,... | collective-permute-start | bytes 2359304 | tf_op jit(solution)/shard_map/ppermute | solution.py:28
  21.1 1.5 %convert_reduce_fusion = s32[768]{0:T(1024)S(1)} fusion(s32[2304]{0:T(1024)S(1)} %pad_add_fusion, s32[768]{0:T(1024)} %param.11), kind=kLoop, calls=%fused_computation | loop fusion | flops 5307648 | bytes 15360 | tf_op jit(solution)/shard_map/reduce_sum | solution.py:310
  22.8 1.1 copy-done
  24.0 13.3 %forward.1 = (bf16[4,768,1792]{2,1,0:T(8,128)(2,1)}, bf16[768,512]{1,0:T(8,128)(2,1)}, bf16[512,768]{1,0:T(8,128)(2,1)}, f32[768,512]{1,0:T(8,128)}) custom-call(s32[768,1]{1,0:T(8,128)S(1)} %reshape_maximum_fusion.refs_0_, bf16[768,512]{1,0:T(8,128)(2,1)S(1)} %copy-done, bf16[1552,128]{1,0:T(8,128)(2,1)S(1)} %collective-permute-done.refs_2_.refs_5_, ...), custom_call_target="tpu_custom_call" | custom-call | flops 2818572288 | bytes 14680064 | tf_op jit(solution)/shard_map/forward/pallas_call | solution.py:318
  37.2 1.7 %collective-permute-done.2.refs_7_ = bf16[768,512]{1,0:T(8,128)(2,1)} collective-permute-done((bf16[768,512]{1,0:T(8,128)(2,1)}, bf16[768,512]{1,0:T(8,128)(2,1)}, u32[]{:S(2)}, u32[]{:S(2)}) %collective-permute-start.2) | collective-permute-done | bytes 786464 | tf_op jit(solution)/shard_map/ppermute | solution.py:28
  38.9 1.5 %collective-permute-start.8 = (bf16[768,512]{1,0:T(8,128)(2,1)}, bf16[768,512]{1,0:T(8,128)(2,1)S(1)}, u32[]{:S(2)}, u32[]{:S(2)}) collective-permute-start(bf16[768,512]{1,0:T(8,128)(2,1)} %collective-permute-done.2.refs_7_), channel_id=1, source_target_pairs={{0,1},{1,2},{2,3},{3,0},{4,5},{5,6},{6,7},{7,4},{8,9},{9,10},{10,1... | collective-permute-start | bytes 2359304 | tf_op jit(solution)/shard_map/ppermute | solution.py:24
  40.4 1.7 %collective-permute-start.9 = (bf16[768,512]{1,0:T(8,128)(2,1)}, bf16[768,512]{1,0:T(8,128)(2,1)}, u32[]{:S(2)}, u32[]{:S(2)}) collective-permute-start(bf16[768,512]{1,0:T(8,128)(2,1)} %collective-permute-done.2.refs_7_), channel_id=1, source_target_pairs={{0,3},{1,0},{2,1},{3,2},{4,7},{5,4},{6,5},{7,6},{8,11},{9,8},{10,9... | collective-permute-start | bytes 2359304 | tf_op jit(solution)/shard_map/ppermute | solution.py:24
  42.2 4.7 %collective-permute-done.5.refs_4_ = bf16[768,512]{1,0:T(8,128)(2,1)S(1)} collective-permute-done((bf16[768,512]{1,0:T(8,128)(2,1)}, bf16[768,512]{1,0:T(8,128)(2,1)S(1)}, u32[]{:S(2)}, u32[]{:S(2)}) %collective-permute-start.5) | collective-permute-done | bytes 786464 | tf_op jit(solution)/shard_map/ppermute | solution.py:24
  47.8 8.2 %project.3 = (f32[768,512]{1,0:T(8,128)S(1)}, bf16[5,512,256]{2,1,0:T(8,128)(2,1)S(1)}, bf16[5,512,256]{2,1,0:T(8,128)(2,1)}) custom-call(s32[6]{0:T(128)S(1)} %stack.56.refs_0_, bf16[512,4096]{1,0:T(8,128)(2,1)} %refs_1_.7, bf16[512,768]{1,0:T(8,128)(2,1)} %get-tuple-element.32.refs_2_, bf16[768,512]{1,0:T(8,128)(2,1)} %refs_3_.1, ...), custom_call_target="tpu_custom_call" | custom-call | flops 4026531840 | bytes 1048576 | tf_op jit(solution)/shard_map/project/pallas_call | solution.py:274
  56.1 1.1 copy-done.3
  57.3 3.2 %collective-permute-start.4 = (bf16[768,512]{1,0:T(8,128)(2,1)}, bf16[768,512]{1,0:T(8,128)(2,1)}, u32[]{:S(2)}, u32[]{:S(2)}) collective-permute-start(bf16[768,512]{1,0:T(8,128)(2,1)} %collective-permute-done.3.refs_6_), channel_id=1, source_target_pairs={{0,4},{1,5},{2,6},{3,7},{4,0},{5,1},{6,2},{7,3},{8,12},{9,13},{10,... | collective-permute-start | bytes 2359304 | tf_op jit(solution)/shard_map/ppermute | solution.py:28
  60.6 3.2 %collective-permute-done.8.refs_3_ = bf16[768,512]{1,0:T(8,128)(2,1)S(1)} collective-permute-done((bf16[768,512]{1,0:T(8,128)(2,1)}, bf16[768,512]{1,0:T(8,128)(2,1)S(1)}, u32[]{:S(2)}, u32[]{:S(2)}) %collective-permute-start.8) | collective-permute-done | bytes 786464 | tf_op jit(solution)/shard_map/ppermute | solution.py:24
  64.7 4.2 %project.4 = (f32[768,512]{1,0:T(8,128)S(1)}, bf16[2,512,256]{2,1,0:T(8,128)(2,1)S(1)}, bf16[2,512,256]{2,1,0:T(8,128)(2,1)S(1)}) custom-call(s32[3]{0:T(128)S(1)} %pad_add_fusion.1.refs_0_, bf16[512,4096]{1,0:T(8,128)(2,1)} %refs_1_.7, bf16[512,768]{1,0:T(8,128)(2,1)} %get-tuple-element.32.refs_2_, bf16[768,512]{1,0:T(8,128)(2,1)} %copy-done.5, ...), custom_call_target="tpu_custom_call" | custom-call | flops 1048576 | bytes 1048576 | tf_op jit(solution)/shard_map/project/pallas_call | solution.py:274
  68.8 1.2 copy-done.1
  71.1 7.8 %collective-permute-done.4.refs_3_ = bf16[768,512]{1,0:T(8,128)(2,1)} collective-permute-done((bf16[768,512]{1,0:T(8,128)(2,1)}, bf16[768,512]{1,0:T(8,128)(2,1)}, u32[]{:S(2)}, u32[]{:S(2)}) %collective-permute-start.4) | collective-permute-done | bytes 786464 | tf_op jit(solution)/shard_map/ppermute | solution.py:28
  79.7 1.4 %copy-done.2 = f32[768,512]{1,0:T(8,128)S(1)} copy-done((f32[768,512]{1,0:T(8,128)S(1)}, f32[768,512]{1,0:T(8,128)}, u32[]{:S(2)}) %copy-start.2) | copy-done | bytes 1572888
  81.1 5.3 %project.5 = (bf16[768,512]{1,0:T(8,128)(2,1)S(1)}, bf16[1,512,256]{2,1,0:T(8,128)(2,1)S(1)}, bf16[1,512,256]{2,1,0:T(8,128)(2,1)S(1)}, bf16[8,512,256]{2,1,0:T(8,128)(2,1)}) custom-call(s32[9]{0:T(128)S(1)} %stack.55.refs_0_, bf16[512,4096]{1,0:T(8,128)(2,1)} %refs_1_.7, bf16[512,768]{1,0:T(8,128)(2,1)} %get-tuple-element.32.refs_2_, ...), custom_call_target="tpu_custom_call" | custom-call | flops 1048576 | bytes 1048576 | tf_op jit(solution)/shard_map/project/pallas_call | solution.py:274
  86.6 1.5 %collective-permute-done.11.come_ref = bf16[1,512,256]{2,1,0:T(8,128)(2,1)S(1)} collective-permute-done((bf16[1,512,256]{2,1,0:T(8,128)(2,1)S(1)}, bf16[1,512,256]{2,1,0:T(8,128)(2,1)S(1)}, u32[]{:S(2)}, u32[]{:S(2)}) %collective-permute-start.11) | collective-permute-done | bytes 262176 | tf_op jit(solution)/shard_map/ppermute | solution.py:32
  88.9 6.1 %all-to-all-start = ((bf16[8,512,256]{2,1,0:T(8,128)(2,1)}), bf16[8,512,256]{2,1,0:T(8,128)(2,1)}, u32[]{:S(2)}, u32[]{:S(2)}) async-start(bf16[8,512,256]{2,1,0:T(8,128)(2,1)} %place.1), calls=%async_computation | async-start | bytes 4194304 | tf_op jit(solution)/shard_map/all_to_all | solution.py:378
  95.0 9.2 %backward_past.1 = (f32[768,512]{1,0:T(8,128)S(1)}, bf16[1536,128]{1,0:T(8,128)(2,1)S(1)}, bf16[1536,128]{1,0:T(8,128)(2,1)S(1)}) custom-call(bf16[768,512]{1,0:T(8,128)(2,1)} %refs_0_.3, bf16[768,512]{1,0:T(8,128)(2,1)S(1)} %get-tuple-element.44.refs_1_, bf16[768,512]{1,0:T(8,128)(2,1)} %get-tuple-element.45.refs_2_, f32[768,512]{1,0:T(8,128)} %get-tuple-element.46.refs_3_, ...), custom_call_target="tpu_custom_call" | custom-call | flops 1048576 | bytes 1048576 | tf_op jit(solution)/shard_map/backward_past/pallas_call | solution.py:383
  104.2 1.3 collective-permute-start.12
  105.5 1.5 %collective-permute-start.13 = (bf16[1536,128]{1,0:T(8,128)(2,1)S(1)}, bf16[1536,128]{1,0:T(8,128)(2,1)S(1)}, u32[]{:S(2)}, u32[]{:S(2)}) collective-permute-start(bf16[1536,128]{1,0:T(8,128)(2,1)S(1)} %get-tuple-element.54), channel_id=1, source_target_pairs={{16,0},{24,8},{32,16},{40,24},{48,32},{56,40},{64,48},{72,56},{80,... | collective-permute-start | bytes 1179656 | tf_op jit(solution)/shard_map/ppermute | solution.py:19
  107.0 7.1 %backward_own.1 = (bf16[768,512]{1,0:T(8,128)(2,1)}, f32[1536,128]{1,0:T(8,128)S(1)}) custom-call(bf16[768,512]{1,0:T(8,128)(2,1)} %refs_0_.3, bf16[768,512]{1,0:T(8,128)(2,1)S(1)} %get-tuple-element.44.refs_1_, bf16[768,512]{1,0:T(8,128)(2,1)} %get-tuple-element.45.refs_2_, f32[768,512]{1,0:T(8,128)} %get-tuple-element.46.refs_3_, ...), custom_call_target="tpu_custom_call" | custom-call | flops 1048576 | bytes 1048576 | tf_op jit(solution)/shard_map/backward_own/pallas_call | solution.py:396
  114.1 9.4 %all-to-all-done = bf16[8,512,256]{2,1,0:T(8,128)(2,1)} async-done(((bf16[8,512,256]{2,1,0:T(8,128)(2,1)}), bf16[8,512,256]{2,1,0:T(8,128)(2,1)}, u32[]{:S(2)}, u32[]{:S(2)}) %all-to-all-start) | async-done | bytes 2097184 | tf_op jit(solution)/shard_map/all_to_all | solution.py:378
  123.5 2.6 %reduce_sum.25 = bf16[512,256]{1,0:T(8,128)(2,1)} reduce(bf16[8,512,256]{2,1,0:T(8,128)(2,1)} %all-to-all-done, bf16[]{:T(256)} %constant.75.clone.1), dimensions={0}, to_apply=%region_1.2 | reduce | flops 917504 | bytes 2359298 | tf_op jit(solution)/shard_map/reduce_sum | solution.py:379
  126.1 7.5 %collective-permute-done.13 = bf16[1536,128]{1,0:T(8,128)(2,1)S(1)} collective-permute-done((bf16[1536,128]{1,0:T(8,128)(2,1)S(1)}, bf16[1536,128]{1,0:T(8,128)(2,1)S(1)}, u32[]{:S(2)}, u32[]{:S(2)}) %collective-permute-start.13) | collective-permute-done | bytes 393248 | tf_op jit(solution)/shard_map/ppermute | solution.py:19
  (34 shorter events, 8.0 us)
Async XLA Ops:
  2.4 12.0 %collective-permute-start.1 = (bf16[1552,128]{1,0:T(8,128)(2,1)S(1)}, bf16[1552,128]{1,0:T(8,128)(2,1)S(1)}, u32[]{:S(2)}, u32[]{:S(2)}) collective-permute-start(bf16[1552,128]{1,0:T(8,128)(2,1)S(1)} %fusion.1.refs_4_.refs_7_), channel_id=1, source_target_pairs={{0,8},{8,16},{16,24},{24,32},{32,40},{40,48},{48,56},{56,64},{64,7... | collective-permute-start | bytes 1191944 | tf_op jit(solution)/shard_map/ppermute | solution.py:19
  3.7 13.8 %collective-permute-start = (bf16[1552,128]{1,0:T(8,128)(2,1)S(1)}, bf16[1552,128]{1,0:T(8,128)(2,1)S(1)}, u32[]{:S(2)}, u32[]{:S(2)}) collective-permute-start(bf16[1552,128]{1,0:T(8,128)(2,1)S(1)} %fusion.1.refs_4_.refs_7_), channel_id=1, source_target_pairs={{0,16},{8,24},{16,32},{24,40},{32,48},{40,56},{48,64},{56,72},{64,... | collective-permute-start | bytes 1191944 | tf_op jit(solution)/shard_map/ppermute | solution.py:19
  7.9 34.3 %collective-permute-start.3 = (bf16[768,512]{1,0:T(8,128)(2,1)}, bf16[768,512]{1,0:T(8,128)(2,1)}, u32[]{:S(2)}, u32[]{:S(2)}) collective-permute-start(bf16[768,512]{1,0:T(8,128)(2,1)} %refs_3_.1), channel_id=1, source_target_pairs={{0,2},{1,3},{2,0},{3,1},{4,6},{5,7},{6,4},{7,5},{8,10},{9,11},{10,... | collective-permute-start | bytes 2359304 | tf_op jit(solution)/shard_map/ppermute | solution.py:24
  11.0 35.9 %collective-permute-start.5 = (bf16[768,512]{1,0:T(8,128)(2,1)}, bf16[768,512]{1,0:T(8,128)(2,1)S(1)}, u32[]{:S(2)}, u32[]{:S(2)}) collective-permute-start(bf16[768,512]{1,0:T(8,128)(2,1)} %refs_3_.1), channel_id=1, source_target_pairs={{0,1},{1,2},{2,3},{3,0},{4,5},{5,6},{6,7},{7,4},{8,9},{9,10},{10,1... | collective-permute-start | bytes 2359304 | tf_op jit(solution)/shard_map/ppermute | solution.py:24
  11.6 36.2 %collective-permute-start.6 = (bf16[768,512]{1,0:T(8,128)(2,1)}, bf16[768,512]{1,0:T(8,128)(2,1)}, u32[]{:S(2)}, u32[]{:S(2)}) collective-permute-start(bf16[768,512]{1,0:T(8,128)(2,1)} %refs_3_.1), channel_id=1, source_target_pairs={{0,3},{1,0},{2,1},{3,2},{4,7},{5,4},{6,5},{7,6},{8,11},{9,8},{10,9... | collective-permute-start | bytes 2359304 | tf_op jit(solution)/shard_map/ppermute | solution.py:24
  17.5 21.4 %collective-permute-start.2 = (bf16[768,512]{1,0:T(8,128)(2,1)}, bf16[768,512]{1,0:T(8,128)(2,1)}, u32[]{:S(2)}, u32[]{:S(2)}) collective-permute-start(bf16[768,512]{1,0:T(8,128)(2,1)} %refs_3_.1), channel_id=1, source_target_pairs={{0,4},{1,5},{2,6},{3,7},{4,0},{5,1},{6,2},{7,3},{8,12},{9,13},{10,... | collective-permute-start | bytes 2359304 | tf_op jit(solution)/shard_map/ppermute | solution.py:28
  22.8 1.1 copy-start
  38.9 24.8 %collective-permute-start.8 = (bf16[768,512]{1,0:T(8,128)(2,1)}, bf16[768,512]{1,0:T(8,128)(2,1)S(1)}, u32[]{:S(2)}, u32[]{:S(2)}) collective-permute-start(bf16[768,512]{1,0:T(8,128)(2,1)} %collective-permute-done.2.refs_7_), channel_id=1, source_target_pairs={{0,1},{1,2},{2,3},{3,0},{4,5},{5,6},{6,7},{7,4},{8,9},{9,10},{10,1... | collective-permute-start | bytes 2359304 | tf_op jit(solution)/shard_map/ppermute | solution.py:24
  40.4 23.4 %collective-permute-start.9 = (bf16[768,512]{1,0:T(8,128)(2,1)}, bf16[768,512]{1,0:T(8,128)(2,1)}, u32[]{:S(2)}, u32[]{:S(2)}) collective-permute-start(bf16[768,512]{1,0:T(8,128)(2,1)} %collective-permute-done.2.refs_7_), channel_id=1, source_target_pairs={{0,3},{1,0},{2,1},{3,2},{4,7},{5,4},{6,5},{7,6},{8,11},{9,8},{10,9... | collective-permute-start | bytes 2359304 | tf_op jit(solution)/shard_map/ppermute | solution.py:24
  46.9 0.9 copy-start.7
  56.1 1.1 copy-start.3
  57.1 21.8 %collective-permute-start.7 = (bf16[5,512,256]{2,1,0:T(8,128)(2,1)}, bf16[5,512,256]{2,1,0:T(8,128)(2,1)}, u32[]{:S(2)}, u32[]{:S(2)}) collective-permute-start(bf16[5,512,256]{2,1,0:T(8,128)(2,1)} %get-tuple-element.35), channel_id=1, source_target_pairs={{0,8},{8,0},{16,24},{24,16},{32,40},{40,32},{48,56},{56,48},{64,72... | collective-permute-start | bytes 3932168 | tf_op jit(solution)/shard_map/ppermute | solution.py:32
  57.3 21.6 %collective-permute-start.4 = (bf16[768,512]{1,0:T(8,128)(2,1)}, bf16[768,512]{1,0:T(8,128)(2,1)}, u32[]{:S(2)}, u32[]{:S(2)}) collective-permute-start(bf16[768,512]{1,0:T(8,128)(2,1)} %collective-permute-done.3.refs_6_), channel_id=1, source_target_pairs={{0,4},{1,5},{2,6},{3,7},{4,0},{5,1},{6,2},{7,3},{8,12},{9,13},{10,... | collective-permute-start | bytes 2359304 | tf_op jit(solution)/shard_map/ppermute | solution.py:28
  63.8 0.9 copy-start.5
  68.8 1.2 copy-start.1
  70.0 0.8 copy-start.4
  70.8 8.1 %collective-permute-start.10 = (bf16[2,512,256]{2,1,0:T(8,128)(2,1)S(1)}, bf16[2,512,256]{2,1,0:T(8,128)(2,1)S(1)}, u32[]{:S(2)}, u32[]{:S(2)}) collective-permute-start(bf16[2,512,256]{2,1,0:T(8,128)(2,1)S(1)} %get-tuple-element.38), channel_id=1, source_target_pairs={{0,8},{8,0},{16,24},{24,16},{32,40},{40,32},{48,56},{56,48},{64,72... | collective-permute-start | bytes 1572872 | tf_op jit(solution)/shard_map/ppermute | solution.py:32
  78.9 0.8 copy-start.6
  79.7 1.4 %copy-start.2 = (f32[768,512]{1,0:T(8,128)S(1)}, f32[768,512]{1,0:T(8,128)}, u32[]{:S(2)}) copy-start(f32[768,512]{1,0:T(8,128)} %copy-done.1) | copy-start | bytes 4718596
  86.5 1.6 %collective-permute-start.11 = (bf16[1,512,256]{2,1,0:T(8,128)(2,1)S(1)}, bf16[1,512,256]{2,1,0:T(8,128)(2,1)S(1)}, u32[]{:S(2)}, u32[]{:S(2)}) collective-permute-start(bf16[1,512,256]{2,1,0:T(8,128)(2,1)S(1)} %get-tuple-element.41), channel_id=1, source_target_pairs={{0,8},{8,0},{16,24},{24,16},{32,40},{40,32},{48,56},{56,48},{64,72... | collective-permute-start | bytes 786440 | tf_op jit(solution)/shard_map/ppermute | solution.py:32
  88.9 34.6 %all-to-all-start = ((bf16[8,512,256]{2,1,0:T(8,128)(2,1)}), bf16[8,512,256]{2,1,0:T(8,128)(2,1)}, u32[]{:S(2)}, u32[]{:S(2)}) async-start(bf16[8,512,256]{2,1,0:T(8,128)(2,1)} %place.1), calls=%async_computation | async-start | bytes 4194304 | tf_op jit(solution)/shard_map/all_to_all | solution.py:378
  104.2 21.9 %collective-permute-start.12 = (bf16[1536,128]{1,0:T(8,128)(2,1)S(1)}, bf16[1536,128]{1,0:T(8,128)(2,1)S(1)}, u32[]{:S(2)}, u32[]{:S(2)}) collective-permute-start(bf16[1536,128]{1,0:T(8,128)(2,1)S(1)} %get-tuple-element.53), channel_id=1, source_target_pairs={{8,0},{16,8},{24,16},{32,24},{40,32},{48,40},{56,48},{64,56},{72,6... | collective-permute-start | bytes 1179656 | tf_op jit(solution)/shard_map/ppermute | solution.py:19
  105.5 28.2 %collective-permute-start.13 = (bf16[1536,128]{1,0:T(8,128)(2,1)S(1)}, bf16[1536,128]{1,0:T(8,128)(2,1)S(1)}, u32[]{:S(2)}, u32[]{:S(2)}) collective-permute-start(bf16[1536,128]{1,0:T(8,128)(2,1)S(1)} %get-tuple-element.54), channel_id=1, source_target_pairs={{16,0},{24,8},{32,16},{40,24},{48,32},{56,40},{64,48},{72,56},{80,... | collective-permute-start | bytes 1179656 | tf_op jit(solution)/shard_map/ppermute | solution.py:19

commit v3 on v2

--- a/solution.py
+++ b/solution.py
@@ -338,7 +338,7 @@
     row, column = tensor // 4, tensor % 4
     at = lambda flip, step: (row ^ flip) * 4 + (column + step) % 4
     core = shard % 2
-    places = [at(0, 0), at(0, 3), at(0, 1), at(0, 2), at(1, 0), at(1, 3), at(1, 1), at(1, 2)]
+    places = [at(0, 0), at(0, 3), at(0, 1), at(1, 0), at(0, 2), at(1, 3), at(1, 1), at(1, 2)]
     where = lambda some: jnp.stack([core, *some]).astype(jnp.int32)
     near_up, near_down, opposite = step_x(out_grad, 1), step_x(out_grad, -1), step_x(out_grad, 2)
     across = step_y(lax.optimization_barrier((out_grad, far, near))[0])
@@ -348,13 +348,13 @@
     real = lambda count: 4 * count * tok * all_heads * all_heads
     last = step_y(opposite)
     total, mine_a, other_a = project(
-        [((p, 0, 0, tok),) for p in range(5)], False, real(5),
-        where(places[:5]), weight, turned, (out_grad, near_up, near_down, opposite, across), (),
+        [((p, 0, 0, tok),) for p in range(4)], False, real(4),
+        where(places[:4]), weight, turned, (out_grad, near_up, near_down, across), (),
     )
     come_a = step_core(other_a)
     total, mine_b, other_b = project(
-        [((p, 0, 0, tok),) for p in range(2)], False, 1 << 20,
-        where(places[5:7]), weight, turned, (across_up, across_down), (total,),
+        [((p, 0, 0, tok),) for p in range(3)], False, real(3),
+        where(places[4:7]), weight, turned, (opposite, across_up, across_down), (total,),
     )
     come_b = step_core(other_b)
     attention_gradient, mine_c, other_c, placed = project(

time: 135 us -> 131 us (0.970)
  local copies, waits for them, and re-layouts: 9.05 us -> 4.75 us
  waiting for transfers between devices: 39.1 us -> 37 us
  starting transfers between devices: 30.6 us -> 32 us
    unnamed x16 -> x12, local copies, waits for them, and re-layouts: 8.12 us -> 3.81 us
    ppermute x2, waiting for transfers between devices: 9.51 us -> 6.51 us  [step_y(): return lax.ppermute(value, 'tensor', [(t, t ^ 4) for t in range(8)])]
    ppermute x3, starting transfers between devices: 0.52 us -> 3.4 us  [step_core(): return lax.ppermute(value, 'seq', [(s, s ^ 1) for s in range(16)])]
  transfers between devices with their start and end apart: 15 -> 15, of which waited for: 8 -> 7; matrix products, arithmetic and copies ran while one was open for 4% -> 4% of each run, Pallas kernels for 31% -> 32%
where the time goes in v3:
time: 131 us; the launch traced here: 129 us
  Pallas kernels  47.8 us (36%)
  waiting for transfers between devices  37 us (28%)
  starting transfers between devices  32 us (24%)
  other arithmetic  7 us (5%)
  local copies, waits for them, and re-layouts  4.75 us (4%)
    pallas_call x3, Pallas kernels, project(): pl.pallas_call(lambda *refs: project_kernel(sources, shapes, groups, *ref...  17.5 us
    pallas_call x1, Pallas kernels, local(): pl.pallas_call(lambda *refs: forward_kernel(tok, span, heads, *refs), gri...  13.3 us
    ppermute x4, waiting for transfers between devices, shifted(): lax.ppermute(value, axis, [(source, source + steps) for source in range(i...  12 us
    all_to_all x1, waiting for transfers between devices, local(): arrived = lax.all_to_all(placed, 'seq', 0, 0, axis_index_groups=groups)  9.37 us
    pallas_call x1, Pallas kernels, local(): pl.pallas_call(lambda *refs: backward_past_kernel(tok, heads, *refs), gri...  9.24 us
    ppermute x5, starting transfers between devices, step_x(): return lax.ppermute(value, 'tensor', pairs)  8.35 us
    ppermute x4, starting transfers between devices, shifted(): lax.ppermute(value, axis, [(source, source + steps) for source in range(i...  8.31 us
    ppermute x5, waiting for transfers between devices, step_x(): return lax.ppermute(value, 'tensor', pairs)  7.5 us
  transfers between devices with their start and end apart: 15, of which 7 were waited for; matrix products, arithmetic and copies ran while one was open for 4% of the time, Pallas kernels for 32%

profile of v3, /device:TPU:0, one launch (start us, length us, event | category | flops | bytes accessed | tf_op | source)
XLA Modules:
  0.0 129.3 jit_solution(11144057713920186857)
XLA Ops:
  1.3 1.0 fusion.1.refs_4_.refs_7_
  2.4 1.3 %collective-permute-start.1 = (bf16[1552,128]{1,0:T(8,128)(2,1)S(1)}, bf16[1552,128]{1,0:T(8,128)(2,1)S(1)}, u32[]{:S(2)}, u32[]{:S(2)}) collective-permute-start(bf16[1552,128]{1,0:T(8,128)(2,1)S(1)} %fusion.1.refs_4_.refs_7_), channel_id=1, source_target_pairs={{0,8},{8,16},{16,24},{24,32},{32,40},{40,48},{48,56},{56,64},{64,7... | collective-permute-start | bytes 1191944 | tf_op jit(solution)/shard_map/ppermute | solution.py:19
  3.7 4.2 %collective-permute-start = (bf16[1552,128]{1,0:T(8,128)(2,1)S(1)}, bf16[1552,128]{1,0:T(8,128)(2,1)S(1)}, u32[]{:S(2)}, u32[]{:S(2)}) collective-permute-start(bf16[1552,128]{1,0:T(8,128)(2,1)S(1)} %fusion.1.refs_4_.refs_7_), channel_id=1, source_target_pairs={{0,16},{8,24},{16,32},{24,40},{32,48},{40,56},{48,64},{56,72},{64,... | collective-permute-start | bytes 1191944 | tf_op jit(solution)/shard_map/ppermute | solution.py:19
  7.9 1.6 %collective-permute-start.5 = (bf16[768,512]{1,0:T(8,128)(2,1)}, bf16[768,512]{1,0:T(8,128)(2,1)S(1)}, u32[]{:S(2)}, u32[]{:S(2)}) collective-permute-start(bf16[768,512]{1,0:T(8,128)(2,1)} %refs_3_.1), channel_id=1, source_target_pairs={{0,1},{1,2},{2,3},{3,0},{4,5},{5,6},{6,7},{7,4},{8,9},{9,10},{10,1... | collective-permute-start | bytes 2359304 | tf_op jit(solution)/shard_map/ppermute | solution.py:24
  9.5 1.7 %collective-permute-start.6 = (bf16[768,512]{1,0:T(8,128)(2,1)}, bf16[768,512]{1,0:T(8,128)(2,1)S(1)}, u32[]{:S(2)}, u32[]{:S(2)}) collective-permute-start(bf16[768,512]{1,0:T(8,128)(2,1)} %refs_3_.1), channel_id=1, source_target_pairs={{0,3},{1,0},{2,1},{3,2},{4,7},{5,4},{6,5},{7,6},{8,11},{9,8},{10,9... | collective-permute-start | bytes 2359304 | tf_op jit(solution)/shard_map/ppermute | solution.py:24
  11.2 1.8 %collective-permute-start.3 = (bf16[768,512]{1,0:T(8,128)(2,1)}, bf16[768,512]{1,0:T(8,128)(2,1)}, u32[]{:S(2)}, u32[]{:S(2)}) collective-permute-start(bf16[768,512]{1,0:T(8,128)(2,1)} %refs_3_.1), channel_id=1, source_target_pairs={{0,2},{1,3},{2,0},{3,1},{4,6},{5,7},{6,4},{7,5},{8,10},{9,11},{10,... | collective-permute-start | bytes 2359304 | tf_op jit(solution)/shard_map/ppermute | solution.py:24
  13.0 4.5 %collective-permute-done.refs_2_.refs_5_ = bf16[1552,128]{1,0:T(8,128)(2,1)S(1)} collective-permute-done((bf16[1552,128]{1,0:T(8,128)(2,1)S(1)}, bf16[1552,128]{1,0:T(8,128)(2,1)S(1)}, u32[]{:S(2)}, u32[]{:S(2)}) %collective-permute-start) | collective-permute-done | bytes 397344 | tf_op jit(solution)/shard_map/ppermute | solution.py:19
  17.5 2.9 %collective-permute-start.2 = (bf16[768,512]{1,0:T(8,128)(2,1)}, bf16[768,512]{1,0:T(8,128)(2,1)S(1)}, u32[]{:S(2)}, u32[]{:S(2)}) collective-permute-start(bf16[768,512]{1,0:T(8,128)(2,1)} %refs_3_.1), channel_id=1, source_target_pairs={{0,4},{1,5},{2,6},{3,7},{4,0},{5,1},{6,2},{7,3},{8,12},{9,13},{10,... | collective-permute-start | bytes 2359304 | tf_op jit(solution)/shard_map/ppermute | solution.py:28
  21.1 1.5 %convert_reduce_fusion = s32[768]{0:T(1024)S(1)} fusion(s32[2304]{0:T(1024)S(1)} %pad_add_fusion, s32[768]{0:T(1024)} %param.11), kind=kLoop, calls=%fused_computation | loop fusion | flops 5307648 | bytes 15360 | tf_op jit(solution)/shard_map/reduce_sum | solution.py:310
  22.8 1.1 copy-done
  24.0 13.3 %forward.1 = (bf16[4,768,1792]{2,1,0:T(8,128)(2,1)}, bf16[768,512]{1,0:T(8,128)(2,1)}, bf16[512,768]{1,0:T(8,128)(2,1)}, f32[768,512]{1,0:T(8,128)}) custom-call(s32[768,1]{1,0:T(8,128)S(1)} %reshape_maximum_fusion.refs_0_, bf16[768,512]{1,0:T(8,128)(2,1)S(1)} %copy-done, bf16[1552,128]{1,0:T(8,128)(2,1)S(1)} %collective-permute-done.refs_2_.refs_5_, ...), custom_call_target="tpu_custom_call" | custom-call | flops 2818572288 | bytes 14680064 | tf_op jit(solution)/shard_map/forward/pallas_call | solution.py:318
  37.2 1.6 %collective-permute-done.2.refs_6_ = bf16[768,512]{1,0:T(8,128)(2,1)S(1)} collective-permute-done((bf16[768,512]{1,0:T(8,128)(2,1)}, bf16[768,512]{1,0:T(8,128)(2,1)S(1)}, u32[]{:S(2)}, u32[]{:S(2)}) %collective-permute-start.2) | collective-permute-done | bytes 786464 | tf_op jit(solution)/shard_map/ppermute | solution.py:28
  38.8 1.5 %collective-permute-start.8 = (bf16[768,512]{1,0:T(8,128)(2,1)S(1)}, bf16[768,512]{1,0:T(8,128)(2,1)}, u32[]{:S(2)}, u32[]{:S(2)}) collective-permute-start(bf16[768,512]{1,0:T(8,128)(2,1)S(1)} %collective-permute-done.2.refs_6_), channel_id=1, source_target_pairs={{0,1},{1,2},{2,3},{3,0},{4,5},{5,6},{6,7},{7,4},{8,9},{9,10},{10,1... | collective-permute-start | bytes 2359304 | tf_op jit(solution)/shard_map/ppermute | solution.py:24
  40.3 1.7 %collective-permute-start.9 = (bf16[768,512]{1,0:T(8,128)(2,1)S(1)}, bf16[768,512]{1,0:T(8,128)(2,1)}, u32[]{:S(2)}, u32[]{:S(2)}) collective-permute-start(bf16[768,512]{1,0:T(8,128)(2,1)S(1)} %collective-permute-done.2.refs_6_), channel_id=1, source_target_pairs={{0,3},{1,0},{2,1},{3,2},{4,7},{5,4},{6,5},{7,6},{8,11},{9,8},{10,9... | collective-permute-start | bytes 2359304 | tf_op jit(solution)/shard_map/ppermute | solution.py:24
  42.2 0.9 copy-done.3
  43.9 7.1 %project.3 = (f32[768,512]{1,0:T(8,128)S(1)}, bf16[4,512,256]{2,1,0:T(8,128)(2,1)S(1)}, bf16[4,512,256]{2,1,0:T(8,128)(2,1)}) custom-call(s32[5]{0:T(128)S(1)} %stack.56.refs_0_, bf16[512,4096]{1,0:T(8,128)(2,1)} %refs_1_.7, bf16[512,768]{1,0:T(8,128)(2,1)} %get-tuple-element.32.refs_2_, bf16[768,512]{1,0:T(8,128)(2,1)} %refs_3_.1, ...), custom_call_target="tpu_custom_call" | custom-call | flops 3221225472 | bytes 1048576 | tf_op jit(solution)/shard_map/project/pallas_call | solution.py:274
  51.1 3.2 %collective-permute-start.7 = (bf16[4,512,256]{2,1,0:T(8,128)(2,1)}, bf16[4,512,256]{2,1,0:T(8,128)(2,1)}, u32[]{:S(2)}, u32[]{:S(2)}) collective-permute-start(bf16[4,512,256]{2,1,0:T(8,128)(2,1)} %get-tuple-element.35), channel_id=1, source_target_pairs={{0,8},{8,0},{16,24},{24,16},{32,40},{40,32},{48,56},{56,48},{64,72... | collective-permute-start | bytes 3145736 | tf_op jit(solution)/shard_map/ppermute | solution.py:32
  54.3 2.8 %collective-permute-start.4 = (bf16[768,512]{1,0:T(8,128)(2,1)}, bf16[768,512]{1,0:T(8,128)(2,1)}, u32[]{:S(2)}, u32[]{:S(2)}) collective-permute-start(bf16[768,512]{1,0:T(8,128)(2,1)} %collective-permute-done.3.refs_3_), channel_id=1, source_target_pairs={{0,4},{1,5},{2,6},{3,7},{4,0},{5,1},{6,2},{7,3},{8,12},{9,13},{10,... | collective-permute-start | bytes 2359304 | tf_op jit(solution)/shard_map/ppermute | solution.py:28
  57.1 7.5 %collective-permute-done.8.refs_4_ = bf16[768,512]{1,0:T(8,128)(2,1)} collective-permute-done((bf16[768,512]{1,0:T(8,128)(2,1)S(1)}, bf16[768,512]{1,0:T(8,128)(2,1)}, u32[]{:S(2)}, u32[]{:S(2)}) %collective-permute-start.8) | collective-permute-done | bytes 786464 | tf_op jit(solution)/shard_map/ppermute | solution.py:24
  64.6 5.2 %project.4 = (f32[768,512]{1,0:T(8,128)S(1)}, bf16[3,512,256]{2,1,0:T(8,128)(2,1)S(1)}, bf16[3,512,256]{2,1,0:T(8,128)(2,1)S(1)}) custom-call(s32[4]{0:T(128)S(1)} %pad_add_fusion.1.refs_0_, bf16[512,4096]{1,0:T(8,128)(2,1)} %refs_1_.7, bf16[512,768]{1,0:T(8,128)(2,1)} %get-tuple-element.32.refs_2_, bf16[768,512]{1,0:T(8,128)(2,1)} %collective-permute-done.3.refs_3_, ...), custom_call_target="tpu_custom_call" | custom-call | flops 2415919104 | bytes 1048576 | tf_op jit(solution)/shard_map/project/pallas_call | solution.py:274
  69.8 0.9 copy-done.2
  70.9 4.9 %collective-permute-done.4.refs_3_ = bf16[768,512]{1,0:T(8,128)(2,1)} collective-permute-done((bf16[768,512]{1,0:T(8,128)(2,1)}, bf16[768,512]{1,0:T(8,128)(2,1)}, u32[]{:S(2)}, u32[]{:S(2)}) %collective-permute-start.4) | collective-permute-done | bytes 786464 | tf_op jit(solution)/shard_map/ppermute | solution.py:28
  75.8 5.2 %project.5 = (bf16[768,512]{1,0:T(8,128)(2,1)S(1)}, bf16[1,512,256]{2,1,0:T(8,128)(2,1)S(1)}, bf16[1,512,256]{2,1,0:T(8,128)(2,1)S(1)}, bf16[8,512,256]{2,1,0:T(8,128)(2,1)}) custom-call(s32[9]{0:T(128)S(1)} %stack.55.refs_0_, bf16[512,4096]{1,0:T(8,128)(2,1)} %refs_1_.7, bf16[512,768]{1,0:T(8,128)(2,1)} %get-tuple-element.32.refs_2_, ...), custom_call_target="tpu_custom_call" | custom-call | flops 1048576 | bytes 1048576 | tf_op jit(solution)/shard_map/project/pallas_call | solution.py:274
  81.1 1.5 %collective-permute-done.11.come_ref = bf16[1,512,256]{2,1,0:T(8,128)(2,1)S(1)} collective-permute-done((bf16[1,512,256]{2,1,0:T(8,128)(2,1)S(1)}, bf16[1,512,256]{2,1,0:T(8,128)(2,1)S(1)}, u32[]{:S(2)}, u32[]{:S(2)}) %collective-permute-start.11) | collective-permute-done | bytes 262176 | tf_op jit(solution)/shard_map/ppermute | solution.py:32
  83.4 6.2 %all-to-all-start = ((bf16[8,512,256]{2,1,0:T(8,128)(2,1)}), bf16[8,512,256]{2,1,0:T(8,128)(2,1)}, u32[]{:S(2)}, u32[]{:S(2)}) async-start(bf16[8,512,256]{2,1,0:T(8,128)(2,1)} %place.1), calls=%async_computation | async-start | bytes 4194304 | tf_op jit(solution)/shard_map/all_to_all | solution.py:378
  89.7 9.2 %backward_past.1 = (f32[768,512]{1,0:T(8,128)S(1)}, bf16[1536,128]{1,0:T(8,128)(2,1)S(1)}, bf16[1536,128]{1,0:T(8,128)(2,1)S(1)}) custom-call(bf16[768,512]{1,0:T(8,128)(2,1)} %refs_0_.3, bf16[768,512]{1,0:T(8,128)(2,1)S(1)} %get-tuple-element.44.refs_1_, bf16[768,512]{1,0:T(8,128)(2,1)} %get-tuple-element.45.refs_2_, f32[768,512]{1,0:T(8,128)} %get-tuple-element.46.refs_3_, ...), custom_call_target="tpu_custom_call" | custom-call | flops 1048576 | bytes 1048576 | tf_op jit(solution)/shard_map/backward_past/pallas_call | solution.py:383
  98.9 1.3 collective-permute-start.12
  100.2 1.5 %collective-permute-start.13 = (bf16[1536,128]{1,0:T(8,128)(2,1)S(1)}, bf16[1536,128]{1,0:T(8,128)(2,1)S(1)}, u32[]{:S(2)}, u32[]{:S(2)}) collective-permute-start(bf16[1536,128]{1,0:T(8,128)(2,1)S(1)} %get-tuple-element.54), channel_id=1, source_target_pairs={{16,0},{24,8},{32,16},{40,24},{48,32},{56,40},{64,48},{72,56},{80,... | collective-permute-start | bytes 1179656 | tf_op jit(solution)/shard_map/ppermute | solution.py:19
  101.7 7.1 %backward_own.1 = (bf16[768,512]{1,0:T(8,128)(2,1)}, f32[1536,128]{1,0:T(8,128)S(1)}) custom-call(bf16[768,512]{1,0:T(8,128)(2,1)} %refs_0_.3, bf16[768,512]{1,0:T(8,128)(2,1)S(1)} %get-tuple-element.44.refs_1_, bf16[768,512]{1,0:T(8,128)(2,1)} %get-tuple-element.45.refs_2_, f32[768,512]{1,0:T(8,128)} %get-tuple-element.46.refs_3_, ...), custom_call_target="tpu_custom_call" | custom-call | flops 1048576 | bytes 1048576 | tf_op jit(solution)/shard_map/backward_own/pallas_call | solution.py:396
  108.8 9.4 %all-to-all-done = bf16[8,512,256]{2,1,0:T(8,128)(2,1)} async-done(((bf16[8,512,256]{2,1,0:T(8,128)(2,1)}), bf16[8,512,256]{2,1,0:T(8,128)(2,1)}, u32[]{:S(2)}, u32[]{:S(2)}) %all-to-all-start) | async-done | bytes 2097184 | tf_op jit(solution)/shard_map/all_to_all | solution.py:378
  118.2 2.6 %reduce_sum.25 = bf16[512,256]{1,0:T(8,128)(2,1)} reduce(bf16[8,512,256]{2,1,0:T(8,128)(2,1)} %all-to-all-done, bf16[]{:T(256)} %constant.75.clone.1), dimensions={0}, to_apply=%region_1.2 | reduce | flops 917504 | bytes 2359298 | tf_op jit(solution)/shard_map/reduce_sum | solution.py:379
  120.8 7.5 %collective-permute-done.13 = bf16[1536,128]{1,0:T(8,128)(2,1)S(1)} collective-permute-done((bf16[1536,128]{1,0:T(8,128)(2,1)S(1)}, bf16[1536,128]{1,0:T(8,128)(2,1)S(1)}, u32[]{:S(2)}, u32[]{:S(2)}) %collective-permute-start.13) | collective-permute-done | bytes 393248 | tf_op jit(solution)/shard_map/ppermute | solution.py:19
  (30 shorter events, 4.6 us)
Async XLA Ops:
  2.4 10.6 %collective-permute-start.1 = (bf16[1552,128]{1,0:T(8,128)(2,1)S(1)}, bf16[1552,128]{1,0:T(8,128)(2,1)S(1)}, u32[]{:S(2)}, u32[]{:S(2)}) collective-permute-start(bf16[1552,128]{1,0:T(8,128)(2,1)S(1)} %fusion.1.refs_4_.refs_7_), channel_id=1, source_target_pairs={{0,8},{8,16},{16,24},{24,32},{32,40},{40,48},{48,56},{56,64},{64,7... | collective-permute-start | bytes 1191944 | tf_op jit(solution)/shard_map/ppermute | solution.py:19
  3.7 13.8 %collective-permute-start = (bf16[1552,128]{1,0:T(8,128)(2,1)S(1)}, bf16[1552,128]{1,0:T(8,128)(2,1)S(1)}, u32[]{:S(2)}, u32[]{:S(2)}) collective-permute-start(bf16[1552,128]{1,0:T(8,128)(2,1)S(1)} %fusion.1.refs_4_.refs_7_), channel_id=1, source_target_pairs={{0,16},{8,24},{16,32},{24,40},{32,48},{40,56},{48,64},{56,72},{64,... | collective-permute-start | bytes 1191944 | tf_op jit(solution)/shard_map/ppermute | solution.py:19
  7.9 34.3 %collective-permute-start.5 = (bf16[768,512]{1,0:T(8,128)(2,1)}, bf16[768,512]{1,0:T(8,128)(2,1)S(1)}, u32[]{:S(2)}, u32[]{:S(2)}) collective-permute-start(bf16[768,512]{1,0:T(8,128)(2,1)} %refs_3_.1), channel_id=1, source_target_pairs={{0,1},{1,2},{2,3},{3,0},{4,5},{5,6},{6,7},{7,4},{8,9},{9,10},{10,1... | collective-permute-start | bytes 2359304 | tf_op jit(solution)/shard_map/ppermute | solution.py:24
  9.5 32.7 %collective-permute-start.6 = (bf16[768,512]{1,0:T(8,128)(2,1)}, bf16[768,512]{1,0:T(8,128)(2,1)S(1)}, u32[]{:S(2)}, u32[]{:S(2)}) collective-permute-start(bf16[768,512]{1,0:T(8,128)(2,1)} %refs_3_.1), channel_id=1, source_target_pairs={{0,3},{1,0},{2,1},{3,2},{4,7},{5,4},{6,5},{7,6},{8,11},{9,8},{10,9... | collective-permute-start | bytes 2359304 | tf_op jit(solution)/shard_map/ppermute | solution.py:24
  11.2 43.1 %collective-permute-start.3 = (bf16[768,512]{1,0:T(8,128)(2,1)}, bf16[768,512]{1,0:T(8,128)(2,1)}, u32[]{:S(2)}, u32[]{:S(2)}) collective-permute-start(bf16[768,512]{1,0:T(8,128)(2,1)} %refs_3_.1), channel_id=1, source_target_pairs={{0,2},{1,3},{2,0},{3,1},{4,6},{5,7},{6,4},{7,5},{8,10},{9,11},{10,... | collective-permute-start | bytes 2359304 | tf_op jit(solution)/shard_map/ppermute | solution.py:24
  17.5 21.3 %collective-permute-start.2 = (bf16[768,512]{1,0:T(8,128)(2,1)}, bf16[768,512]{1,0:T(8,128)(2,1)S(1)}, u32[]{:S(2)}, u32[]{:S(2)}) collective-permute-start(bf16[768,512]{1,0:T(8,128)(2,1)} %refs_3_.1), channel_id=1, source_target_pairs={{0,4},{1,5},{2,6},{3,7},{4,0},{5,1},{6,2},{7,3},{8,12},{9,13},{10,... | collective-permute-start | bytes 2359304 | tf_op jit(solution)/shard_map/ppermute | solution.py:28
  22.8 1.1 copy-start
  38.8 3.3 %copy-start.5 = (bf16[768,512]{1,0:T(8,128)(2,1)}, bf16[768,512]{1,0:T(8,128)(2,1)S(1)}, u32[]{:S(2)}) copy-start(bf16[768,512]{1,0:T(8,128)(2,1)S(1)} %collective-permute-done.2.refs_6_) | copy-start | bytes 2359300
  38.8 25.8 %collective-permute-start.8 = (bf16[768,512]{1,0:T(8,128)(2,1)S(1)}, bf16[768,512]{1,0:T(8,128)(2,1)}, u32[]{:S(2)}, u32[]{:S(2)}) collective-permute-start(bf16[768,512]{1,0:T(8,128)(2,1)S(1)} %collective-permute-done.2.refs_6_), channel_id=1, source_target_pairs={{0,1},{1,2},{2,3},{3,0},{4,5},{5,6},{6,7},{7,4},{8,9},{9,10},{10,1... | collective-permute-start | bytes 2359304 | tf_op jit(solution)/shard_map/ppermute | solution.py:24
  40.3 24.3 %collective-permute-start.9 = (bf16[768,512]{1,0:T(8,128)(2,1)S(1)}, bf16[768,512]{1,0:T(8,128)(2,1)}, u32[]{:S(2)}, u32[]{:S(2)}) collective-permute-start(bf16[768,512]{1,0:T(8,128)(2,1)S(1)} %collective-permute-done.2.refs_6_), channel_id=1, source_target_pairs={{0,3},{1,0},{2,1},{3,2},{4,7},{5,4},{6,5},{7,6},{8,11},{9,8},{10,9... | collective-permute-start | bytes 2359304 | tf_op jit(solution)/shard_map/ppermute | solution.py:24
  42.2 0.9 copy-start.3
  43.1 0.9 copy-start.4
  51.1 18.8 %copy-start.1 = (bf16[4,512,256]{2,1,0:T(8,128)(2,1)}, bf16[4,512,256]{2,1,0:T(8,128)(2,1)S(1)}, u32[]{:S(2)}) copy-start(bf16[4,512,256]{2,1,0:T(8,128)(2,1)S(1)} %get-tuple-element.34.refs_4_) | copy-start | bytes 3145732
  51.1 24.8 %collective-permute-start.7 = (bf16[4,512,256]{2,1,0:T(8,128)(2,1)}, bf16[4,512,256]{2,1,0:T(8,128)(2,1)}, u32[]{:S(2)}, u32[]{:S(2)}) collective-permute-start(bf16[4,512,256]{2,1,0:T(8,128)(2,1)} %get-tuple-element.35), channel_id=1, source_target_pairs={{0,8},{8,0},{16,24},{24,16},{32,40},{40,32},{48,56},{56,48},{64,72... | collective-permute-start | bytes 3145736 | tf_op jit(solution)/shard_map/ppermute | solution.py:32
  54.3 21.5 %collective-permute-start.4 = (bf16[768,512]{1,0:T(8,128)(2,1)}, bf16[768,512]{1,0:T(8,128)(2,1)}, u32[]{:S(2)}, u32[]{:S(2)}) collective-permute-start(bf16[768,512]{1,0:T(8,128)(2,1)} %collective-permute-done.3.refs_3_), channel_id=1, source_target_pairs={{0,4},{1,5},{2,6},{3,7},{4,0},{5,1},{6,2},{7,3},{8,12},{9,13},{10,... | collective-permute-start | bytes 2359304 | tf_op jit(solution)/shard_map/ppermute | solution.py:28
  69.8 0.9 copy-start.2
  70.7 5.1 %collective-permute-start.10 = (bf16[3,512,256]{2,1,0:T(8,128)(2,1)S(1)}, bf16[3,512,256]{2,1,0:T(8,128)(2,1)}, u32[]{:S(2)}, u32[]{:S(2)}) collective-permute-start(bf16[3,512,256]{2,1,0:T(8,128)(2,1)S(1)} %get-tuple-element.38), channel_id=1, source_target_pairs={{0,8},{8,0},{16,24},{24,16},{32,40},{40,32},{48,56},{56,48},{64,72... | collective-permute-start | bytes 2359304 | tf_op jit(solution)/shard_map/ppermute | solution.py:32
  81.0 1.6 %collective-permute-start.11 = (bf16[1,512,256]{2,1,0:T(8,128)(2,1)S(1)}, bf16[1,512,256]{2,1,0:T(8,128)(2,1)S(1)}, u32[]{:S(2)}, u32[]{:S(2)}) collective-permute-start(bf16[1,512,256]{2,1,0:T(8,128)(2,1)S(1)} %get-tuple-element.41), channel_id=1, source_target_pairs={{0,8},{8,0},{16,24},{24,16},{32,40},{40,32},{48,56},{56,48},{64,72... | collective-permute-start | bytes 786440 | tf_op jit(solution)/shard_map/ppermute | solution.py:32
  83.4 34.7 %all-to-all-start = ((bf16[8,512,256]{2,1,0:T(8,128)(2,1)}), bf16[8,512,256]{2,1,0:T(8,128)(2,1)}, u32[]{:S(2)}, u32[]{:S(2)}) async-start(bf16[8,512,256]{2,1,0:T(8,128)(2,1)} %place.1), calls=%async_computation | async-start | bytes 4194304 | tf_op jit(solution)/shard_map/all_to_all | solution.py:378
  98.9 21.9 %collective-permute-start.12 = (bf16[1536,128]{1,0:T(8,128)(2,1)S(1)}, bf16[1536,128]{1,0:T(8,128)(2,1)S(1)}, u32[]{:S(2)}, u32[]{:S(2)}) collective-permute-start(bf16[1536,128]{1,0:T(8,128)(2,1)S(1)} %get-tuple-element.53), channel_id=1, source_target_pairs={{8,0},{16,8},{24,16},{32,24},{40,32},{48,40},{56,48},{64,56},{72,6... | collective-permute-start | bytes 1179656 | tf_op jit(solution)/shard_map/ppermute | solution.py:19
  100.2 28.2 %collective-permute-start.13 = (bf16[1536,128]{1,0:T(8,128)(2,1)S(1)}, bf16[1536,128]{1,0:T(8,128)(2,1)S(1)}, u32[]{:S(2)}, u32[]{:S(2)}) collective-permute-start(bf16[1536,128]{1,0:T(8,128)(2,1)S(1)} %get-tuple-element.54), channel_id=1, source_target_pairs={{16,0},{24,8},{32,16},{40,24},{48,32},{56,40},{64,48},{72,56},{80,... | collective-permute-start | bytes 1179656 | tf_op jit(solution)/shard_map/ppermute | solution.py:19

commit v4 on v3

--- a/solution.py
+++ b/solution.py
@@ -283,11 +283,14 @@
     )(where, weight, turned, *pieces, *earlier, *before)
 
 
-def place_kernel(where_ref, mine_ref, come_ref, earlier_ref, out_ref, both, sem):
-    both[...] = (mine_ref[...].astype(jnp.float32) + come_ref[...].astype(jnp.float32)).astype(both.dtype)
-    copy = pltpu.make_async_copy(both, out_ref.at[pl.ds(where_ref[0], 1)], sem)
-    copy.start()
-    copy.wait()
+def place_kernel(where_ref, mine_ref, come_ref, earlier_ref, out_ref, both, sems):
+    copies = []
+    for index in range(both.shape[0]):
+        both[index] = (mine_ref[index].astype(jnp.float32) + come_ref[index].astype(jnp.float32)).astype(both.dtype)
+        copies.append(pltpu.make_async_copy(both.at[index], out_ref.at[where_ref[index]], sems.at[index]))
+        copies[-1].start()
+    for copy in copies:
+        copy.wait()
 
 
 def whole():
@@ -338,28 +341,29 @@
     row, column = tensor // 4, tensor % 4
     at = lambda flip, step: (row ^ flip) * 4 + (column + step) % 4
     core = shard % 2
-    places = [at(0, 0), at(0, 3), at(0, 1), at(1, 0), at(0, 2), at(1, 3), at(1, 1), at(1, 2)]
+    places = [at(0, 0), at(0, 2), at(1, 0), at(0, 3), at(0, 1), at(1, 2), at(1, 3), at(1, 1)]
     where = lambda some: jnp.stack([core, *some]).astype(jnp.int32)
-    near_up, near_down, opposite = step_x(out_grad, 1), step_x(out_grad, -1), step_x(out_grad, 2)
-    across = step_y(lax.optimization_barrier((out_grad, far, near))[0])
-    across, turned = lax.optimization_barrier((across, turned))
+    opposite = step_x(out_grad, 2)
+    later = lax.optimization_barrier((out_grad, far, near))[0]
+    across, near_up, near_down = step_y(later), step_x(later, 1), step_x(later, -1)
+    across, opposite, turned = lax.optimization_barrier((across, opposite, turned))
     across_up, across_down = step_x(across, 1), step_x(across, -1)
     weight, turned = in_hbm(out_weight), in_hbm(turned)
     real = lambda count: 4 * count * tok * all_heads * all_heads
     last = step_y(opposite)
     total, mine_a, other_a = project(
-        [((p, 0, 0, tok),) for p in range(4)], False, real(4),
-        where(places[:4]), weight, turned, (out_grad, near_up, near_down, across), (),
+        [((p, 0, 0, tok),) for p in range(3)], False, real(3),
+        where(places[:3]), weight, turned, (out_grad, opposite, across), (),
     )
     come_a = step_core(other_a)
     total, mine_b, other_b = project(
         [((p, 0, 0, tok),) for p in range(3)], False, real(3),
-        where(places[4:7]), weight, turned, (opposite, across_up, across_down), (total,),
+        where(places[3:6]), weight, turned, (near_up, near_down, last), (total,),
     )
     come_b = step_core(other_b)
     attention_gradient, mine_c, other_c, placed = project(
-        [((0, 0, 0, tok),)], True, 1 << 20, where(places[7:] + places[:7]), weight, turned, (last,), (total,),
-        (mine_a, come_a, mine_b, come_b),
+        [((p, 0, 0, tok),) for p in range(2)], True, 1 << 20, where(places[6:] + places[:6]), weight, turned,
+        (across_up, across_down), (total,), (mine_a, come_a, mine_b, come_b),
     )
     come_c = step_core(other_c)
     placed = pl.pallas_call(
@@ -368,11 +372,11 @@
         out_specs=hbm(),
         out_shape=pltpu.HBM(placed.shape, placed.dtype),
         input_output_aliases={3: 0},
-        scratch_shapes=[pltpu.VMEM(mine_c.shape, mine_c.dtype), pltpu.SemaphoreType.DMA(())],
+        scratch_shapes=[pltpu.VMEM(mine_c.shape, mine_c.dtype), pltpu.SemaphoreType.DMA((mine_c.shape[0],))],
         compiler_params=pltpu.CompilerParams(vmem_limit_bytes=VMEM_BYTES),
         cost_estimate=pl.CostEstimate(flops=1 << 20, bytes_accessed=1 << 20, transcendentals=0),
         name="place",
-    )(jnp.stack(places[7:]).astype(jnp.int32), mine_c, come_c, placed)
+    )(jnp.stack(places[6:]).astype(jnp.int32), mine_c, come_c, placed)
     placed, attention_gradient = lax.optimization_barrier((placed, attention_gradient))
     groups = [[2 * chip + c for chip in range(8)] for c in range(2)]
     arrived = lax.all_to_all(placed, "seq", 0, 0, axis_index_groups=groups)
@@ -391,7 +395,9 @@
         cost_estimate=pl.CostEstimate(flops=1 << 20, bytes_accessed=1 << 20, transcendentals=0),
         name="backward_past",
     )(queries, attention_gradient, attn, inverse, expo, far, near)
-    far_come, near_come = shifted(far_sum, "seq", -2), shifted(near_sum, "seq", -1)
+    crossed = step_core(near_sum)
+    sent = far_sum.astype(jnp.float32) + jnp.where(core == 1, crossed, 0).astype(jnp.float32)
+    come = shifted(sent.astype(jnp.bfloat16), "seq", -2)
     last_blocks = [pl.BlockSpec((heads, ROWS, ROWS), lambda b, i=i: (0, b, span // ROWS - blocks + i)) for i in range(blocks)]
     grad_queries, own_sum = pl.pallas_call(
         lambda *refs: backward_own_kernel(tok, heads, *refs),
@@ -405,7 +411,7 @@
         name="backward_own",
     )(queries, attention_gradient, attn, inverse, *([expo] * blocks), own, past_queries)
     own_sum, weight_grad = lax.optimization_barrier((own_sum, weight_grad))
-    total = own_sum + near_come.astype(jnp.float32) + far_come.astype(jnp.float32)
+    total = own_sum + jnp.where(core == 0, crossed, 0).astype(jnp.float32) + come.astype(jnp.float32)
     total = total.astype(jnp.bfloat16)
     return (grad_queries, total[:tok], total[tok:], weight_grad)
 

time: 131 us -> 126 us (0.962)
  waiting for transfers between devices: 37 us -> 33.3 us
  starting transfers between devices: 32 us -> 28.7 us
  other arithmetic: 7 us -> 10.2 us
    ppermute x5, waiting for transfers between devices: 7.5 us -> 0.01 us  [step_x(): return lax.ppermute(value, 'tensor', pairs)]
    ppermute x2, waiting for transfers between devices: 6.51 us -> 12.1 us  [step_y(): return lax.ppermute(value, 'tensor', [(t, t ^ 4) for t in range(8)])]
    ppermute x3 -> x4, waiting for transfers between devices: 1.53 us -> 6.04 us  [step_core(): return lax.ppermute(value, 'seq', [(s, s ^ 1) for s in range(16)])]
    all_to_all x1, waiting for transfers between devices: 9.37 us -> 5.22 us  [local(): arrived = lax.all_to_all(placed, 'seq', 0, 0, axis_index_groups=groups)]
    ppermute x3 -> x4, starting transfers between devices: 3.4 us -> 0.41 us  [step_core(): return lax.ppermute(value, 'seq', [(s, s ^ 1) for s in range(16)])]
    ppermute x4 -> x3, waiting for transfers between devices: 12 us -> 9.95 us  [shifted(): lax.ppermute(value, axis, [(source, source + steps) for source in range(i...]
    convert_element_type x0 -> x1, other arithmetic: none -> 2.02 us  [local(): come = shifted(sent.astype(jnp.bfloat16), 'seq', -2)]
    ppermute x2, starting transfers between devices: 5.67 us -> 4.28 us  [step_y(): return lax.ppermute(value, 'tensor', [(t, t ^ 4) for t in range(8)])]
  transfers between devices with their start and end apart: 15 -> 15, of which waited for: 7 -> 7; matrix products, arithmetic and copies ran while one was open for 4% -> 6% of each run, Pallas kernels for 32% -> 33%
where the time goes in v4:
time: 126 us; the launch traced here: 125 us
  Pallas kernels  48.4 us (38%)
  waiting for transfers between devices  33.3 us (26%)
  starting transfers between devices  28.7 us (23%)
  other arithmetic  10.2 us (8%)
  local copies, waits for them, and re-layouts  3.66 us (3%)
    pallas_call x3, Pallas kernels, project(): pl.pallas_call(lambda *refs: project_kernel(sources, shapes, groups, *ref...  16.7 us
    pallas_call x1, Pallas kernels, local(): pl.pallas_call(lambda *refs: forward_kernel(tok, span, heads, *refs), gri...  13.3 us
    ppermute x2, waiting for transfers between devices, step_y(): return lax.ppermute(value, 'tensor', [(t, t ^ 4) for t in range(8)])  12.1 us
    pallas_call x1, Pallas kernels, local(): pl.pallas_call(lambda *refs: backward_past_kernel(tok, heads, *refs), gri...  9.97 us
    ppermute x3, waiting for transfers between devices, shifted(): lax.ppermute(value, axis, [(source, source + steps) for source in range(i...  9.95 us
    ppermute x5, starting transfers between devices, step_x(): return lax.ppermute(value, 'tensor', pairs)  9.58 us
    all_to_all x1, starting transfers between devices, local(): arrived = lax.all_to_all(placed, 'seq', 0, 0, axis_index_groups=groups)  7.42 us
    pallas_call x1, Pallas kernels, local(): pl.pallas_call(lambda *refs: backward_own_kernel(tok, heads, *refs), grid...  7.06 us
  transfers between devices with their start and end apart: 15, of which 7 were waited for; matrix products, arithmetic and copies ran while one was open for 6% of the time, Pallas kernels for 33%

profile of v4, /device:TPU:0, one launch (start us, length us, event | category | flops | bytes accessed | tf_op | source)
XLA Modules:
  0.0 125.1 jit_solution(12336921590323524904)
XLA Ops:
  1.3 1.0 fusion.1.refs_4_.refs_7_
  2.4 1.3 %collective-permute-start.1 = (bf16[1552,128]{1,0:T(8,128)(2,1)S(1)}, bf16[1552,128]{1,0:T(8,128)(2,1)S(1)}, u32[]{:S(2)}, u32[]{:S(2)}) collective-permute-start(bf16[1552,128]{1,0:T(8,128)(2,1)S(1)} %fusion.1.refs_4_.refs_7_), channel_id=1, source_target_pairs={{0,8},{8,16},{16,24},{24,32},{32,40},{40,48},{48,56},{56,64},{64,7... | collective-permute-start | bytes 1191944 | tf_op jit(solution)/shard_map/ppermute | solution.py:19
  3.7 4.2 %collective-permute-start = (bf16[1552,128]{1,0:T(8,128)(2,1)S(1)}, bf16[1552,128]{1,0:T(8,128)(2,1)S(1)}, u32[]{:S(2)}, u32[]{:S(2)}) collective-permute-start(bf16[1552,128]{1,0:T(8,128)(2,1)S(1)} %fusion.1.refs_4_.refs_7_), channel_id=1, source_target_pairs={{0,16},{8,24},{16,32},{24,40},{32,48},{40,56},{48,64},{56,72},{64,... | collective-permute-start | bytes 1191944 | tf_op jit(solution)/shard_map/ppermute | solution.py:19
  7.9 3.1 %collective-permute-start.3 = (bf16[768,512]{1,0:T(8,128)(2,1)}, bf16[768,512]{1,0:T(8,128)(2,1)S(1)}, u32[]{:S(2)}, u32[]{:S(2)}) collective-permute-start(bf16[768,512]{1,0:T(8,128)(2,1)} %refs_3_.1), channel_id=1, source_target_pairs={{0,2},{1,3},{2,0},{3,1},{4,6},{5,7},{6,4},{7,5},{8,10},{9,11},{10,... | collective-permute-start | bytes 2359304 | tf_op jit(solution)/shard_map/ppermute | solution.py:24
  11.0 6.5 %collective-permute-done.refs_2_.refs_5_ = bf16[1552,128]{1,0:T(8,128)(2,1)S(1)} collective-permute-done((bf16[1552,128]{1,0:T(8,128)(2,1)S(1)}, bf16[1552,128]{1,0:T(8,128)(2,1)S(1)}, u32[]{:S(2)}, u32[]{:S(2)}) %collective-permute-start) | collective-permute-done | bytes 397344 | tf_op jit(solution)/shard_map/ppermute | solution.py:19
  17.5 2.9 %collective-permute-start.2 = (bf16[768,512]{1,0:T(8,128)(2,1)}, bf16[768,512]{1,0:T(8,128)(2,1)}, u32[]{:S(2)}, u32[]{:S(2)}) collective-permute-start(bf16[768,512]{1,0:T(8,128)(2,1)} %refs_3_.1), channel_id=1, source_target_pairs={{0,4},{1,5},{2,6},{3,7},{4,0},{5,1},{6,2},{7,3},{8,12},{9,13},{10,... | collective-permute-start | bytes 2359304 | tf_op jit(solution)/shard_map/ppermute | solution.py:28
  20.4 1.5 %collective-permute-start.7 = (bf16[768,512]{1,0:T(8,128)(2,1)}, bf16[768,512]{1,0:T(8,128)(2,1)S(1)}, u32[]{:S(2)}, u32[]{:S(2)}) collective-permute-start(bf16[768,512]{1,0:T(8,128)(2,1)} %refs_3_.1), channel_id=1, source_target_pairs={{0,1},{1,2},{2,3},{3,0},{4,5},{5,6},{6,7},{7,4},{8,9},{9,10},{10,1... | collective-permute-start | bytes 2359304 | tf_op jit(solution)/shard_map/ppermute | solution.py:24
  21.9 1.7 %collective-permute-start.8 = (bf16[768,512]{1,0:T(8,128)(2,1)}, bf16[768,512]{1,0:T(8,128)(2,1)}, u32[]{:S(2)}, u32[]{:S(2)}) collective-permute-start(bf16[768,512]{1,0:T(8,128)(2,1)} %refs_3_.1), channel_id=1, source_target_pairs={{0,3},{1,0},{2,1},{3,2},{4,7},{5,4},{6,5},{7,6},{8,11},{9,8},{10,9... | collective-permute-start | bytes 2359304 | tf_op jit(solution)/shard_map/ppermute | solution.py:24
  24.4 1.5 %convert_reduce_fusion = s32[768]{0:T(1024)S(1)} fusion(s32[2304]{0:T(1024)S(1)} %pad_add_fusion, s32[768]{0:T(1024)} %param.11), kind=kLoop, calls=%fused_computation | loop fusion | flops 5307648 | bytes 15360 | tf_op jit(solution)/shard_map/reduce_sum | solution.py:313
  26.1 1.1 copy-done
  27.2 13.3 %forward.1 = (bf16[4,768,1792]{2,1,0:T(8,128)(2,1)}, bf16[768,512]{1,0:T(8,128)(2,1)}, bf16[512,768]{1,0:T(8,128)(2,1)}, f32[768,512]{1,0:T(8,128)}) custom-call(s32[768,1]{1,0:T(8,128)S(1)} %reshape_maximum_fusion.refs_0_, bf16[768,512]{1,0:T(8,128)(2,1)S(1)} %copy-done, bf16[1552,128]{1,0:T(8,128)(2,1)S(1)} %collective-permute-done.refs_2_.refs_5_, ...), custom_call_target="tpu_custom_call" | custom-call | flops 2818572288 | bytes 14680064 | tf_op jit(solution)/shard_map/forward/pallas_call | solution.py:321
  40.5 1.4 %collective-permute-start.9 = (bf16[768,512]{1,0:T(8,128)(2,1)S(1)}, bf16[768,512]{1,0:T(8,128)(2,1)}, u32[]{:S(2)}, u32[]{:S(2)}) collective-permute-start(bf16[768,512]{1,0:T(8,128)(2,1)S(1)} %collective-permute-done.3.refs_4_), channel_id=1, source_target_pairs={{0,4},{1,5},{2,6},{3,7},{4,0},{5,1},{6,2},{7,3},{8,12},{9,13},{10,... | collective-permute-start | bytes 2359304 | tf_op jit(solution)/shard_map/ppermute | solution.py:28
  42.0 1.5 %collective-permute-start.4 = (bf16[768,512]{1,0:T(8,128)(2,1)}, bf16[768,512]{1,0:T(8,128)(2,1)}, u32[]{:S(2)}, u32[]{:S(2)}) collective-permute-start(bf16[768,512]{1,0:T(8,128)(2,1)} %collective-permute-done.2.refs_5_), channel_id=1, source_target_pairs={{0,1},{1,2},{2,3},{3,0},{4,5},{5,6},{6,7},{7,4},{8,9},{9,10},{10,1... | collective-permute-start | bytes 2359304 | tf_op jit(solution)/shard_map/ppermute | solution.py:24
  43.5 1.7 %collective-permute-start.5 = (bf16[768,512]{1,0:T(8,128)(2,1)}, bf16[768,512]{1,0:T(8,128)(2,1)}, u32[]{:S(2)}, u32[]{:S(2)}) collective-permute-start(bf16[768,512]{1,0:T(8,128)(2,1)} %collective-permute-done.2.refs_5_), channel_id=1, source_target_pairs={{0,3},{1,0},{2,1},{3,2},{4,7},{5,4},{6,5},{7,6},{8,11},{9,8},{10,9... | collective-permute-start | bytes 2359304 | tf_op jit(solution)/shard_map/ppermute | solution.py:24
  45.2 5.1 %project.3 = (f32[768,512]{1,0:T(8,128)S(1)}, bf16[3,512,256]{2,1,0:T(8,128)(2,1)S(1)}, bf16[3,512,256]{2,1,0:T(8,128)(2,1)S(1)}) custom-call(s32[4]{0:T(128)S(1)} %pad_add_fusion.2.refs_0_, bf16[512,4096]{1,0:T(8,128)(2,1)} %refs_1_.7, bf16[512,768]{1,0:T(8,128)(2,1)} %get-tuple-element.33.refs_2_, bf16[768,512]{1,0:T(8,128)(2,1)} %refs_3_.1, ...), custom_call_target="tpu_custom_call" | custom-call | flops 2415919104 | bytes 1048576 | tf_op jit(solution)/shard_map/project/pallas_call | solution.py:274
  50.5 12.1 %collective-permute-done.9.refs_5_ = bf16[768,512]{1,0:T(8,128)(2,1)} collective-permute-done((bf16[768,512]{1,0:T(8,128)(2,1)S(1)}, bf16[768,512]{1,0:T(8,128)(2,1)}, u32[]{:S(2)}, u32[]{:S(2)}) %collective-permute-start.9) | collective-permute-done | bytes 786464 | tf_op jit(solution)/shard_map/ppermute | solution.py:28
  62.6 6.1 %project.4 = (f32[768,512]{1,0:T(8,128)S(1)}, bf16[3,512,256]{2,1,0:T(8,128)(2,1)S(1)}, bf16[3,512,256]{2,1,0:T(8,128)(2,1)}) custom-call(s32[4]{0:T(128)S(1)} %pad_add_fusion.3.refs_0_, bf16[512,4096]{1,0:T(8,128)(2,1)} %refs_1_.7, bf16[512,768]{1,0:T(8,128)(2,1)} %get-tuple-element.33.refs_2_, bf16[768,512]{1,0:T(8,128)(2,1)} %copy-done.7, ...), custom_call_target="tpu_custom_call" | custom-call | flops 2415919104 | bytes 1048576 | tf_op jit(solution)/shard_map/project/pallas_call | solution.py:274
  68.7 0.9 copy-done.2
  69.8 2.4 %collective-permute-done.10.refs_8_ = bf16[3,512,256]{2,1,0:T(8,128)(2,1)} collective-permute-done((bf16[3,512,256]{2,1,0:T(8,128)(2,1)}, bf16[3,512,256]{2,1,0:T(8,128)(2,1)}, u32[]{:S(2)}, u32[]{:S(2)}) %collective-permute-start.10) | collective-permute-done | bytes 786464 | tf_op jit(solution)/shard_map/ppermute | solution.py:32
  72.2 5.5 %project.5 = (bf16[768,512]{1,0:T(8,128)(2,1)S(1)}, bf16[2,512,256]{2,1,0:T(8,128)(2,1)S(1)}, bf16[2,512,256]{2,1,0:T(8,128)(2,1)S(1)}, bf16[8,512,256]{2,1,0:T(8,128)(2,1)}) custom-call(s32[9]{0:T(128)S(1)} %stack.59.refs_0_, bf16[512,4096]{1,0:T(8,128)(2,1)} %refs_1_.7, bf16[512,768]{1,0:T(8,128)(2,1)} %get-tuple-element.33.refs_2_, ...), custom_call_target="tpu_custom_call" | custom-call | flops 1048576 | bytes 1048576 | tf_op jit(solution)/shard_map/project/pallas_call | solution.py:274
  78.0 1.7 %collective-permute-done.11.come_ref = bf16[2,512,256]{2,1,0:T(8,128)(2,1)S(1)} collective-permute-done((bf16[2,512,256]{2,1,0:T(8,128)(2,1)S(1)}, bf16[2,512,256]{2,1,0:T(8,128)(2,1)S(1)}, u32[]{:S(2)}, u32[]{:S(2)}) %collective-permute-start.11) | collective-permute-done | bytes 524320 | tf_op jit(solution)/shard_map/ppermute | solution.py:32
  79.7 1.4 %place.1 = bf16[8,512,256]{2,1,0:T(8,128)(2,1)} custom-call(s32[2]{0:T(128)S(1)} %pad_add_fusion.1.where_ref, bf16[2,512,256]{2,1,0:T(8,128)(2,1)S(1)} %get-tuple-element.42.mine_ref, bf16[2,512,256]{2,1,0:T(8,128)(2,1)S(1)} %collective-permute-done.11.come_ref, bf16[8,512,256]{2,1,0:T(8,128)(2,1)} %get-tuple-element.44.earlier_ref), custom_call_target="tpu_custom_call", output_to_operand_aliasing={{}: (3, {})} | custom-call | flops 1048576 | bytes 1048576 | tf_op jit(solution)/shard_map/place/pallas_call | solution.py:369
  81.1 7.4 %all-to-all-start = ((bf16[8,512,256]{2,1,0:T(8,128)(2,1)}), bf16[8,512,256]{2,1,0:T(8,128)(2,1)}, u32[]{:S(2)}, u32[]{:S(2)}) async-start(bf16[8,512,256]{2,1,0:T(8,128)(2,1)} %place.1), calls=%async_computation | async-start | bytes 4194304 | tf_op jit(solution)/shard_map/all_to_all | solution.py:382
  88.6 10.0 %backward_past.1 = (f32[768,512]{1,0:T(8,128)S(1)}, bf16[1536,128]{1,0:T(8,128)(2,1)S(1)}, bf16[1536,128]{1,0:T(8,128)(2,1)}) custom-call(bf16[768,512]{1,0:T(8,128)(2,1)} %refs_0_.3, bf16[768,512]{1,0:T(8,128)(2,1)S(1)} %get-tuple-element.46.refs_1_, bf16[768,512]{1,0:T(8,128)(2,1)} %get-tuple-element.47.refs_2_, f32[768,512]{1,0:T(8,128)} %get-tuple-element.48.refs_3_, ...), custom_call_target="tpu_custom_call" | custom-call | flops 1048576 | bytes 1048576 | tf_op jit(solution)/shard_map/backward_past/pallas_call | solution.py:387
  99.3 1.9 %collective-permute-done.12 = bf16[1536,128]{1,0:T(8,128)(2,1)S(1)} collective-permute-done((bf16[1536,128]{1,0:T(8,128)(2,1)}, bf16[1536,128]{1,0:T(8,128)(2,1)S(1)}, u32[]{:S(2)}, u32[]{:S(2)}) %collective-permute-start.12) | collective-permute-done | bytes 393248 | tf_op jit(solution)/shard_map/ppermute | solution.py:32
  101.2 2.0 %add_convert_fusion.1 = bf16[1536,128]{1,0:T(8,128)(2,1)} fusion(bf16[1536,128]{1,0:T(8,128)(2,1)} %copy-done.3, bf16[1536,128]{1,0:T(8,128)(2,1)S(1)} %collective-permute-done.12, pred[]{:T(512)S(6)} %eq.18), kind=kLoop, calls=%fused_computation.4 | loop fusion | flops 983040 | bytes 1179649 | tf_op jit(solution)/shard_map/convert_element_type | solution.py:400
  103.3 1.5 %collective-permute-start.13 = (bf16[1536,128]{1,0:T(8,128)(2,1)}, bf16[1536,128]{1,0:T(8,128)(2,1)}, u32[]{:S(2)}, u32[]{:S(2)}) collective-permute-start(bf16[1536,128]{1,0:T(8,128)(2,1)} %add_convert_fusion.1), channel_id=1, source_target_pairs={{16,0},{24,8},{32,16},{40,24},{48,32},{56,40},{64,48},{72,56},{80,... | collective-permute-start | bytes 1179656 | tf_op jit(solution)/shard_map/ppermute | solution.py:19
  104.8 7.1 %backward_own.1 = (bf16[768,512]{1,0:T(8,128)(2,1)}, f32[1536,128]{1,0:T(8,128)S(1)}) custom-call(bf16[768,512]{1,0:T(8,128)(2,1)} %refs_0_.3, bf16[768,512]{1,0:T(8,128)(2,1)S(1)} %get-tuple-element.46.refs_1_, bf16[768,512]{1,0:T(8,128)(2,1)} %get-tuple-element.47.refs_2_, f32[768,512]{1,0:T(8,128)} %get-tuple-element.48.refs_3_, ...), custom_call_target="tpu_custom_call" | custom-call | flops 1048576 | bytes 1048576 | tf_op jit(solution)/shard_map/backward_own/pallas_call | solution.py:402
  111.9 5.2 %all-to-all-done = bf16[8,512,256]{2,1,0:T(8,128)(2,1)} async-done(((bf16[8,512,256]{2,1,0:T(8,128)(2,1)}), bf16[8,512,256]{2,1,0:T(8,128)(2,1)}, u32[]{:S(2)}, u32[]{:S(2)}) %all-to-all-start) | async-done | bytes 2097184 | tf_op jit(solution)/shard_map/all_to_all | solution.py:382
  117.1 2.6 %reduce_sum.25 = bf16[512,256]{1,0:T(8,128)(2,1)} reduce(bf16[8,512,256]{2,1,0:T(8,128)(2,1)} %all-to-all-done, bf16[]{:T(256)} %constant.75.clone.1), dimensions={0}, to_apply=%region_1.2 | reduce | flops 917504 | bytes 2359298 | tf_op jit(solution)/shard_map/reduce_sum | solution.py:383
  119.7 3.4 %collective-permute-done.13 = bf16[1536,128]{1,0:T(8,128)(2,1)} collective-permute-done((bf16[1536,128]{1,0:T(8,128)(2,1)}, bf16[1536,128]{1,0:T(8,128)(2,1)}, u32[]{:S(2)}, u32[]{:S(2)}) %collective-permute-start.13) | collective-permute-done | bytes 393248 | tf_op jit(solution)/shard_map/ppermute | solution.py:19
  123.2 1.2 add_convert_fusion
  (36 shorter events, 3.9 us)
Async XLA Ops:
  2.4 8.6 %collective-permute-start.1 = (bf16[1552,128]{1,0:T(8,128)(2,1)S(1)}, bf16[1552,128]{1,0:T(8,128)(2,1)S(1)}, u32[]{:S(2)}, u32[]{:S(2)}) collective-permute-start(bf16[1552,128]{1,0:T(8,128)(2,1)S(1)} %fusion.1.refs_4_.refs_7_), channel_id=1, source_target_pairs={{0,8},{8,16},{16,24},{24,32},{32,40},{40,48},{48,56},{56,64},{64,7... | collective-permute-start | bytes 1191944 | tf_op jit(solution)/shard_map/ppermute | solution.py:19
  3.7 13.8 %collective-permute-start = (bf16[1552,128]{1,0:T(8,128)(2,1)S(1)}, bf16[1552,128]{1,0:T(8,128)(2,1)S(1)}, u32[]{:S(2)}, u32[]{:S(2)}) collective-permute-start(bf16[1552,128]{1,0:T(8,128)(2,1)S(1)} %fusion.1.refs_4_.refs_7_), channel_id=1, source_target_pairs={{0,16},{8,24},{16,32},{24,40},{32,48},{40,56},{48,64},{56,72},{64,... | collective-permute-start | bytes 1191944 | tf_op jit(solution)/shard_map/ppermute | solution.py:19
  7.9 32.6 %collective-permute-start.3 = (bf16[768,512]{1,0:T(8,128)(2,1)}, bf16[768,512]{1,0:T(8,128)(2,1)S(1)}, u32[]{:S(2)}, u32[]{:S(2)}) collective-permute-start(bf16[768,512]{1,0:T(8,128)(2,1)} %refs_3_.1), channel_id=1, source_target_pairs={{0,2},{1,3},{2,0},{3,1},{4,6},{5,7},{6,4},{7,5},{8,10},{9,11},{10,... | collective-permute-start | bytes 2359304 | tf_op jit(solution)/shard_map/ppermute | solution.py:24
  17.5 22.9 %collective-permute-start.2 = (bf16[768,512]{1,0:T(8,128)(2,1)}, bf16[768,512]{1,0:T(8,128)(2,1)}, u32[]{:S(2)}, u32[]{:S(2)}) collective-permute-start(bf16[768,512]{1,0:T(8,128)(2,1)} %refs_3_.1), channel_id=1, source_target_pairs={{0,4},{1,5},{2,6},{3,7},{4,0},{5,1},{6,2},{7,3},{8,12},{9,13},{10,... | collective-permute-start | bytes 2359304 | tf_op jit(solution)/shard_map/ppermute | solution.py:28
  20.4 29.9 %collective-permute-start.7 = (bf16[768,512]{1,0:T(8,128)(2,1)}, bf16[768,512]{1,0:T(8,128)(2,1)S(1)}, u32[]{:S(2)}, u32[]{:S(2)}) collective-permute-start(bf16[768,512]{1,0:T(8,128)(2,1)} %refs_3_.1), channel_id=1, source_target_pairs={{0,1},{1,2},{2,3},{3,0},{4,5},{5,6},{6,7},{7,4},{8,9},{9,10},{10,1... | collective-permute-start | bytes 2359304 | tf_op jit(solution)/shard_map/ppermute | solution.py:24
  21.9 28.6 %collective-permute-start.8 = (bf16[768,512]{1,0:T(8,128)(2,1)}, bf16[768,512]{1,0:T(8,128)(2,1)}, u32[]{:S(2)}, u32[]{:S(2)}) collective-permute-start(bf16[768,512]{1,0:T(8,128)(2,1)} %refs_3_.1), channel_id=1, source_target_pairs={{0,3},{1,0},{2,1},{3,2},{4,7},{5,4},{6,5},{7,6},{8,11},{9,8},{10,9... | collective-permute-start | bytes 2359304 | tf_op jit(solution)/shard_map/ppermute | solution.py:24
  26.1 1.1 copy-start
  40.5 4.8 %copy-start.6 = (bf16[768,512]{1,0:T(8,128)(2,1)}, bf16[768,512]{1,0:T(8,128)(2,1)S(1)}, u32[]{:S(2)}) copy-start(bf16[768,512]{1,0:T(8,128)(2,1)S(1)} %collective-permute-done.3.refs_4_) | copy-start | bytes 2359300
  40.5 22.1 %collective-permute-start.9 = (bf16[768,512]{1,0:T(8,128)(2,1)S(1)}, bf16[768,512]{1,0:T(8,128)(2,1)}, u32[]{:S(2)}, u32[]{:S(2)}) collective-permute-start(bf16[768,512]{1,0:T(8,128)(2,1)S(1)} %collective-permute-done.3.refs_4_), channel_id=1, source_target_pairs={{0,4},{1,5},{2,6},{3,7},{4,0},{5,1},{6,2},{7,3},{8,12},{9,13},{10,... | collective-permute-start | bytes 2359304 | tf_op jit(solution)/shard_map/ppermute | solution.py:28
  42.0 27.8 %collective-permute-start.4 = (bf16[768,512]{1,0:T(8,128)(2,1)}, bf16[768,512]{1,0:T(8,128)(2,1)}, u32[]{:S(2)}, u32[]{:S(2)}) collective-permute-start(bf16[768,512]{1,0:T(8,128)(2,1)} %collective-permute-done.2.refs_5_), channel_id=1, source_target_pairs={{0,1},{1,2},{2,3},{3,0},{4,5},{5,6},{6,7},{7,4},{8,9},{9,10},{10,1... | collective-permute-start | bytes 2359304 | tf_op jit(solution)/shard_map/ppermute | solution.py:24
  43.5 26.3 %collective-permute-start.5 = (bf16[768,512]{1,0:T(8,128)(2,1)}, bf16[768,512]{1,0:T(8,128)(2,1)}, u32[]{:S(2)}, u32[]{:S(2)}) collective-permute-start(bf16[768,512]{1,0:T(8,128)(2,1)} %collective-permute-done.2.refs_5_), channel_id=1, source_target_pairs={{0,3},{1,0},{2,1},{3,2},{4,7},{5,4},{6,5},{7,6},{8,11},{9,8},{10,9... | collective-permute-start | bytes 2359304 | tf_op jit(solution)/shard_map/ppermute | solution.py:24
  50.4 18.3 %copy-start.1 = (bf16[3,512,256]{2,1,0:T(8,128)(2,1)}, bf16[3,512,256]{2,1,0:T(8,128)(2,1)S(1)}, u32[]{:S(2)}) copy-start(bf16[3,512,256]{2,1,0:T(8,128)(2,1)S(1)} %get-tuple-element.36.refs_5_) | copy-start | bytes 2359300
  50.4 12.2 %copy-start.7 = (bf16[768,512]{1,0:T(8,128)(2,1)}, bf16[768,512]{1,0:T(8,128)(2,1)S(1)}, u32[]{:S(2)}) copy-start(bf16[768,512]{1,0:T(8,128)(2,1)S(1)} %collective-permute-done.7.refs_3_) | copy-start | bytes 2359300
  50.4 19.4 %collective-permute-start.6 = (bf16[3,512,256]{2,1,0:T(8,128)(2,1)S(1)}, bf16[3,512,256]{2,1,0:T(8,128)(2,1)}, u32[]{:S(2)}, u32[]{:S(2)}) collective-permute-start(bf16[3,512,256]{2,1,0:T(8,128)(2,1)S(1)} %get-tuple-element.37), channel_id=1, source_target_pairs={{0,8},{8,0},{16,24},{24,16},{32,40},{40,32},{48,56},{56,48},{64,72... | collective-permute-start | bytes 2359304 | tf_op jit(solution)/shard_map/ppermute | solution.py:32
  68.7 0.9 copy-start.2
  69.6 2.6 %collective-permute-start.10 = (bf16[3,512,256]{2,1,0:T(8,128)(2,1)}, bf16[3,512,256]{2,1,0:T(8,128)(2,1)}, u32[]{:S(2)}, u32[]{:S(2)}) collective-permute-start(bf16[3,512,256]{2,1,0:T(8,128)(2,1)} %get-tuple-element.40), channel_id=1, source_target_pairs={{0,8},{8,0},{16,24},{24,16},{32,40},{40,32},{48,56},{56,48},{64,72... | collective-permute-start | bytes 2359304 | tf_op jit(solution)/shard_map/ppermute | solution.py:32
  77.7 2.0 %collective-permute-start.11 = (bf16[2,512,256]{2,1,0:T(8,128)(2,1)S(1)}, bf16[2,512,256]{2,1,0:T(8,128)(2,1)S(1)}, u32[]{:S(2)}, u32[]{:S(2)}) collective-permute-start(bf16[2,512,256]{2,1,0:T(8,128)(2,1)S(1)} %get-tuple-element.43), channel_id=1, source_target_pairs={{0,8},{8,0},{16,24},{24,16},{32,40},{40,32},{48,56},{56,48},{64,72... | collective-permute-start | bytes 1572872 | tf_op jit(solution)/shard_map/ppermute | solution.py:32
  81.1 35.9 %all-to-all-start = ((bf16[8,512,256]{2,1,0:T(8,128)(2,1)}), bf16[8,512,256]{2,1,0:T(8,128)(2,1)}, u32[]{:S(2)}, u32[]{:S(2)}) async-start(bf16[8,512,256]{2,1,0:T(8,128)(2,1)} %place.1), calls=%async_computation | async-start | bytes 4194304 | tf_op jit(solution)/shard_map/all_to_all | solution.py:382
  98.5 0.8 copy-start.3
  99.3 1.9 %collective-permute-start.12 = (bf16[1536,128]{1,0:T(8,128)(2,1)}, bf16[1536,128]{1,0:T(8,128)(2,1)S(1)}, u32[]{:S(2)}, u32[]{:S(2)}) collective-permute-start(bf16[1536,128]{1,0:T(8,128)(2,1)} %get-tuple-element.55), channel_id=1, source_target_pairs={{0,8},{8,0},{16,24},{24,16},{32,40},{40,32},{48,56},{56,48},{64,72... | collective-permute-start | bytes 1179656 | tf_op jit(solution)/shard_map/ppermute | solution.py:32
  101.2 3.5 %copy-start.4 = (bf16[1536,128]{1,0:T(8,128)(2,1)}, bf16[1536,128]{1,0:T(8,128)(2,1)S(1)}, u32[]{:S(2)}) copy-start(bf16[1536,128]{1,0:T(8,128)(2,1)S(1)} %collective-permute-done.12) | copy-start | bytes 1179652
  103.3 19.9 %collective-permute-start.13 = (bf16[1536,128]{1,0:T(8,128)(2,1)}, bf16[1536,128]{1,0:T(8,128)(2,1)}, u32[]{:S(2)}, u32[]{:S(2)}) collective-permute-start(bf16[1536,128]{1,0:T(8,128)(2,1)} %add_convert_fusion.1), channel_id=1, source_target_pairs={{16,0},{24,8},{32,16},{40,24},{48,32},{56,40},{64,48},{72,56},{80,... | collective-permute-start | bytes 1179656 | tf_op jit(solution)/shard_map/ppermute | solution.py:19
  111.9 11.3 %copy-start.5 = (bf16[1536,128]{1,0:T(8,128)(2,1)S(1)}, bf16[1536,128]{1,0:T(8,128)(2,1)}, u32[]{:S(2)}) copy-start(bf16[1536,128]{1,0:T(8,128)(2,1)} %copy-done.4) | copy-start | bytes 1179652

commit v5 on v4

--- a/solution.py
+++ b/solution.py
@@ -283,14 +283,42 @@
     )(where, weight, turned, *pieces, *earlier, *before)
 
 
-def place_kernel(where_ref, mine_ref, come_ref, earlier_ref, out_ref, both, sems):
-    copies = []
-    for index in range(both.shape[0]):
-        both[index] = (mine_ref[index].astype(jnp.float32) + come_ref[index].astype(jnp.float32)).astype(both.dtype)
-        copies.append(pltpu.make_async_copy(both.at[index], out_ref.at[where_ref[index]], sems.at[index]))
-        copies[-1].start()
+def place_kernel(where_ref, mine_ref, come_ref, last_mine_ref, last_come_ref, earlier_ref, out_ref, both, sems):
+    copies, slot = [], 0
+    for mine, come in ((last_mine_ref, last_come_ref), (mine_ref, come_ref)):
+        for index in range(mine.shape[0]):
+            both[slot] = (mine[index].astype(jnp.float32) + come[index].astype(jnp.float32)).astype(both.dtype)
+            place = where_ref[index if mine is mine_ref else mine_ref.shape[0]]
+            copies.append(pltpu.make_async_copy(both.at[slot], out_ref.at[place], sems.at[slot]))
+            copies[-1].start()
+            slot += 1
     for copy in copies:
         copy.wait()
+
+
+def send_kernel(core_ref, far_ref, crossed_ref, out_ref):
+    crossed = jnp.where(core_ref[0] == 1, crossed_ref[...].astype(jnp.float32), 0.0)
+    out_ref[...] = (far_ref[...].astype(jnp.float32) + crossed).astype(out_ref.dtype)
+
+
+def finish_kernel(core_ref, own_ref, crossed_ref, come_ref, key_ref, value_ref):
+    tok = key_ref.shape[0]
+    for index, out in enumerate((key_ref, value_ref)):
+        rows = pl.ds(index * tok, tok)
+        crossed = jnp.where(core_ref[0] == 0, crossed_ref[rows, :].astype(jnp.float32), 0.0)
+        out[...] = (own_ref[rows, :] + crossed + come_ref[rows, :].astype(jnp.float32)).astype(out.dtype)
+
+
+def on_core(kernel, name, out_shape, core, *operands):
+    return pl.pallas_call(
+        kernel,
+        in_specs=[pl.BlockSpec(memory_space=pltpu.SMEM)] + [whole()] * len(operands),
+        out_specs=[whole()] * len(out_shape),
+        out_shape=out_shape,
+        compiler_params=pltpu.CompilerParams(vmem_limit_bytes=VMEM_BYTES // 2),
+        cost_estimate=pl.CostEstimate(flops=1 << 20, bytes_accessed=1 << 20, transcendentals=0),
+        name=name,
+    )(core[None].astype(jnp.int32), *operands)
 
 
 def whole():
@@ -341,7 +369,7 @@
     row, column = tensor // 4, tensor % 4
     at = lambda flip, step: (row ^ flip) * 4 + (column + step) % 4
     core = shard % 2
-    places = [at(0, 0), at(0, 2), at(1, 0), at(0, 3), at(0, 1), at(1, 2), at(1, 3), at(1, 1)]
+    places = [at(0, 0), at(0, 2), at(1, 0), at(0, 3), at(0, 1), at(1, 3), at(1, 1), at(1, 2)]
     where = lambda some: jnp.stack([core, *some]).astype(jnp.int32)
     opposite = step_x(out_grad, 2)
     later = lax.optimization_barrier((out_grad, far, near))[0]
@@ -357,26 +385,30 @@
     )
     come_a = step_core(other_a)
     total, mine_b, other_b = project(
-        [((p, 0, 0, tok),) for p in range(3)], False, real(3),
-        where(places[3:6]), weight, turned, (near_up, near_down, last), (total,),
+        [((p, 0, 0, tok),) for p in range(2)], False, real(2),
+        where(places[3:5]), weight, turned, (near_up, near_down), (total,),
     )
     come_b = step_core(other_b)
+    total, mine_d, other_d = project(
+        [((0, 0, 0, tok),)], False, real(1), where(places[7:]), weight, turned, (last,), (total,),
+    )
+    come_d = step_core(other_d)
     attention_gradient, mine_c, other_c, placed = project(
-        [((p, 0, 0, tok),) for p in range(2)], True, 1 << 20, where(places[6:] + places[:6]), weight, turned,
+        [((p, 0, 0, tok),) for p in range(2)], True, 1 << 20, where(places[5:7] + places[:5]), weight, turned,
         (across_up, across_down), (total,), (mine_a, come_a, mine_b, come_b),
     )
     come_c = step_core(other_c)
     placed = pl.pallas_call(
         place_kernel,
-        in_specs=[pl.BlockSpec(memory_space=pltpu.SMEM), whole(), whole(), hbm()],
+        in_specs=[pl.BlockSpec(memory_space=pltpu.SMEM)] + [whole()] * 4 + [hbm()],
         out_specs=hbm(),
         out_shape=pltpu.HBM(placed.shape, placed.dtype),
-        input_output_aliases={3: 0},
-        scratch_shapes=[pltpu.VMEM(mine_c.shape, mine_c.dtype), pltpu.SemaphoreType.DMA((mine_c.shape[0],))],
+        input_output_aliases={5: 0},
+        scratch_shapes=[pltpu.VMEM((3,) + mine_c.shape[1:], mine_c.dtype), pltpu.SemaphoreType.DMA((3,))],
         compiler_params=pltpu.CompilerParams(vmem_limit_bytes=VMEM_BYTES),
         cost_estimate=pl.CostEstimate(flops=1 << 20, bytes_accessed=1 << 20, transcendentals=0),
         name="place",
-    )(jnp.stack(places[6:]).astype(jnp.int32), mine_c, come_c, placed)
+    )(jnp.stack(places[5:]).astype(jnp.int32), mine_c, come_c, mine_d, come_d, placed)
     placed, attention_gradient = lax.optimization_barrier((placed, attention_gradient))
     groups = [[2 * chip + c for chip in range(8)] for c in range(2)]
     arrived = lax.all_to_all(placed, "seq", 0, 0, axis_index_groups=groups)
@@ -396,8 +428,8 @@
         name="backward_past",
     )(queries, attention_gradient, attn, inverse, expo, far, near)
     crossed = step_core(near_sum)
-    sent = far_sum.astype(jnp.float32) + jnp.where(core == 1, crossed, 0).astype(jnp.float32)
-    come = shifted(sent.astype(jnp.bfloat16), "seq", -2)
+    (sent,) = on_core(send_kernel, "send", [pair(jnp.bfloat16)], core, far_sum, crossed)
+    come = shifted(sent, "seq", -2)
     last_blocks = [pl.BlockSpec((heads, ROWS, ROWS), lambda b, i=i: (0, b, span // ROWS - blocks + i)) for i in range(blocks)]
     grad_queries, own_sum = pl.pallas_call(
         lambda *refs: backward_own_kernel(tok, heads, *refs),
@@ -411,9 +443,9 @@
         name="backward_own",
     )(queries, attention_gradient, attn, inverse, *([expo] * blocks), own, past_queries)
     own_sum, weight_grad = lax.optimization_barrier((own_sum, weight_grad))
-    total = own_sum + jnp.where(core == 0, crossed, 0).astype(jnp.float32) + come.astype(jnp.float32)
-    total = total.astype(jnp.bfloat16)
-    return (grad_queries, total[:tok], total[tok:], weight_grad)
+    key_shape = jax.ShapeDtypeStruct((tok, HEAD_SIZE), jnp.bfloat16)
+    grad_keys, grad_values = on_core(finish_kernel, "finish", [key_shape] * 2, core, own_sum, crossed, come)
+    return (grad_queries, grad_keys, grad_values, weight_grad)
 
 
 def solution(mesh):

time: 126 us -> 122 us (0.968)
  waiting for transfers between devices: 33.3 us -> 28.7 us
  other arithmetic: 10.2 us -> 7.09 us
  Pallas kernels: 48.4 us -> 50.6 us
  starting transfers between devices: 28.7 us -> 30.4 us
    ppermute x2, waiting for transfers between devices: 12.1 us -> 6.81 us  [step_y(): return lax.ppermute(value, 'tensor', [(t, t ^ 4) for t in range(8)])]
    all_to_all x1, waiting for transfers between devices: 5.22 us -> 8.74 us  [local(): arrived = lax.all_to_all(placed, 'seq', 0, 0, axis_index_groups=groups)]
    convert_element_type x2 -> x0, other arithmetic: 3.2 us -> none  [the longest x1 2.02 us: local(): come = shifted(sent.astype(jnp.bfloat16), 'seq', -2)]
    ppermute x4 -> x5, waiting for transfers between devices: 6.04 us -> 3.42 us  [step_core(): return lax.ppermute(value, 'seq', [(s, s ^ 1) for s in range(16)])]
    pallas_call x3 -> x4, Pallas kernels: 16.7 us -> 18.6 us  [project(): pl.pallas_call(lambda *refs: project_kernel(sources, shapes, groups, *ref...]
    ppermute x2, starting transfers between devices: 4.28 us -> 5.8 us  [step_y(): return lax.ppermute(value, 'tensor', [(t, t ^ 4) for t in range(8)])]
    unnamed x16 -> x10, local copies, waits for them, and re-layouts: 2.81 us -> 3.89 us
  transfers between devices with their start and end apart: 15 -> 16, of which waited for: 7 -> 7; matrix products, arithmetic and copies ran while one was open for 6% -> 4% of each run, Pallas kernels for 33% -> 35%
where the time goes in v5:
time: 122 us
  Pallas kernels  50.6 us (41%)
  starting transfers between devices  30.4 us (25%)
  waiting for transfers between devices  28.7 us (24%)
  other arithmetic  7.09 us (6%)
  local copies, waits for them, and re-layouts  3.98 us (3%)
    pallas_call x4, Pallas kernels, project(): pl.pallas_call(lambda *refs: project_kernel(sources, shapes, groups, *ref...  18.6 us
    pallas_call x1, Pallas kernels, local(): pl.pallas_call(lambda *refs: forward_kernel(tok, span, heads, *refs), gri...  13.2 us
    ppermute x3, waiting for transfers between devices, shifted(): lax.ppermute(value, axis, [(source, source + steps) for source in range(i...  9.77 us
    ppermute x5, starting transfers between devices, step_x(): return lax.ppermute(value, 'tensor', pairs)  9.31 us
    pallas_call x1, Pallas kernels, local(): pl.pallas_call(lambda *refs: backward_past_kernel(tok, heads, *refs), gri...  9.25 us
    all_to_all x1, waiting for transfers between devices, local(): arrived = lax.all_to_all(placed, 'seq', 0, 0, axis_index_groups=groups)  8.74 us
    all_to_all x1, starting transfers between devices, local(): arrived = lax.all_to_all(placed, 'seq', 0, 0, axis_index_groups=groups)  7.25 us
    pallas_call x1, Pallas kernels, local(): pl.pallas_call(lambda *refs: backward_own_kernel(tok, heads, *refs), grid...  7.07 us
  transfers between devices with their start and end apart: 16, of which 7 were waited for; matrix products, arithmetic and copies ran while one was open for 4% of the time, Pallas kernels for 35%

profile of v5, /device:TPU:0, one launch (start us, length us, event | category | flops | bytes accessed | tf_op | source)
XLA Modules:
  0.0 121.6 jit_solution(7041551398962322357)
XLA Ops:
  1.3 1.0 fusion.1.refs_4_.refs_7_
  2.4 1.3 %collective-permute-start.1 = (bf16[1552,128]{1,0:T(8,128)(2,1)S(1)}, bf16[1552,128]{1,0:T(8,128)(2,1)S(1)}, u32[]{:S(2)}, u32[]{:S(2)}) collective-permute-start(bf16[1552,128]{1,0:T(8,128)(2,1)S(1)} %fusion.1.refs_4_.refs_7_), channel_id=1, source_target_pairs={{0,8},{8,16},{16,24},{24,32},{32,40},{40,48},{48,56},{56,64},{64,7... | collective-permute-start | bytes 1191944 | tf_op jit(solution)/shard_map/ppermute | solution.py:19
  3.7 4.2 %collective-permute-start = (bf16[1552,128]{1,0:T(8,128)(2,1)S(1)}, bf16[1552,128]{1,0:T(8,128)(2,1)S(1)}, u32[]{:S(2)}, u32[]{:S(2)}) collective-permute-start(bf16[1552,128]{1,0:T(8,128)(2,1)S(1)} %fusion.1.refs_4_.refs_7_), channel_id=1, source_target_pairs={{0,16},{8,24},{16,32},{24,40},{32,48},{40,56},{48,64},{56,72},{64,... | collective-permute-start | bytes 1191944 | tf_op jit(solution)/shard_map/ppermute | solution.py:19
  7.9 3.1 %collective-permute-start.3 = (bf16[768,512]{1,0:T(8,128)(2,1)}, bf16[768,512]{1,0:T(8,128)(2,1)}, u32[]{:S(2)}, u32[]{:S(2)}) collective-permute-start(bf16[768,512]{1,0:T(8,128)(2,1)} %refs_3_.1), channel_id=1, source_target_pairs={{0,2},{1,3},{2,0},{3,1},{4,6},{5,7},{6,4},{7,5},{8,10},{9,11},{10,... | collective-permute-start | bytes 2359304 | tf_op jit(solution)/shard_map/ppermute | solution.py:24
  11.1 6.4 %collective-permute-done.refs_2_.refs_5_ = bf16[1552,128]{1,0:T(8,128)(2,1)S(1)} collective-permute-done((bf16[1552,128]{1,0:T(8,128)(2,1)S(1)}, bf16[1552,128]{1,0:T(8,128)(2,1)S(1)}, u32[]{:S(2)}, u32[]{:S(2)}) %collective-permute-start) | collective-permute-done | bytes 397344 | tf_op jit(solution)/shard_map/ppermute | solution.py:19
  17.5 2.8 %collective-permute-start.8 = (bf16[768,512]{1,0:T(8,128)(2,1)}, bf16[768,512]{1,0:T(8,128)(2,1)S(1)}, u32[]{:S(2)}, u32[]{:S(2)}) collective-permute-start(bf16[768,512]{1,0:T(8,128)(2,1)} %refs_3_.1), channel_id=1, source_target_pairs={{0,3},{1,0},{2,1},{3,2},{4,7},{5,4},{6,5},{7,6},{8,11},{9,8},{10,9... | collective-permute-start | bytes 2359304 | tf_op jit(solution)/shard_map/ppermute | solution.py:24
  20.3 2.9 %collective-permute-start.2 = (bf16[768,512]{1,0:T(8,128)(2,1)}, bf16[768,512]{1,0:T(8,128)(2,1)}, u32[]{:S(2)}, u32[]{:S(2)}) collective-permute-start(bf16[768,512]{1,0:T(8,128)(2,1)} %refs_3_.1), channel_id=1, source_target_pairs={{0,4},{1,5},{2,6},{3,7},{4,0},{5,1},{6,2},{7,3},{8,12},{9,13},{10,... | collective-permute-start | bytes 2359304 | tf_op jit(solution)/shard_map/ppermute | solution.py:28
  23.9 1.5 %convert_reduce_fusion = s32[768]{0:T(1024)S(1)} fusion(s32[2304]{0:T(1024)S(1)} %pad_add_fusion, s32[768]{0:T(1024)} %param.11), kind=kLoop, calls=%fused_computation | loop fusion | flops 5307648 | bytes 15360 | tf_op jit(solution)/shard_map/reduce_sum | solution.py:341
  25.6 1.1 copy-done
  26.7 13.2 %forward.1 = (bf16[4,768,1792]{2,1,0:T(8,128)(2,1)}, bf16[768,512]{1,0:T(8,128)(2,1)}, bf16[512,768]{1,0:T(8,128)(2,1)}, f32[768,512]{1,0:T(8,128)}) custom-call(s32[768,1]{1,0:T(8,128)S(1)} %reshape_maximum_fusion.refs_0_, bf16[768,512]{1,0:T(8,128)(2,1)S(1)} %copy-done, bf16[1552,128]{1,0:T(8,128)(2,1)S(1)} %collective-permute-done.refs_2_.refs_5_, ...), custom_call_target="tpu_custom_call" | custom-call | flops 2818572288 | bytes 14680064 | tf_op jit(solution)/shard_map/forward/pallas_call | solution.py:349
  39.9 2.1 %collective-permute-done.2.refs_5_ = bf16[768,512]{1,0:T(8,128)(2,1)} collective-permute-done((bf16[768,512]{1,0:T(8,128)(2,1)}, bf16[768,512]{1,0:T(8,128)(2,1)}, u32[]{:S(2)}, u32[]{:S(2)}) %collective-permute-start.2) | collective-permute-done | bytes 786464 | tf_op jit(solution)/shard_map/ppermute | solution.py:28
  42.0 3.4 %collective-permute-start.5 = (bf16[768,512]{1,0:T(8,128)(2,1)}, bf16[768,512]{1,0:T(8,128)(2,1)}, u32[]{:S(2)}, u32[]{:S(2)}) collective-permute-start(bf16[768,512]{1,0:T(8,128)(2,1)} %collective-permute-done.2.refs_5_), channel_id=1, source_target_pairs={{0,3},{1,0},{2,1},{3,2},{4,7},{5,4},{6,5},{7,6},{8,11},{9,8},{10,9... | collective-permute-start | bytes 2359304 | tf_op jit(solution)/shard_map/ppermute | solution.py:24
  45.5 2.9 %collective-permute-start.10 = (bf16[768,512]{1,0:T(8,128)(2,1)}, bf16[768,512]{1,0:T(8,128)(2,1)}, u32[]{:S(2)}, u32[]{:S(2)}) collective-permute-start(bf16[768,512]{1,0:T(8,128)(2,1)} %collective-permute-done.3.refs_4_), channel_id=1, source_target_pairs={{0,4},{1,5},{2,6},{3,7},{4,0},{5,1},{6,2},{7,3},{8,12},{9,13},{10,... | collective-permute-start | bytes 2359304 | tf_op jit(solution)/shard_map/ppermute | solution.py:28
  48.4 5.1 %project.4 = (f32[768,512]{1,0:T(8,128)S(1)}, bf16[3,512,256]{2,1,0:T(8,128)(2,1)S(1)}, bf16[3,512,256]{2,1,0:T(8,128)(2,1)S(1)}) custom-call(s32[4]{0:T(128)S(1)} %pad_add_fusion.2.refs_0_, bf16[512,4096]{1,0:T(8,128)(2,1)} %refs_1_.9, bf16[512,768]{1,0:T(8,128)(2,1)} %get-tuple-element.38.refs_2_, bf16[768,512]{1,0:T(8,128)(2,1)} %refs_3_.1, ...), custom_call_target="tpu_custom_call" | custom-call | flops 2415919104 | bytes 1048576 | tf_op jit(solution)/shard_map/project/pallas_call | solution.py:274
  53.5 0.9 copy-done.1
  54.5 0.8 copy-done.3
  55.6 5.0 %project.5 = (f32[768,512]{1,0:T(8,128)S(1)}, bf16[2,512,256]{2,1,0:T(8,128)(2,1)S(1)}, bf16[2,512,256]{2,1,0:T(8,128)(2,1)}) custom-call(s32[3]{0:T(128)S(1)} %pad_add_fusion.3.refs_0_, bf16[512,4096]{1,0:T(8,128)(2,1)} %refs_1_.9, bf16[512,768]{1,0:T(8,128)(2,1)} %get-tuple-element.38.refs_2_, bf16[768,512]{1,0:T(8,128)(2,1)} %copy-done.4, ...), custom_call_target="tpu_custom_call" | custom-call | flops 1610612736 | bytes 1048576 | tf_op jit(solution)/shard_map/project/pallas_call | solution.py:274
  60.6 0.8 copy-done.2
  61.9 4.7 %collective-permute-done.10.refs_3_ = bf16[768,512]{1,0:T(8,128)(2,1)} collective-permute-done((bf16[768,512]{1,0:T(8,128)(2,1)}, bf16[768,512]{1,0:T(8,128)(2,1)}, u32[]{:S(2)}, u32[]{:S(2)}) %collective-permute-start.10) | collective-permute-done | bytes 786464 | tf_op jit(solution)/shard_map/ppermute | solution.py:28
  66.6 3.1 %project.6 = (f32[768,512]{1,0:T(8,128)S(1)}, bf16[1,512,256]{2,1,0:T(8,128)(2,1)S(1)}, bf16[1,512,256]{2,1,0:T(8,128)(2,1)S(1)}) custom-call(s32[2]{0:T(128)S(1)} %pad_add_fusion.4.refs_0_, bf16[512,4096]{1,0:T(8,128)(2,1)} %refs_1_.9, bf16[512,768]{1,0:T(8,128)(2,1)} %get-tuple-element.38.refs_2_, bf16[768,512]{1,0:T(8,128)(2,1)} %collective-permute-done.10.refs_3_, ...), custom_call_target="tpu_custom_call" | custom-call | flops 805306368 | bytes 1048576 | tf_op jit(solution)/shard_map/project/pallas_call | solution.py:274
  69.7 5.4 %project.7 = (bf16[768,512]{1,0:T(8,128)(2,1)S(1)}, bf16[2,512,256]{2,1,0:T(8,128)(2,1)S(1)}, bf16[2,512,256]{2,1,0:T(8,128)(2,1)S(1)}, bf16[8,512,256]{2,1,0:T(8,128)(2,1)}) custom-call(s32[8]{0:T(128)S(1)} %stack.63.refs_0_, bf16[512,4096]{1,0:T(8,128)(2,1)} %refs_1_.9, bf16[512,768]{1,0:T(8,128)(2,1)} %get-tuple-element.38.refs_2_, ...), custom_call_target="tpu_custom_call" | custom-call | flops 1048576 | bytes 1048576 | tf_op jit(solution)/shard_map/project/pallas_call | solution.py:274
  75.7 1.7 %collective-permute-done.12.last_come_ref = bf16[1,512,256]{2,1,0:T(8,128)(2,1)S(1)} collective-permute-done((bf16[1,512,256]{2,1,0:T(8,128)(2,1)S(1)}, bf16[1,512,256]{2,1,0:T(8,128)(2,1)S(1)}, u32[]{:S(2)}, u32[]{:S(2)}) %collective-permute-start.12) | collective-permute-done | bytes 262176 | tf_op jit(solution)/shard_map/ppermute | solution.py:32
  77.5 1.6 %place.1 = bf16[8,512,256]{2,1,0:T(8,128)(2,1)} custom-call(s32[3]{0:T(128)S(1)} %pad_add_fusion.1.where_ref, bf16[2,512,256]{2,1,0:T(8,128)(2,1)S(1)} %get-tuple-element.48.mine_ref, bf16[2,512,256]{2,1,0:T(8,128)(2,1)S(1)} %collective-permute-done.11.come_ref, ...), custom_call_target="tpu_custom_call", output_to_operand_aliasing={{}: (5, {})} | custom-call | flops 1048576 | bytes 1048576 | tf_op jit(solution)/shard_map/place/pallas_call | solution.py:401
  79.0 7.2 %all-to-all-start = ((bf16[8,512,256]{2,1,0:T(8,128)(2,1)}), bf16[8,512,256]{2,1,0:T(8,128)(2,1)}, u32[]{:S(2)}, u32[]{:S(2)}) async-start(bf16[8,512,256]{2,1,0:T(8,128)(2,1)} %place.1), calls=%async_computation | async-start | bytes 4194304 | tf_op jit(solution)/shard_map/all_to_all | solution.py:414
  86.3 9.2 %backward_past.1 = (f32[768,512]{1,0:T(8,128)S(1)}, bf16[1536,128]{1,0:T(8,128)(2,1)S(1)}, bf16[1536,128]{1,0:T(8,128)(2,1)S(1)}) custom-call(bf16[768,512]{1,0:T(8,128)(2,1)} %refs_0_.3, bf16[768,512]{1,0:T(8,128)(2,1)S(1)} %get-tuple-element.54.refs_1_, bf16[768,512]{1,0:T(8,128)(2,1)} %get-tuple-element.55.refs_2_, f32[768,512]{1,0:T(8,128)} %get-tuple-element.56.refs_3_, ...), custom_call_target="tpu_custom_call" | custom-call | flops 1048576 | bytes 1048576 | tf_op jit(solution)/shard_map/backward_past/pallas_call | solution.py:419
  95.6 1.7 %collective-permute-done.13.crossed_ref = bf16[1536,128]{1,0:T(8,128)(2,1)S(1)} collective-permute-done((bf16[1536,128]{1,0:T(8,128)(2,1)S(1)}, bf16[1536,128]{1,0:T(8,128)(2,1)S(1)}, u32[]{:S(2)}, u32[]{:S(2)}) %collective-permute-start.13) | collective-permute-done | bytes 393248 | tf_op jit(solution)/shard_map/ppermute | solution.py:32
  97.4 1.5 %collective-permute-start.14 = (bf16[1536,128]{1,0:T(8,128)(2,1)S(1)}, bf16[1536,128]{1,0:T(8,128)(2,1)S(1)}, u32[]{:S(2)}, u32[]{:S(2)}) collective-permute-start(bf16[1536,128]{1,0:T(8,128)(2,1)S(1)} %send.1), channel_id=1, source_target_pairs={{16,0},{24,8},{32,16},{40,24},{48,32},{56,40},{64,48},{72,56},{80,... | collective-permute-start | bytes 1179656 | tf_op jit(solution)/shard_map/ppermute | solution.py:19
  99.0 7.1 %backward_own.1 = (bf16[768,512]{1,0:T(8,128)(2,1)}, f32[1536,128]{1,0:T(8,128)S(1)}) custom-call(bf16[768,512]{1,0:T(8,128)(2,1)} %refs_0_.3, bf16[768,512]{1,0:T(8,128)(2,1)S(1)} %get-tuple-element.54.refs_1_, bf16[768,512]{1,0:T(8,128)(2,1)} %get-tuple-element.55.refs_2_, f32[768,512]{1,0:T(8,128)} %get-tuple-element.56.refs_3_, ...), custom_call_target="tpu_custom_call" | custom-call | flops 1048576 | bytes 1048576 | tf_op jit(solution)/shard_map/backward_own/pallas_call | solution.py:434
  106.0 8.7 %all-to-all-done = bf16[8,512,256]{2,1,0:T(8,128)(2,1)} async-done(((bf16[8,512,256]{2,1,0:T(8,128)(2,1)}), bf16[8,512,256]{2,1,0:T(8,128)(2,1)}, u32[]{:S(2)}, u32[]{:S(2)}) %all-to-all-start) | async-done | bytes 2097184 | tf_op jit(solution)/shard_map/all_to_all | solution.py:414
  114.8 2.6 %reduce_sum.25 = bf16[512,256]{1,0:T(8,128)(2,1)} reduce(bf16[8,512,256]{2,1,0:T(8,128)(2,1)} %all-to-all-done, bf16[]{:T(256)} %constant.75.clone.1), dimensions={0}, to_apply=%region_1.2 | reduce | flops 917504 | bytes 2359298 | tf_op jit(solution)/shard_map/reduce_sum | solution.py:415
  117.4 3.3 %collective-permute-done.14.come_ref = bf16[1536,128]{1,0:T(8,128)(2,1)S(1)} collective-permute-done((bf16[1536,128]{1,0:T(8,128)(2,1)S(1)}, bf16[1536,128]{1,0:T(8,128)(2,1)S(1)}, u32[]{:S(2)}, u32[]{:S(2)}) %collective-permute-start.14) | collective-permute-done | bytes 393248 | tf_op jit(solution)/shard_map/ppermute | solution.py:19
  120.8 0.8 finish.1
  (33 shorter events, 3.4 us)
Async XLA Ops:
  2.4 8.7 %collective-permute-start.1 = (bf16[1552,128]{1,0:T(8,128)(2,1)S(1)}, bf16[1552,128]{1,0:T(8,128)(2,1)S(1)}, u32[]{:S(2)}, u32[]{:S(2)}) collective-permute-start(bf16[1552,128]{1,0:T(8,128)(2,1)S(1)} %fusion.1.refs_4_.refs_7_), channel_id=1, source_target_pairs={{0,8},{8,16},{16,24},{24,32},{32,40},{40,48},{48,56},{56,64},{64,7... | collective-permute-start | bytes 1191944 | tf_op jit(solution)/shard_map/ppermute | solution.py:19
  3.7 13.8 %collective-permute-start = (bf16[1552,128]{1,0:T(8,128)(2,1)S(1)}, bf16[1552,128]{1,0:T(8,128)(2,1)S(1)}, u32[]{:S(2)}, u32[]{:S(2)}) collective-permute-start(bf16[1552,128]{1,0:T(8,128)(2,1)S(1)} %fusion.1.refs_4_.refs_7_), channel_id=1, source_target_pairs={{0,16},{8,24},{16,32},{24,40},{32,48},{40,56},{48,64},{56,72},{64,... | collective-permute-start | bytes 1191944 | tf_op jit(solution)/shard_map/ppermute | solution.py:19
  7.9 32.0 %collective-permute-start.3 = (bf16[768,512]{1,0:T(8,128)(2,1)}, bf16[768,512]{1,0:T(8,128)(2,1)}, u32[]{:S(2)}, u32[]{:S(2)}) collective-permute-start(bf16[768,512]{1,0:T(8,128)(2,1)} %refs_3_.1), channel_id=1, source_target_pairs={{0,2},{1,3},{2,0},{3,1},{4,6},{5,7},{6,4},{7,5},{8,10},{9,11},{10,... | collective-permute-start | bytes 2359304 | tf_op jit(solution)/shard_map/ppermute | solution.py:24
  17.5 36.9 %collective-permute-start.8 = (bf16[768,512]{1,0:T(8,128)(2,1)}, bf16[768,512]{1,0:T(8,128)(2,1)S(1)}, u32[]{:S(2)}, u32[]{:S(2)}) collective-permute-start(bf16[768,512]{1,0:T(8,128)(2,1)} %refs_3_.1), channel_id=1, source_target_pairs={{0,3},{1,0},{2,1},{3,2},{4,7},{5,4},{6,5},{7,6},{8,11},{9,8},{10,9... | collective-permute-start | bytes 2359304 | tf_op jit(solution)/shard_map/ppermute | solution.py:24
  20.3 34.2 %collective-permute-start.7 = (bf16[768,512]{1,0:T(8,128)(2,1)}, bf16[768,512]{1,0:T(8,128)(2,1)S(1)}, u32[]{:S(2)}, u32[]{:S(2)}) collective-permute-start(bf16[768,512]{1,0:T(8,128)(2,1)} %refs_3_.1), channel_id=1, source_target_pairs={{0,1},{1,2},{2,3},{3,0},{4,5},{5,6},{6,7},{7,4},{8,9},{9,10},{10,1... | collective-permute-start | bytes 2359304 | tf_op jit(solution)/shard_map/ppermute | solution.py:24
  20.3 21.7 %collective-permute-start.2 = (bf16[768,512]{1,0:T(8,128)(2,1)}, bf16[768,512]{1,0:T(8,128)(2,1)}, u32[]{:S(2)}, u32[]{:S(2)}) collective-permute-start(bf16[768,512]{1,0:T(8,128)(2,1)} %refs_3_.1), channel_id=1, source_target_pairs={{0,4},{1,5},{2,6},{3,7},{4,0},{5,1},{6,2},{7,3},{8,12},{9,13},{10,... | collective-permute-start | bytes 2359304 | tf_op jit(solution)/shard_map/ppermute | solution.py:28
  25.6 1.1 copy-start
  42.0 27.6 %collective-permute-start.5 = (bf16[768,512]{1,0:T(8,128)(2,1)}, bf16[768,512]{1,0:T(8,128)(2,1)}, u32[]{:S(2)}, u32[]{:S(2)}) collective-permute-start(bf16[768,512]{1,0:T(8,128)(2,1)} %collective-permute-done.2.refs_5_), channel_id=1, source_target_pairs={{0,3},{1,0},{2,1},{3,2},{4,7},{5,4},{6,5},{7,6},{8,11},{9,8},{10,9... | collective-permute-start | bytes 2359304 | tf_op jit(solution)/shard_map/ppermute | solution.py:24
  45.5 24.2 %collective-permute-start.4 = (bf16[768,512]{1,0:T(8,128)(2,1)}, bf16[768,512]{1,0:T(8,128)(2,1)}, u32[]{:S(2)}, u32[]{:S(2)}) collective-permute-start(bf16[768,512]{1,0:T(8,128)(2,1)} %collective-permute-done.2.refs_5_), channel_id=1, source_target_pairs={{0,1},{1,2},{2,3},{3,0},{4,5},{5,6},{6,7},{7,4},{8,9},{9,10},{10,1... | collective-permute-start | bytes 2359304 | tf_op jit(solution)/shard_map/ppermute | solution.py:24
  45.5 21.1 %collective-permute-start.10 = (bf16[768,512]{1,0:T(8,128)(2,1)}, bf16[768,512]{1,0:T(8,128)(2,1)}, u32[]{:S(2)}, u32[]{:S(2)}) collective-permute-start(bf16[768,512]{1,0:T(8,128)(2,1)} %collective-permute-done.3.refs_4_), channel_id=1, source_target_pairs={{0,4},{1,5},{2,6},{3,7},{4,0},{5,1},{6,2},{7,3},{8,12},{9,13},{10,... | collective-permute-start | bytes 2359304 | tf_op jit(solution)/shard_map/ppermute | solution.py:28
  53.5 0.9 copy-start.1
  54.4 0.9 copy-start.3
  54.4 15.3 %collective-permute-start.6 = (bf16[3,512,256]{2,1,0:T(8,128)(2,1)S(1)}, bf16[3,512,256]{2,1,0:T(8,128)(2,1)}, u32[]{:S(2)}, u32[]{:S(2)}) collective-permute-start(bf16[3,512,256]{2,1,0:T(8,128)(2,1)S(1)} %get-tuple-element.42), channel_id=1, source_target_pairs={{0,8},{8,0},{16,24},{24,16},{32,40},{40,32},{48,56},{56,48},{64,72... | collective-permute-start | bytes 2359304 | tf_op jit(solution)/shard_map/ppermute | solution.py:32
  54.5 1.1 copy-start.4
  60.6 0.8 copy-start.2
  61.4 8.3 %collective-permute-start.9 = (bf16[2,512,256]{2,1,0:T(8,128)(2,1)}, bf16[2,512,256]{2,1,0:T(8,128)(2,1)}, u32[]{:S(2)}, u32[]{:S(2)}) collective-permute-start(bf16[2,512,256]{2,1,0:T(8,128)(2,1)} %get-tuple-element.45), channel_id=1, source_target_pairs={{0,8},{8,0},{16,24},{24,16},{32,40},{40,32},{48,56},{56,48},{64,72... | collective-permute-start | bytes 1572872 | tf_op jit(solution)/shard_map/ppermute | solution.py:32
  75.1 2.4 %collective-permute-start.11 = (bf16[2,512,256]{2,1,0:T(8,128)(2,1)S(1)}, bf16[2,512,256]{2,1,0:T(8,128)(2,1)S(1)}, u32[]{:S(2)}, u32[]{:S(2)}) collective-permute-start(bf16[2,512,256]{2,1,0:T(8,128)(2,1)S(1)} %get-tuple-element.49), channel_id=1, source_target_pairs={{0,8},{8,0},{16,24},{24,16},{32,40},{40,32},{48,56},{56,48},{64,72... | collective-permute-start | bytes 1572872 | tf_op jit(solution)/shard_map/ppermute | solution.py:32
  75.2 2.3 %collective-permute-start.12 = (bf16[1,512,256]{2,1,0:T(8,128)(2,1)S(1)}, bf16[1,512,256]{2,1,0:T(8,128)(2,1)S(1)}, u32[]{:S(2)}, u32[]{:S(2)}) collective-permute-start(bf16[1,512,256]{2,1,0:T(8,128)(2,1)S(1)} %get-tuple-element.51), channel_id=1, source_target_pairs={{0,8},{8,0},{16,24},{24,16},{32,40},{40,32},{48,56},{56,48},{64,72... | collective-permute-start | bytes 786440 | tf_op jit(solution)/shard_map/ppermute | solution.py:32
  79.0 35.8 %all-to-all-start = ((bf16[8,512,256]{2,1,0:T(8,128)(2,1)}), bf16[8,512,256]{2,1,0:T(8,128)(2,1)}, u32[]{:S(2)}, u32[]{:S(2)}) async-start(bf16[8,512,256]{2,1,0:T(8,128)(2,1)} %place.1), calls=%async_computation | async-start | bytes 4194304 | tf_op jit(solution)/shard_map/all_to_all | solution.py:414
  95.5 1.8 %collective-permute-start.13 = (bf16[1536,128]{1,0:T(8,128)(2,1)S(1)}, bf16[1536,128]{1,0:T(8,128)(2,1)S(1)}, u32[]{:S(2)}, u32[]{:S(2)}) collective-permute-start(bf16[1536,128]{1,0:T(8,128)(2,1)S(1)} %get-tuple-element.63), channel_id=1, source_target_pairs={{0,8},{8,0},{16,24},{24,16},{32,40},{40,32},{48,56},{56,48},{64,72... | collective-permute-start | bytes 1179656 | tf_op jit(solution)/shard_map/ppermute | solution.py:32
  97.4 23.3 %collective-permute-start.14 = (bf16[1536,128]{1,0:T(8,128)(2,1)S(1)}, bf16[1536,128]{1,0:T(8,128)(2,1)S(1)}, u32[]{:S(2)}, u32[]{:S(2)}) collective-permute-start(bf16[1536,128]{1,0:T(8,128)(2,1)S(1)} %send.1), channel_id=1, source_target_pairs={{16,0},{24,8},{32,16},{40,24},{48,32},{56,40},{64,48},{72,56},{80,... | collective-permute-start | bytes 1179656 | tf_op jit(solution)/shard_map/ppermute | solution.py:19

commit v6 on v5

--- a/solution.py
+++ b/solution.py
@@ -372,8 +372,9 @@
     places = [at(0, 0), at(0, 2), at(1, 0), at(0, 3), at(0, 1), at(1, 3), at(1, 1), at(1, 2)]
     where = lambda some: jnp.stack([core, *some]).astype(jnp.int32)
     opposite = step_x(out_grad, 2)
-    later = lax.optimization_barrier((out_grad, far, near))[0]
-    across, near_up, near_down = step_y(later), step_x(later, 1), step_x(later, -1)
+    across = step_y(lax.optimization_barrier((out_grad, far, near))[0])
+    later, low = lax.optimization_barrier((out_grad, low))
+    near_up, near_down = step_x(later, 1), step_x(later, -1)
     across, opposite, turned = lax.optimization_barrier((across, opposite, turned))
     across_up, across_down = step_x(across, 1), step_x(across, -1)
     weight, turned = in_hbm(out_weight), in_hbm(turned)

time: 122 us -> 121 us (level)
  starting transfers between devices: 30.4 us -> 29.1 us
    ppermute x2, starting transfers between devices: 5.8 us -> 4.07 us  [step_y(): return lax.ppermute(value, 'tensor', [(t, t ^ 4) for t in range(8)])]
  transfers between devices with their start and end apart: 16 -> 16, of which waited for: 7 -> 6; matrix products, arithmetic and copies ran while one was open for 4% -> 4% of each run, Pallas kernels for 35% -> 35%
where the time goes in v6:
time: 121 us
  Pallas kernels  50.6 us (42%)
  starting transfers between devices  29.1 us (24%)
  waiting for transfers between devices  28.8 us (24%)
  other arithmetic  7.08 us (6%)
  local copies, waits for them, and re-layouts  4.35 us (4%)
    pallas_call x4, Pallas kernels, project(): pl.pallas_call(lambda *refs: project_kernel(sources, shapes, groups, *ref...  18.6 us
    pallas_call x1, Pallas kernels, local(): pl.pallas_call(lambda *refs: forward_kernel(tok, span, heads, *refs), gri...  13.2 us
    ppermute x3, waiting for transfers between devices, shifted(): lax.ppermute(value, axis, [(source, source + steps) for source in range(i...  9.85 us
    ppermute x5, starting transfers between devices, step_x(): return lax.ppermute(value, 'tensor', pairs)  9.24 us
    pallas_call x1, Pallas kernels, local(): pl.pallas_call(lambda *refs: backward_past_kernel(tok, heads, *refs), gri...  9.24 us
    all_to_all x1, waiting for transfers between devices, local(): arrived = lax.all_to_all(placed, 'seq', 0, 0, axis_index_groups=groups)  8.76 us
    all_to_all x1, starting transfers between devices, local(): arrived = lax.all_to_all(placed, 'seq', 0, 0, axis_index_groups=groups)  7.53 us
    pallas_call x1, Pallas kernels, local(): pl.pallas_call(lambda *refs: backward_own_kernel(tok, heads, *refs), grid...  7.06 us
  transfers between devices with their start and end apart: 16, of which 6 were waited for; matrix products, arithmetic and copies ran while one was open for 4% of the time, Pallas kernels for 35%

profile of v6, /device:TPU:0, one launch (start us, length us, event | category | flops | bytes accessed | tf_op | source)
XLA Modules:
  0.0 120.7 jit_solution(1948054134300922557)
XLA Ops:
  1.3 1.0 fusion.1.refs_4_.refs_7_
  2.4 1.3 %collective-permute-start.1 = (bf16[1552,128]{1,0:T(8,128)(2,1)S(1)}, bf16[1552,128]{1,0:T(8,128)(2,1)S(1)}, u32[]{:S(2)}, u32[]{:S(2)}) collective-permute-start(bf16[1552,128]{1,0:T(8,128)(2,1)S(1)} %fusion.1.refs_4_.refs_7_), channel_id=1, source_target_pairs={{0,8},{8,16},{16,24},{24,32},{32,40},{40,48},{48,56},{56,64},{64,7... | collective-permute-start | bytes 1191944 | tf_op jit(solution)/shard_map/ppermute | solution.py:19
  3.7 4.2 %collective-permute-start = (bf16[1552,128]{1,0:T(8,128)(2,1)S(1)}, bf16[1552,128]{1,0:T(8,128)(2,1)S(1)}, u32[]{:S(2)}, u32[]{:S(2)}) collective-permute-start(bf16[1552,128]{1,0:T(8,128)(2,1)S(1)} %fusion.1.refs_4_.refs_7_), channel_id=1, source_target_pairs={{0,16},{8,24},{16,32},{24,40},{32,48},{40,56},{48,64},{56,72},{64,... | collective-permute-start | bytes 1191944 | tf_op jit(solution)/shard_map/ppermute | solution.py:19
  7.9 3.1 %collective-permute-start.3 = (bf16[768,512]{1,0:T(8,128)(2,1)}, bf16[768,512]{1,0:T(8,128)(2,1)}, u32[]{:S(2)}, u32[]{:S(2)}) collective-permute-start(bf16[768,512]{1,0:T(8,128)(2,1)} %refs_3_.1), channel_id=1, source_target_pairs={{0,2},{1,3},{2,0},{3,1},{4,6},{5,7},{6,4},{7,5},{8,10},{9,11},{10,... | collective-permute-start | bytes 2359304 | tf_op jit(solution)/shard_map/ppermute | solution.py:24
  11.0 6.5 %collective-permute-done.refs_2_.refs_5_ = bf16[1552,128]{1,0:T(8,128)(2,1)S(1)} collective-permute-done((bf16[1552,128]{1,0:T(8,128)(2,1)S(1)}, bf16[1552,128]{1,0:T(8,128)(2,1)S(1)}, u32[]{:S(2)}, u32[]{:S(2)}) %collective-permute-start) | collective-permute-done | bytes 397344 | tf_op jit(solution)/shard_map/ppermute | solution.py:19
  17.5 2.9 %collective-permute-start.2 = (bf16[768,512]{1,0:T(8,128)(2,1)}, bf16[768,512]{1,0:T(8,128)(2,1)}, u32[]{:S(2)}, u32[]{:S(2)}) collective-permute-start(bf16[768,512]{1,0:T(8,128)(2,1)} %refs_3_.1), channel_id=1, source_target_pairs={{0,4},{1,5},{2,6},{3,7},{4,0},{5,1},{6,2},{7,3},{8,12},{9,13},{10,... | collective-permute-start | bytes 2359304 | tf_op jit(solution)/shard_map/ppermute | solution.py:28
  20.4 0.7 pad_add_fusion
  21.1 1.5 %convert_reduce_fusion = s32[768]{0:T(1024)S(1)} fusion(s32[2304]{0:T(1024)S(1)} %pad_add_fusion, s32[768]{0:T(1024)} %param.11), kind=kLoop, calls=%fused_computation | loop fusion | flops 5307648 | bytes 15360 | tf_op jit(solution)/shard_map/reduce_sum | solution.py:341
  22.8 2.8 %collective-permute-start.8 = (bf16[768,512]{1,0:T(8,128)(2,1)}, bf16[768,512]{1,0:T(8,128)(2,1)S(1)}, u32[]{:S(2)}, u32[]{:S(2)}) collective-permute-start(bf16[768,512]{1,0:T(8,128)(2,1)} %refs_3_.1), channel_id=1, source_target_pairs={{0,3},{1,0},{2,1},{3,2},{4,7},{5,4},{6,5},{7,6},{8,11},{9,8},{10,9... | collective-permute-start | bytes 2359304 | tf_op jit(solution)/shard_map/ppermute | solution.py:24
  25.7 1.1 copy-done
  26.9 13.2 %forward.1 = (bf16[4,768,1792]{2,1,0:T(8,128)(2,1)}, bf16[768,512]{1,0:T(8,128)(2,1)}, bf16[512,768]{1,0:T(8,128)(2,1)}, f32[768,512]{1,0:T(8,128)}) custom-call(s32[768,1]{1,0:T(8,128)S(1)} %reshape_maximum_fusion.refs_0_, bf16[768,512]{1,0:T(8,128)(2,1)S(1)} %copy-done, bf16[1552,128]{1,0:T(8,128)(2,1)S(1)} %collective-permute-done.refs_2_.refs_5_, ...), custom_call_target="tpu_custom_call" | custom-call | flops 2818572288 | bytes 14680064 | tf_op jit(solution)/shard_map/forward/pallas_call | solution.py:349
  40.1 3.3 %collective-permute-start.5 = (bf16[768,512]{1,0:T(8,128)(2,1)}, bf16[768,512]{1,0:T(8,128)(2,1)}, u32[]{:S(2)}, u32[]{:S(2)}) collective-permute-start(bf16[768,512]{1,0:T(8,128)(2,1)} %collective-permute-done.2.refs_5_), channel_id=1, source_target_pairs={{0,3},{1,0},{2,1},{3,2},{4,7},{5,4},{6,5},{7,6},{8,11},{9,8},{10,9... | collective-permute-start | bytes 2359304 | tf_op jit(solution)/shard_map/ppermute | solution.py:24
  43.4 1.2 collective-permute-start.10
  44.6 5.1 %project.4 = (f32[768,512]{1,0:T(8,128)S(1)}, bf16[3,512,256]{2,1,0:T(8,128)(2,1)S(1)}, bf16[3,512,256]{2,1,0:T(8,128)(2,1)S(1)}) custom-call(s32[4]{0:T(128)S(1)} %pad_add_fusion.2.refs_0_, bf16[512,4096]{1,0:T(8,128)(2,1)} %refs_1_.9, bf16[512,768]{1,0:T(8,128)(2,1)} %get-tuple-element.39.refs_2_, bf16[768,512]{1,0:T(8,128)(2,1)} %refs_3_.1, ...), custom_call_target="tpu_custom_call" | custom-call | flops 2415919104 | bytes 1048576 | tf_op jit(solution)/shard_map/project/pallas_call | solution.py:274
  49.7 0.9 copy-done.1
  51.5 0.9 copy-done.4
  52.4 5.0 %project.5 = (f32[768,512]{1,0:T(8,128)S(1)}, bf16[2,512,256]{2,1,0:T(8,128)(2,1)S(1)}, bf16[2,512,256]{2,1,0:T(8,128)(2,1)}) custom-call(s32[3]{0:T(128)S(1)} %pad_add_fusion.3.refs_0_, bf16[512,4096]{1,0:T(8,128)(2,1)} %refs_1_.9, bf16[512,768]{1,0:T(8,128)(2,1)} %get-tuple-element.39.refs_2_, bf16[768,512]{1,0:T(8,128)(2,1)} %copy-done.4, ...), custom_call_target="tpu_custom_call" | custom-call | flops 1610612736 | bytes 1048576 | tf_op jit(solution)/shard_map/project/pallas_call | solution.py:274
  57.5 0.8 copy-done.2
  58.7 6.7 %collective-permute-done.10.refs_3_ = bf16[768,512]{1,0:T(8,128)(2,1)} collective-permute-done((bf16[768,512]{1,0:T(8,128)(2,1)}, bf16[768,512]{1,0:T(8,128)(2,1)}, u32[]{:S(2)}, u32[]{:S(2)}) %collective-permute-start.10) | collective-permute-done | bytes 786464 | tf_op jit(solution)/shard_map/ppermute | solution.py:28
  65.4 3.0 %project.6 = (f32[768,512]{1,0:T(8,128)S(1)}, bf16[1,512,256]{2,1,0:T(8,128)(2,1)S(1)}, bf16[1,512,256]{2,1,0:T(8,128)(2,1)S(1)}) custom-call(s32[2]{0:T(128)S(1)} %pad_add_fusion.4.refs_0_, bf16[512,4096]{1,0:T(8,128)(2,1)} %refs_1_.9, bf16[512,768]{1,0:T(8,128)(2,1)} %get-tuple-element.39.refs_2_, bf16[768,512]{1,0:T(8,128)(2,1)} %collective-permute-done.10.refs_3_, ...), custom_call_target="tpu_custom_call" | custom-call | flops 805306368 | bytes 1048576 | tf_op jit(solution)/shard_map/project/pallas_call | solution.py:274
  68.5 5.4 %project.7 = (bf16[768,512]{1,0:T(8,128)(2,1)S(1)}, bf16[2,512,256]{2,1,0:T(8,128)(2,1)S(1)}, bf16[2,512,256]{2,1,0:T(8,128)(2,1)S(1)}, bf16[8,512,256]{2,1,0:T(8,128)(2,1)}) custom-call(s32[8]{0:T(128)S(1)} %stack.63.refs_0_, bf16[512,4096]{1,0:T(8,128)(2,1)} %refs_1_.9, bf16[512,768]{1,0:T(8,128)(2,1)} %get-tuple-element.39.refs_2_, ...), custom_call_target="tpu_custom_call" | custom-call | flops 1048576 | bytes 1048576 | tf_op jit(solution)/shard_map/project/pallas_call | solution.py:274
  74.6 1.7 %collective-permute-done.12.last_come_ref = bf16[1,512,256]{2,1,0:T(8,128)(2,1)S(1)} collective-permute-done((bf16[1,512,256]{2,1,0:T(8,128)(2,1)S(1)}, bf16[1,512,256]{2,1,0:T(8,128)(2,1)S(1)}, u32[]{:S(2)}, u32[]{:S(2)}) %collective-permute-start.12) | collective-permute-done | bytes 262176 | tf_op jit(solution)/shard_map/ppermute | solution.py:32
  76.3 1.6 %place.1 = bf16[8,512,256]{2,1,0:T(8,128)(2,1)} custom-call(s32[3]{0:T(128)S(1)} %pad_add_fusion.1.where_ref, bf16[2,512,256]{2,1,0:T(8,128)(2,1)S(1)} %get-tuple-element.50.mine_ref, bf16[2,512,256]{2,1,0:T(8,128)(2,1)S(1)} %collective-permute-done.11.come_ref, ...), custom_call_target="tpu_custom_call", output_to_operand_aliasing={{}: (5, {})} | custom-call | flops 1048576 | bytes 1048576 | tf_op jit(solution)/shard_map/place/pallas_call | solution.py:402
  77.8 7.5 %all-to-all-start = ((bf16[8,512,256]{2,1,0:T(8,128)(2,1)}), bf16[8,512,256]{2,1,0:T(8,128)(2,1)}, u32[]{:S(2)}, u32[]{:S(2)}) async-start(bf16[8,512,256]{2,1,0:T(8,128)(2,1)} %place.1), calls=%async_computation | async-start | bytes 4194304 | tf_op jit(solution)/shard_map/all_to_all | solution.py:415
  85.4 9.2 %backward_past.1 = (f32[768,512]{1,0:T(8,128)S(1)}, bf16[1536,128]{1,0:T(8,128)(2,1)S(1)}, bf16[1536,128]{1,0:T(8,128)(2,1)S(1)}) custom-call(bf16[768,512]{1,0:T(8,128)(2,1)} %refs_0_.3, bf16[768,512]{1,0:T(8,128)(2,1)S(1)} %get-tuple-element.56.refs_1_, bf16[768,512]{1,0:T(8,128)(2,1)} %get-tuple-element.57.refs_2_, f32[768,512]{1,0:T(8,128)} %get-tuple-element.58.refs_3_, ...), custom_call_target="tpu_custom_call" | custom-call | flops 1048576 | bytes 1048576 | tf_op jit(solution)/shard_map/backward_past/pallas_call | solution.py:420
  94.7 1.7 %collective-permute-done.13.crossed_ref = bf16[1536,128]{1,0:T(8,128)(2,1)S(1)} collective-permute-done((bf16[1536,128]{1,0:T(8,128)(2,1)S(1)}, bf16[1536,128]{1,0:T(8,128)(2,1)S(1)}, u32[]{:S(2)}, u32[]{:S(2)}) %collective-permute-start.13) | collective-permute-done | bytes 393248 | tf_op jit(solution)/shard_map/ppermute | solution.py:32
  96.5 1.5 %collective-permute-start.14 = (bf16[1536,128]{1,0:T(8,128)(2,1)S(1)}, bf16[1536,128]{1,0:T(8,128)(2,1)S(1)}, u32[]{:S(2)}, u32[]{:S(2)}) collective-permute-start(bf16[1536,128]{1,0:T(8,128)(2,1)S(1)} %send.1), channel_id=1, source_target_pairs={{16,0},{24,8},{32,16},{40,24},{48,32},{56,40},{64,48},{72,56},{80,... | collective-permute-start | bytes 1179656 | tf_op jit(solution)/shard_map/ppermute | solution.py:19
  98.0 7.1 %backward_own.1 = (bf16[768,512]{1,0:T(8,128)(2,1)}, f32[1536,128]{1,0:T(8,128)S(1)}) custom-call(bf16[768,512]{1,0:T(8,128)(2,1)} %refs_0_.3, bf16[768,512]{1,0:T(8,128)(2,1)S(1)} %get-tuple-element.56.refs_1_, bf16[768,512]{1,0:T(8,128)(2,1)} %get-tuple-element.57.refs_2_, f32[768,512]{1,0:T(8,128)} %get-tuple-element.58.refs_3_, ...), custom_call_target="tpu_custom_call" | custom-call | flops 1048576 | bytes 1048576 | tf_op jit(solution)/shard_map/backward_own/pallas_call | solution.py:435
  105.1 8.8 %all-to-all-done = bf16[8,512,256]{2,1,0:T(8,128)(2,1)} async-done(((bf16[8,512,256]{2,1,0:T(8,128)(2,1)}), bf16[8,512,256]{2,1,0:T(8,128)(2,1)}, u32[]{:S(2)}, u32[]{:S(2)}) %all-to-all-start) | async-done | bytes 2097184 | tf_op jit(solution)/shard_map/all_to_all | solution.py:415
  113.9 2.6 %reduce_sum.25 = bf16[512,256]{1,0:T(8,128)(2,1)} reduce(bf16[8,512,256]{2,1,0:T(8,128)(2,1)} %all-to-all-done, bf16[]{:T(256)} %constant.75.clone.1), dimensions={0}, to_apply=%region_1.2 | reduce | flops 917504 | bytes 2359298 | tf_op jit(solution)/shard_map/reduce_sum | solution.py:416
  116.5 3.3 %collective-permute-done.14.come_ref = bf16[1536,128]{1,0:T(8,128)(2,1)S(1)} collective-permute-done((bf16[1536,128]{1,0:T(8,128)(2,1)S(1)}, bf16[1536,128]{1,0:T(8,128)(2,1)S(1)}, u32[]{:S(2)}, u32[]{:S(2)}) %collective-permute-start.14) | collective-permute-done | bytes 393248 | tf_op jit(solution)/shard_map/ppermute | solution.py:19
  119.8 0.8 finish.1
  (33 shorter events, 3.2 us)
Async XLA Ops:
  2.4 8.6 %collective-permute-start.1 = (bf16[1552,128]{1,0:T(8,128)(2,1)S(1)}, bf16[1552,128]{1,0:T(8,128)(2,1)S(1)}, u32[]{:S(2)}, u32[]{:S(2)}) collective-permute-start(bf16[1552,128]{1,0:T(8,128)(2,1)S(1)} %fusion.1.refs_4_.refs_7_), channel_id=1, source_target_pairs={{0,8},{8,16},{16,24},{24,32},{32,40},{40,48},{48,56},{56,64},{64,7... | collective-permute-start | bytes 1191944 | tf_op jit(solution)/shard_map/ppermute | solution.py:19
  3.7 13.8 %collective-permute-start = (bf16[1552,128]{1,0:T(8,128)(2,1)S(1)}, bf16[1552,128]{1,0:T(8,128)(2,1)S(1)}, u32[]{:S(2)}, u32[]{:S(2)}) collective-permute-start(bf16[1552,128]{1,0:T(8,128)(2,1)S(1)} %fusion.1.refs_4_.refs_7_), channel_id=1, source_target_pairs={{0,16},{8,24},{16,32},{24,40},{32,48},{40,56},{48,64},{56,72},{64,... | collective-permute-start | bytes 1191944 | tf_op jit(solution)/shard_map/ppermute | solution.py:19
  7.9 32.2 %collective-permute-start.3 = (bf16[768,512]{1,0:T(8,128)(2,1)}, bf16[768,512]{1,0:T(8,128)(2,1)}, u32[]{:S(2)}, u32[]{:S(2)}) collective-permute-start(bf16[768,512]{1,0:T(8,128)(2,1)} %refs_3_.1), channel_id=1, source_target_pairs={{0,2},{1,3},{2,0},{3,1},{4,6},{5,7},{6,4},{7,5},{8,10},{9,11},{10,... | collective-permute-start | bytes 2359304 | tf_op jit(solution)/shard_map/ppermute | solution.py:24
  17.5 22.6 %collective-permute-start.2 = (bf16[768,512]{1,0:T(8,128)(2,1)}, bf16[768,512]{1,0:T(8,128)(2,1)}, u32[]{:S(2)}, u32[]{:S(2)}) collective-permute-start(bf16[768,512]{1,0:T(8,128)(2,1)} %refs_3_.1), channel_id=1, source_target_pairs={{0,4},{1,5},{2,6},{3,7},{4,0},{5,1},{6,2},{7,3},{8,12},{9,13},{10,... | collective-permute-start | bytes 2359304 | tf_op jit(solution)/shard_map/ppermute | solution.py:28
  22.8 27.8 %collective-permute-start.8 = (bf16[768,512]{1,0:T(8,128)(2,1)}, bf16[768,512]{1,0:T(8,128)(2,1)S(1)}, u32[]{:S(2)}, u32[]{:S(2)}) collective-permute-start(bf16[768,512]{1,0:T(8,128)(2,1)} %refs_3_.1), channel_id=1, source_target_pairs={{0,3},{1,0},{2,1},{3,2},{4,7},{5,4},{6,5},{7,6},{8,11},{9,8},{10,9... | collective-permute-start | bytes 2359304 | tf_op jit(solution)/shard_map/ppermute | solution.py:24
  25.6 25.3 %collective-permute-start.7 = (bf16[768,512]{1,0:T(8,128)(2,1)}, bf16[768,512]{1,0:T(8,128)(2,1)S(1)}, u32[]{:S(2)}, u32[]{:S(2)}) collective-permute-start(bf16[768,512]{1,0:T(8,128)(2,1)} %refs_3_.1), channel_id=1, source_target_pairs={{0,1},{1,2},{2,3},{3,0},{4,5},{5,6},{6,7},{7,4},{8,9},{9,10},{10,1... | collective-permute-start | bytes 2359304 | tf_op jit(solution)/shard_map/ppermute | solution.py:24
  25.7 1.1 copy-start
  40.1 28.3 %collective-permute-start.5 = (bf16[768,512]{1,0:T(8,128)(2,1)}, bf16[768,512]{1,0:T(8,128)(2,1)}, u32[]{:S(2)}, u32[]{:S(2)}) collective-permute-start(bf16[768,512]{1,0:T(8,128)(2,1)} %collective-permute-done.2.refs_5_), channel_id=1, source_target_pairs={{0,3},{1,0},{2,1},{3,2},{4,7},{5,4},{6,5},{7,6},{8,11},{9,8},{10,9... | collective-permute-start | bytes 2359304 | tf_op jit(solution)/shard_map/ppermute | solution.py:24
  43.4 25.0 %collective-permute-start.4 = (bf16[768,512]{1,0:T(8,128)(2,1)}, bf16[768,512]{1,0:T(8,128)(2,1)}, u32[]{:S(2)}, u32[]{:S(2)}) collective-permute-start(bf16[768,512]{1,0:T(8,128)(2,1)} %collective-permute-done.2.refs_5_), channel_id=1, source_target_pairs={{0,1},{1,2},{2,3},{3,0},{4,5},{5,6},{6,7},{7,4},{8,9},{9,10},{10,1... | collective-permute-start | bytes 2359304 | tf_op jit(solution)/shard_map/ppermute | solution.py:24
  43.4 22.0 %collective-permute-start.10 = (bf16[768,512]{1,0:T(8,128)(2,1)}, bf16[768,512]{1,0:T(8,128)(2,1)}, u32[]{:S(2)}, u32[]{:S(2)}) collective-permute-start(bf16[768,512]{1,0:T(8,128)(2,1)} %collective-permute-done.3.refs_4_), channel_id=1, source_target_pairs={{0,4},{1,5},{2,6},{3,7},{4,0},{5,1},{6,2},{7,3},{8,12},{9,13},{10,... | collective-permute-start | bytes 2359304 | tf_op jit(solution)/shard_map/ppermute | solution.py:28
  49.7 0.9 copy-start.1
  50.7 0.9 copy-start.3
  50.7 17.8 %collective-permute-start.6 = (bf16[3,512,256]{2,1,0:T(8,128)(2,1)S(1)}, bf16[3,512,256]{2,1,0:T(8,128)(2,1)}, u32[]{:S(2)}, u32[]{:S(2)}) collective-permute-start(bf16[3,512,256]{2,1,0:T(8,128)(2,1)S(1)} %get-tuple-element.43), channel_id=1, source_target_pairs={{0,8},{8,0},{16,24},{24,16},{32,40},{40,32},{48,56},{56,48},{64,72... | collective-permute-start | bytes 2359304 | tf_op jit(solution)/shard_map/ppermute | solution.py:32
  51.5 0.9 copy-start.4
  57.4 0.8 copy-start.2
  58.2 10.2 %collective-permute-start.9 = (bf16[2,512,256]{2,1,0:T(8,128)(2,1)}, bf16[2,512,256]{2,1,0:T(8,128)(2,1)}, u32[]{:S(2)}, u32[]{:S(2)}) collective-permute-start(bf16[2,512,256]{2,1,0:T(8,128)(2,1)} %get-tuple-element.47), channel_id=1, source_target_pairs={{0,8},{8,0},{16,24},{24,16},{32,40},{40,32},{48,56},{56,48},{64,72... | collective-permute-start | bytes 1572872 | tf_op jit(solution)/shard_map/ppermute | solution.py:32
  73.9 2.4 %collective-permute-start.11 = (bf16[2,512,256]{2,1,0:T(8,128)(2,1)S(1)}, bf16[2,512,256]{2,1,0:T(8,128)(2,1)S(1)}, u32[]{:S(2)}, u32[]{:S(2)}) collective-permute-start(bf16[2,512,256]{2,1,0:T(8,128)(2,1)S(1)} %get-tuple-element.51), channel_id=1, source_target_pairs={{0,8},{8,0},{16,24},{24,16},{32,40},{40,32},{48,56},{56,48},{64,72... | collective-permute-start | bytes 1572872 | tf_op jit(solution)/shard_map/ppermute | solution.py:32
  74.0 2.3 %collective-permute-start.12 = (bf16[1,512,256]{2,1,0:T(8,128)(2,1)S(1)}, bf16[1,512,256]{2,1,0:T(8,128)(2,1)S(1)}, u32[]{:S(2)}, u32[]{:S(2)}) collective-permute-start(bf16[1,512,256]{2,1,0:T(8,128)(2,1)S(1)} %get-tuple-element.53), channel_id=1, source_target_pairs={{0,8},{8,0},{16,24},{24,16},{32,40},{40,32},{48,56},{56,48},{64,72... | collective-permute-start | bytes 786440 | tf_op jit(solution)/shard_map/ppermute | solution.py:32
  77.8 36.0 %all-to-all-start = ((bf16[8,512,256]{2,1,0:T(8,128)(2,1)}), bf16[8,512,256]{2,1,0:T(8,128)(2,1)}, u32[]{:S(2)}, u32[]{:S(2)}) async-start(bf16[8,512,256]{2,1,0:T(8,128)(2,1)} %place.1), calls=%async_computation | async-start | bytes 4194304 | tf_op jit(solution)/shard_map/all_to_all | solution.py:415
  94.6 1.8 %collective-permute-start.13 = (bf16[1536,128]{1,0:T(8,128)(2,1)S(1)}, bf16[1536,128]{1,0:T(8,128)(2,1)S(1)}, u32[]{:S(2)}, u32[]{:S(2)}) collective-permute-start(bf16[1536,128]{1,0:T(8,128)(2,1)S(1)} %get-tuple-element.65), channel_id=1, source_target_pairs={{0,8},{8,0},{16,24},{24,16},{32,40},{40,32},{48,56},{56,48},{64,72... | collective-permute-start | bytes 1179656 | tf_op jit(solution)/shard_map/ppermute | solution.py:32
  96.5 23.3 %collective-permute-start.14 = (bf16[1536,128]{1,0:T(8,128)(2,1)S(1)}, bf16[1536,128]{1,0:T(8,128)(2,1)S(1)}, u32[]{:S(2)}, u32[]{:S(2)}) collective-permute-start(bf16[1536,128]{1,0:T(8,128)(2,1)S(1)} %send.1), channel_id=1, source_target_pairs={{16,0},{24,8},{32,16},{40,24},{48,32},{56,40},{64,48},{72,56},{80,... | collective-permute-start | bytes 1179656 | tf_op jit(solution)/shard_map/ppermute | solution.py:19

commit v7 on v6

--- a/solution.py
+++ b/solution.py
@@ -9,6 +9,7 @@
 
 HEAD_SIZE = 128
 NEG_BIG = -1e30
+DOCS = 8
 ROWS = 256
 VMEM_BYTES = 20 << 20
 
@@ -52,7 +53,7 @@
 
 
 def forward_kernel(
-    tok, span, heads, low_ref, q_ref, far_ref, near_ref, own_ref,
+    tok, span, heads, shard_ref, doc_ref, q_ref, far_ref, near_ref, own_ref,
     expo_ref, attn_ref, turned_ref, inverse_ref, key_all, value_all, bias,
 ):
     @pl.when(pl.program_id(0) == 0)
@@ -63,7 +64,21 @@
     window = pl.ds(begin, span)
     key_at = lax.broadcasted_iota(jnp.int32, (ROWS, span), 1)
     row_at = lax.broadcasted_iota(jnp.int32, (ROWS, 1), 0)
-    visible = (key_at >= low_ref[...] - begin) & (key_at <= row_at + 2 * tok)
+    doc_rows = pl.ds(2 * tok, 16)
+    used = lax.broadcasted_iota(jnp.int32, (16, HEAD_SIZE), 0) < tok // HEAD_SIZE
+    docs = [
+        jnp.where(shard_ref[0] >= hop, part[doc_rows, :].astype(jnp.float32), -1.0)
+        for part, hop in ((far_ref, 2), (near_ref, 1), (own_ref, 0))
+    ]
+    first = jnp.zeros((ROWS, 1), jnp.float32)
+    for doc in range(1, DOCS):
+        before = sum(jnp.where(used & (part < doc), 1.0, 0.0) for part in docs)
+        before = jnp.sum(jnp.sum(before, axis=0, keepdims=True), axis=1, keepdims=True)
+        first = jnp.where(doc_ref[...] == doc, before, first)
+    none = sum(jnp.where(used & (part < 0), 1.0, 0.0) for part in docs)
+    none = jnp.sum(jnp.sum(none, axis=0, keepdims=True), axis=1, keepdims=True)
+    first = jnp.where(doc_ref[...] == 0, none, first).astype(jnp.int32)
+    visible = (key_at >= jnp.maximum(first - begin, row_at + 1)) & (key_at <= row_at + 2 * tok)
     bias[...] = jnp.where(visible, 0.0, NEG_BIG)
     for head in range(heads):
         columns = slice(head * HEAD_SIZE, (head + 1) * HEAD_SIZE)
@@ -334,13 +349,6 @@
     docs = jnp.pad(doc_ids.astype(jnp.bfloat16).reshape(tok // HEAD_SIZE, HEAD_SIZE), ((0, 16 - tok // HEAD_SIZE), (0, 0)))
     own = jnp.concatenate([keys, values, docs], axis=0)
     far, near = shifted(own, "seq", 2), shifted(own, "seq", 1)
-    doc_of = lambda part: part[2 * tok : 2 * tok + tok // HEAD_SIZE].reshape(tok).astype(jnp.int32)
-    doc_keys = jnp.concatenate([
-        jnp.where(shard >= 2, doc_of(far), -1), jnp.where(shard >= 1, doc_of(near), -1), doc_ids
-    ])
-    earlier = jnp.sum((doc_keys[None, :] < doc_ids[:, None]).astype(jnp.int32), axis=1)
-    low = jnp.maximum(earlier, jnp.arange(tok, dtype=jnp.int32) + 1)[:, None]
-
     all_heads = heads * HEAD_SIZE
     row_block = pl.BlockSpec((ROWS, all_heads), lambda b: (b, 0))
     held = [pltpu.VMEM((3 * tok, HEAD_SIZE), jnp.bfloat16)] * 2
@@ -349,7 +357,8 @@
     expo, attn, turned, inverse = pl.pallas_call(
         lambda *refs: forward_kernel(tok, span, heads, *refs),
         grid=(blocks,),
-        in_specs=[pl.BlockSpec((ROWS, 1), lambda b: (b, 0)), row_block, whole(), whole(), whole()],
+        in_specs=[pl.BlockSpec(memory_space=pltpu.SMEM), pl.BlockSpec((ROWS, 1), lambda b: (b, 0)), row_block]
+        + [whole()] * 3,
         out_specs=[
             pl.BlockSpec((heads, ROWS, span), lambda b: (0, b, 0)), row_block,
             pl.BlockSpec((all_heads, ROWS), lambda b: (0, b)), row_block,
@@ -362,7 +371,7 @@
         compiler_params=pltpu.CompilerParams(vmem_limit_bytes=VMEM_BYTES),
         cost_estimate=pl.CostEstimate(flops=2 * work, bytes_accessed=14 << 20, transcendentals=heads * tok * span),
         name="forward",
-    )(low, queries, far, near, own)
+    )(shard[None].astype(jnp.int32), doc_ids[:, None], queries, far, near, own)
     expo, attn, inverse, queries = in_hbm(expo), in_hbm(attn), in_hbm(inverse), in_hbm(queries)
 
     tensor = lax.axis_index("tensor")
@@ -373,7 +382,8 @@
     where = lambda some: jnp.stack([core, *some]).astype(jnp.int32)
     opposite = step_x(out_grad, 2)
     across = step_y(lax.optimization_barrier((out_grad, far, near))[0])
-    later, low = lax.optimization_barrier((out_grad, low))
+    landed = far[:16] + near[:16]
+    later = lax.optimization_barrier((out_grad, landed))[0]
     near_up, near_down = step_x(later, 1), step_x(later, -1)
     across, opposite, turned = lax.optimization_barrier((across, opposite, turned))
     across_up, across_down = step_x(across, 1), step_x(across, -1)

time: 121 us -> 120 us (level)
  other arithmetic: 7.08 us -> 4.69 us
  waiting for transfers between devices: 28.8 us -> 27.5 us
    reduce_sum x1 -> x0, other arithmetic: 1.52 us -> none  [local(): jnp.sum((doc_keys[None, :] < doc_ids[:, None]).astype(jnp.int32), axis=1)]
    ppermute x2, starting transfers between devices: 4.07 us -> 5.52 us  [step_y(): return lax.ppermute(value, 'tensor', [(t, t ^ 4) for t in range(8)])]
  transfers between devices with their start and end apart: 16 -> 16, of which waited for: 6 -> 7; matrix products, arithmetic and copies ran while one was open for 4% -> 3% of each run, Pallas kernels for 35% -> 36%
where the time goes in v7:
time: 120 us; the launch traced here: 119 us
  Pallas kernels  50.7 us (42%)
  starting transfers between devices  30.2 us (25%)
  waiting for transfers between devices  27.5 us (23%)
  local copies, waits for them, and re-layouts  5.22 us (4%)
  other arithmetic  4.69 us (4%)
    pallas_call x4, Pallas kernels, project(): pl.pallas_call(lambda *refs: project_kernel(sources, shapes, groups, *ref...  18.6 us
    pallas_call x1, Pallas kernels, local(): pl.pallas_call(lambda *refs: forward_kernel(tok, span, heads, *refs), gri...  13.4 us
    ppermute x3, waiting for transfers between devices, shifted(): lax.ppermute(value, axis, [(source, source + steps) for source in range(i...  9.85 us
    pallas_call x1, Pallas kernels, local(): pl.pallas_call(lambda *refs: backward_past_kernel(tok, heads, *refs), gri...  9.24 us
    ppermute x5, starting transfers between devices, step_x(): return lax.ppermute(value, 'tensor', pairs)  8.91 us
    all_to_all x1, waiting for transfers between devices, local(): arrived = lax.all_to_all(placed, 'seq', 0, 0, axis_index_groups=groups)  8.75 us
    all_to_all x1, starting transfers between devices, local(): arrived = lax.all_to_all(placed, 'seq', 0, 0, axis_index_groups=groups)  7.52 us
    pallas_call x1, Pallas kernels, local(): pl.pallas_call(lambda *refs: backward_own_kernel(tok, heads, *refs), grid...  7.07 us
  transfers between devices with their start and end apart: 16, of which 7 were waited for; matrix products, arithmetic and copies ran while one was open for 3% of the time, Pallas kernels for 36%

profile of v7, /device:TPU:0, one launch (start us, length us, event | category | flops | bytes accessed | tf_op | source)
XLA Modules:
  0.0 119.2 jit_solution(11061334046332738760)
XLA Ops:
  0.6 0.7 convert_bitcast_fusion
  1.3 1.0 fusion.1.refs_5_.refs_7_
  2.4 1.3 %collective-permute-start.1 = (bf16[1552,128]{1,0:T(8,128)(2,1)S(1)}, bf16[1552,128]{1,0:T(8,128)(2,1)S(1)}, u32[]{:S(2)}, u32[]{:S(2)}) collective-permute-start(bf16[1552,128]{1,0:T(8,128)(2,1)S(1)} %fusion.1.refs_5_.refs_7_), channel_id=1, source_target_pairs={{0,8},{8,16},{16,24},{24,32},{32,40},{40,48},{48,56},{56,64},{64,7... | collective-permute-start | bytes 1191944 | tf_op jit(solution)/shard_map/ppermute | solution.py:20
  3.7 4.2 %collective-permute-start = (bf16[1552,128]{1,0:T(8,128)(2,1)S(1)}, bf16[1552,128]{1,0:T(8,128)(2,1)S(1)}, u32[]{:S(2)}, u32[]{:S(2)}) collective-permute-start(bf16[1552,128]{1,0:T(8,128)(2,1)S(1)} %fusion.1.refs_5_.refs_7_), channel_id=1, source_target_pairs={{0,16},{8,24},{16,32},{24,40},{32,48},{40,56},{48,64},{56,72},{64,... | collective-permute-start | bytes 1191944 | tf_op jit(solution)/shard_map/ppermute | solution.py:20
  7.9 3.1 %collective-permute-start.3 = (bf16[768,512]{1,0:T(8,128)(2,1)}, bf16[768,512]{1,0:T(8,128)(2,1)}, u32[]{:S(2)}, u32[]{:S(2)}) collective-permute-start(bf16[768,512]{1,0:T(8,128)(2,1)} %refs_3_.1), channel_id=1, source_target_pairs={{0,2},{1,3},{2,0},{3,1},{4,6},{5,7},{6,4},{7,5},{8,10},{9,11},{10,... | collective-permute-start | bytes 2359304 | tf_op jit(solution)/shard_map/ppermute | solution.py:25
  11.0 6.5 %collective-permute-done.refs_3_.refs_5_ = bf16[1552,128]{1,0:T(8,128)(2,1)S(1)} collective-permute-done((bf16[1552,128]{1,0:T(8,128)(2,1)S(1)}, bf16[1552,128]{1,0:T(8,128)(2,1)S(1)}, u32[]{:S(2)}, u32[]{:S(2)}) %collective-permute-start) | collective-permute-done | bytes 397344 | tf_op jit(solution)/shard_map/ppermute | solution.py:20
  17.5 2.9 %collective-permute-start.2 = (bf16[768,512]{1,0:T(8,128)(2,1)}, bf16[768,512]{1,0:T(8,128)(2,1)}, u32[]{:S(2)}, u32[]{:S(2)}) collective-permute-start(bf16[768,512]{1,0:T(8,128)(2,1)} %refs_3_.1), channel_id=1, source_target_pairs={{0,4},{1,5},{2,6},{3,7},{4,0},{5,1},{6,2},{7,3},{8,12},{9,13},{10,... | collective-permute-start | bytes 2359304 | tf_op jit(solution)/shard_map/ppermute | solution.py:29
  20.4 2.8 %collective-permute-start.8 = (bf16[768,512]{1,0:T(8,128)(2,1)}, bf16[768,512]{1,0:T(8,128)(2,1)S(1)}, u32[]{:S(2)}, u32[]{:S(2)}) collective-permute-start(bf16[768,512]{1,0:T(8,128)(2,1)} %refs_3_.1), channel_id=1, source_target_pairs={{0,3},{1,0},{2,1},{3,2},{4,7},{5,4},{6,5},{7,6},{8,11},{9,8},{10,9... | collective-permute-start | bytes 2359304 | tf_op jit(solution)/shard_map/ppermute | solution.py:25
  23.2 0.8 broadcast_in_dim.10.refs_1_
  24.2 1.1 copy-done
  25.3 13.4 %forward.1 = (bf16[4,768,1792]{2,1,0:T(8,128)(2,1)}, bf16[768,512]{1,0:T(8,128)(2,1)}, bf16[512,768]{1,0:T(8,128)(2,1)}, f32[768,512]{1,0:T(8,128)}) custom-call(s32[1]{0:T(128)} %bitcast.10.refs_0_, s32[768,1]{1,0:T(8,128)S(1)} %broadcast_in_dim.10.refs_1_, bf16[768,512]{1,0:T(8,128)(2,1)S(1)} %copy-done, ...), custom_call_target="tpu_custom_call" | custom-call | flops 2818572288 | bytes 14680064 | tf_op jit(solution)/shard_map/forward/pallas_call | solution.py:357
  38.9 3.0 %collective-permute-start.5 = (bf16[768,512]{1,0:T(8,128)(2,1)}, bf16[768,512]{1,0:T(8,128)(2,1)}, u32[]{:S(2)}, u32[]{:S(2)}) collective-permute-start(bf16[768,512]{1,0:T(8,128)(2,1)} %collective-permute-done.2.refs_5_), channel_id=1, source_target_pairs={{0,3},{1,0},{2,1},{3,2},{4,7},{5,4},{6,5},{7,6},{8,11},{9,8},{10,9... | collective-permute-start | bytes 2359304 | tf_op jit(solution)/shard_map/ppermute | solution.py:25
  42.0 2.6 %collective-permute-start.10 = (bf16[768,512]{1,0:T(8,128)(2,1)}, bf16[768,512]{1,0:T(8,128)(2,1)}, u32[]{:S(2)}, u32[]{:S(2)}) collective-permute-start(bf16[768,512]{1,0:T(8,128)(2,1)} %collective-permute-done.3.refs_4_), channel_id=1, source_target_pairs={{0,4},{1,5},{2,6},{3,7},{4,0},{5,1},{6,2},{7,3},{8,12},{9,13},{10,... | collective-permute-start | bytes 2359304 | tf_op jit(solution)/shard_map/ppermute | solution.py:29
  44.6 5.1 %project.4 = (f32[768,512]{1,0:T(8,128)S(1)}, bf16[3,512,256]{2,1,0:T(8,128)(2,1)S(1)}, bf16[3,512,256]{2,1,0:T(8,128)(2,1)S(1)}) custom-call(s32[4]{0:T(128)S(1)} %pad_add_fusion.1.refs_0_, bf16[512,4096]{1,0:T(8,128)(2,1)} %refs_1_.7, bf16[512,768]{1,0:T(8,128)(2,1)} %get-tuple-element.38.refs_2_, bf16[768,512]{1,0:T(8,128)(2,1)} %refs_3_.1, ...), custom_call_target="tpu_custom_call" | custom-call | flops 2415919104 | bytes 1048576 | tf_op jit(solution)/shard_map/project/pallas_call | solution.py:289
  49.7 0.9 copy-done.1
  51.6 0.9 copy-done.4
  52.5 5.0 %project.5 = (f32[768,512]{1,0:T(8,128)S(1)}, bf16[2,512,256]{2,1,0:T(8,128)(2,1)S(1)}, bf16[2,512,256]{2,1,0:T(8,128)(2,1)}) custom-call(s32[3]{0:T(128)S(1)} %pad_add_fusion.2.refs_0_, bf16[512,4096]{1,0:T(8,128)(2,1)} %refs_1_.7, bf16[512,768]{1,0:T(8,128)(2,1)} %get-tuple-element.38.refs_2_, bf16[768,512]{1,0:T(8,128)(2,1)} %copy-done.4, ...), custom_call_target="tpu_custom_call" | custom-call | flops 1610612736 | bytes 1048576 | tf_op jit(solution)/shard_map/project/pallas_call | solution.py:289
  57.5 0.8 copy-done.2
  58.7 5.3 %collective-permute-done.10.refs_3_ = bf16[768,512]{1,0:T(8,128)(2,1)} collective-permute-done((bf16[768,512]{1,0:T(8,128)(2,1)}, bf16[768,512]{1,0:T(8,128)(2,1)}, u32[]{:S(2)}, u32[]{:S(2)}) %collective-permute-start.10) | collective-permute-done | bytes 786464 | tf_op jit(solution)/shard_map/ppermute | solution.py:29
  63.9 3.1 %project.6 = (f32[768,512]{1,0:T(8,128)S(1)}, bf16[1,512,256]{2,1,0:T(8,128)(2,1)S(1)}, bf16[1,512,256]{2,1,0:T(8,128)(2,1)S(1)}) custom-call(s32[2]{0:T(128)S(1)} %pad_add_fusion.3.refs_0_, bf16[512,4096]{1,0:T(8,128)(2,1)} %refs_1_.7, bf16[512,768]{1,0:T(8,128)(2,1)} %get-tuple-element.38.refs_2_, bf16[768,512]{1,0:T(8,128)(2,1)} %collective-permute-done.10.refs_3_, ...), custom_call_target="tpu_custom_call" | custom-call | flops 805306368 | bytes 1048576 | tf_op jit(solution)/shard_map/project/pallas_call | solution.py:289
  67.0 5.4 %project.7 = (bf16[768,512]{1,0:T(8,128)(2,1)S(1)}, bf16[2,512,256]{2,1,0:T(8,128)(2,1)S(1)}, bf16[2,512,256]{2,1,0:T(8,128)(2,1)S(1)}, bf16[8,512,256]{2,1,0:T(8,128)(2,1)}) custom-call(s32[8]{0:T(128)S(1)} %stack.63.refs_0_, bf16[512,4096]{1,0:T(8,128)(2,1)} %refs_1_.7, bf16[512,768]{1,0:T(8,128)(2,1)} %get-tuple-element.38.refs_2_, ...), custom_call_target="tpu_custom_call" | custom-call | flops 1048576 | bytes 1048576 | tf_op jit(solution)/shard_map/project/pallas_call | solution.py:289
  73.1 1.7 %collective-permute-done.12.last_come_ref = bf16[1,512,256]{2,1,0:T(8,128)(2,1)S(1)} collective-permute-done((bf16[1,512,256]{2,1,0:T(8,128)(2,1)S(1)}, bf16[1,512,256]{2,1,0:T(8,128)(2,1)S(1)}, u32[]{:S(2)}, u32[]{:S(2)}) %collective-permute-start.12) | collective-permute-done | bytes 262176 | tf_op jit(solution)/shard_map/ppermute | solution.py:33
  74.8 1.5 %place.1 = bf16[8,512,256]{2,1,0:T(8,128)(2,1)} custom-call(s32[3]{0:T(128)S(1)} %pad_add_fusion.where_ref, bf16[2,512,256]{2,1,0:T(8,128)(2,1)S(1)} %get-tuple-element.48.mine_ref, bf16[2,512,256]{2,1,0:T(8,128)(2,1)S(1)} %collective-permute-done.11.come_ref, ...), custom_call_target="tpu_custom_call", output_to_operand_aliasing={{}: (5, {})} | custom-call | flops 1048576 | bytes 1048576 | tf_op jit(solution)/shard_map/place/pallas_call | solution.py:412
  76.4 7.5 %all-to-all-start = ((bf16[8,512,256]{2,1,0:T(8,128)(2,1)}), bf16[8,512,256]{2,1,0:T(8,128)(2,1)}, u32[]{:S(2)}, u32[]{:S(2)}) async-start(bf16[8,512,256]{2,1,0:T(8,128)(2,1)} %place.1), calls=%async_computation | async-start | bytes 4194304 | tf_op jit(solution)/shard_map/all_to_all | solution.py:425
  83.9 9.2 %backward_past.1 = (f32[768,512]{1,0:T(8,128)S(1)}, bf16[1536,128]{1,0:T(8,128)(2,1)S(1)}, bf16[1536,128]{1,0:T(8,128)(2,1)S(1)}) custom-call(bf16[768,512]{1,0:T(8,128)(2,1)} %refs_0_.3, bf16[768,512]{1,0:T(8,128)(2,1)S(1)} %get-tuple-element.54.refs_1_, bf16[768,512]{1,0:T(8,128)(2,1)} %get-tuple-element.55.refs_2_, f32[768,512]{1,0:T(8,128)} %get-tuple-element.56.refs_3_, ...), custom_call_target="tpu_custom_call" | custom-call | flops 1048576 | bytes 1048576 | tf_op jit(solution)/shard_map/backward_past/pallas_call | solution.py:430
  93.2 1.7 %collective-permute-done.13.crossed_ref = bf16[1536,128]{1,0:T(8,128)(2,1)S(1)} collective-permute-done((bf16[1536,128]{1,0:T(8,128)(2,1)S(1)}, bf16[1536,128]{1,0:T(8,128)(2,1)S(1)}, u32[]{:S(2)}, u32[]{:S(2)}) %collective-permute-start.13) | collective-permute-done | bytes 393248 | tf_op jit(solution)/shard_map/ppermute | solution.py:33
  95.0 1.5 %collective-permute-start.14 = (bf16[1536,128]{1,0:T(8,128)(2,1)S(1)}, bf16[1536,128]{1,0:T(8,128)(2,1)S(1)}, u32[]{:S(2)}, u32[]{:S(2)}) collective-permute-start(bf16[1536,128]{1,0:T(8,128)(2,1)S(1)} %send.1), channel_id=1, source_target_pairs={{16,0},{24,8},{32,16},{40,24},{48,32},{56,40},{64,48},{72,56},{80,... | collective-permute-start | bytes 1179656 | tf_op jit(solution)/shard_map/ppermute | solution.py:20
  96.6 7.1 %backward_own.1 = (bf16[768,512]{1,0:T(8,128)(2,1)}, f32[1536,128]{1,0:T(8,128)S(1)}) custom-call(bf16[768,512]{1,0:T(8,128)(2,1)} %refs_0_.3, bf16[768,512]{1,0:T(8,128)(2,1)S(1)} %get-tuple-element.54.refs_1_, bf16[768,512]{1,0:T(8,128)(2,1)} %get-tuple-element.55.refs_2_, f32[768,512]{1,0:T(8,128)} %get-tuple-element.56.refs_3_, ...), custom_call_target="tpu_custom_call" | custom-call | flops 1048576 | bytes 1048576 | tf_op jit(solution)/shard_map/backward_own/pallas_call | solution.py:445
  103.6 8.7 %all-to-all-done = bf16[8,512,256]{2,1,0:T(8,128)(2,1)} async-done(((bf16[8,512,256]{2,1,0:T(8,128)(2,1)}), bf16[8,512,256]{2,1,0:T(8,128)(2,1)}, u32[]{:S(2)}, u32[]{:S(2)}) %all-to-all-start) | async-done | bytes 2097184 | tf_op jit(solution)/shard_map/all_to_all | solution.py:425
  112.4 2.6 %reduce_sum.12 = bf16[512,256]{1,0:T(8,128)(2,1)} reduce(bf16[8,512,256]{2,1,0:T(8,128)(2,1)} %all-to-all-done, bf16[]{:T(256)} %constant.73.clone.1), dimensions={0}, to_apply=%region_0.1 | reduce | flops 917504 | bytes 2359298 | tf_op jit(solution)/shard_map/reduce_sum | solution.py:426
  115.0 3.3 %collective-permute-done.14.come_ref = bf16[1536,128]{1,0:T(8,128)(2,1)S(1)} collective-permute-done((bf16[1536,128]{1,0:T(8,128)(2,1)S(1)}, bf16[1536,128]{1,0:T(8,128)(2,1)S(1)}, u32[]{:S(2)}, u32[]{:S(2)}) %collective-permute-start.14) | collective-permute-done | bytes 393248 | tf_op jit(solution)/shard_map/ppermute | solution.py:20
  118.4 0.8 finish.1
  (29 shorter events, 2.6 us)
Async XLA Ops:
  2.4 8.6 %collective-permute-start.1 = (bf16[1552,128]{1,0:T(8,128)(2,1)S(1)}, bf16[1552,128]{1,0:T(8,128)(2,1)S(1)}, u32[]{:S(2)}, u32[]{:S(2)}) collective-permute-start(bf16[1552,128]{1,0:T(8,128)(2,1)S(1)} %fusion.1.refs_5_.refs_7_), channel_id=1, source_target_pairs={{0,8},{8,16},{16,24},{24,32},{32,40},{40,48},{48,56},{56,64},{64,7... | collective-permute-start | bytes 1191944 | tf_op jit(solution)/shard_map/ppermute | solution.py:20
  3.7 13.8 %collective-permute-start = (bf16[1552,128]{1,0:T(8,128)(2,1)S(1)}, bf16[1552,128]{1,0:T(8,128)(2,1)S(1)}, u32[]{:S(2)}, u32[]{:S(2)}) collective-permute-start(bf16[1552,128]{1,0:T(8,128)(2,1)S(1)} %fusion.1.refs_5_.refs_7_), channel_id=1, source_target_pairs={{0,16},{8,24},{16,32},{24,40},{32,48},{40,56},{48,64},{56,72},{64,... | collective-permute-start | bytes 1191944 | tf_op jit(solution)/shard_map/ppermute | solution.py:20
  7.9 30.8 %collective-permute-start.3 = (bf16[768,512]{1,0:T(8,128)(2,1)}, bf16[768,512]{1,0:T(8,128)(2,1)}, u32[]{:S(2)}, u32[]{:S(2)}) collective-permute-start(bf16[768,512]{1,0:T(8,128)(2,1)} %refs_3_.1), channel_id=1, source_target_pairs={{0,2},{1,3},{2,0},{3,1},{4,6},{5,7},{6,4},{7,5},{8,10},{9,11},{10,... | collective-permute-start | bytes 2359304 | tf_op jit(solution)/shard_map/ppermute | solution.py:25
  17.5 21.4 %collective-permute-start.2 = (bf16[768,512]{1,0:T(8,128)(2,1)}, bf16[768,512]{1,0:T(8,128)(2,1)}, u32[]{:S(2)}, u32[]{:S(2)}) collective-permute-start(bf16[768,512]{1,0:T(8,128)(2,1)} %refs_3_.1), channel_id=1, source_target_pairs={{0,4},{1,5},{2,6},{3,7},{4,0},{5,1},{6,2},{7,3},{8,12},{9,13},{10,... | collective-permute-start | bytes 2359304 | tf_op jit(solution)/shard_map/ppermute | solution.py:29
  20.4 30.2 %collective-permute-start.8 = (bf16[768,512]{1,0:T(8,128)(2,1)}, bf16[768,512]{1,0:T(8,128)(2,1)S(1)}, u32[]{:S(2)}, u32[]{:S(2)}) collective-permute-start(bf16[768,512]{1,0:T(8,128)(2,1)} %refs_3_.1), channel_id=1, source_target_pairs={{0,3},{1,0},{2,1},{3,2},{4,7},{5,4},{6,5},{7,6},{8,11},{9,8},{10,9... | collective-permute-start | bytes 2359304 | tf_op jit(solution)/shard_map/ppermute | solution.py:25
  23.2 27.8 %collective-permute-start.7 = (bf16[768,512]{1,0:T(8,128)(2,1)}, bf16[768,512]{1,0:T(8,128)(2,1)S(1)}, u32[]{:S(2)}, u32[]{:S(2)}) collective-permute-start(bf16[768,512]{1,0:T(8,128)(2,1)} %refs_3_.1), channel_id=1, source_target_pairs={{0,1},{1,2},{2,3},{3,0},{4,5},{5,6},{6,7},{7,4},{8,9},{9,10},{10,1... | collective-permute-start | bytes 2359304 | tf_op jit(solution)/shard_map/ppermute | solution.py:25
  24.2 1.1 copy-start
  38.9 28.1 %collective-permute-start.5 = (bf16[768,512]{1,0:T(8,128)(2,1)}, bf16[768,512]{1,0:T(8,128)(2,1)}, u32[]{:S(2)}, u32[]{:S(2)}) collective-permute-start(bf16[768,512]{1,0:T(8,128)(2,1)} %collective-permute-done.2.refs_5_), channel_id=1, source_target_pairs={{0,3},{1,0},{2,1},{3,2},{4,7},{5,4},{6,5},{7,6},{8,11},{9,8},{10,9... | collective-permute-start | bytes 2359304 | tf_op jit(solution)/shard_map/ppermute | solution.py:25
  42.0 25.0 %collective-permute-start.4 = (bf16[768,512]{1,0:T(8,128)(2,1)}, bf16[768,512]{1,0:T(8,128)(2,1)}, u32[]{:S(2)}, u32[]{:S(2)}) collective-permute-start(bf16[768,512]{1,0:T(8,128)(2,1)} %collective-permute-done.2.refs_5_), channel_id=1, source_target_pairs={{0,1},{1,2},{2,3},{3,0},{4,5},{5,6},{6,7},{7,4},{8,9},{9,10},{10,1... | collective-permute-start | bytes 2359304 | tf_op jit(solution)/shard_map/ppermute | solution.py:25
  42.0 22.0 %collective-permute-start.10 = (bf16[768,512]{1,0:T(8,128)(2,1)}, bf16[768,512]{1,0:T(8,128)(2,1)}, u32[]{:S(2)}, u32[]{:S(2)}) collective-permute-start(bf16[768,512]{1,0:T(8,128)(2,1)} %collective-permute-done.3.refs_4_), channel_id=1, source_target_pairs={{0,4},{1,5},{2,6},{3,7},{4,0},{5,1},{6,2},{7,3},{8,12},{9,13},{10,... | collective-permute-start | bytes 2359304 | tf_op jit(solution)/shard_map/ppermute | solution.py:29
  49.7 0.9 copy-start.1
  50.7 0.9 copy-start.3
  50.7 16.4 %collective-permute-start.6 = (bf16[3,512,256]{2,1,0:T(8,128)(2,1)S(1)}, bf16[3,512,256]{2,1,0:T(8,128)(2,1)}, u32[]{:S(2)}, u32[]{:S(2)}) collective-permute-start(bf16[3,512,256]{2,1,0:T(8,128)(2,1)S(1)} %get-tuple-element.42), channel_id=1, source_target_pairs={{0,8},{8,0},{16,24},{24,16},{32,40},{40,32},{48,56},{56,48},{64,72... | collective-permute-start | bytes 2359304 | tf_op jit(solution)/shard_map/ppermute | solution.py:33
  51.6 0.9 copy-start.4
  57.5 0.8 copy-start.2
  58.3 8.7 %collective-permute-start.9 = (bf16[2,512,256]{2,1,0:T(8,128)(2,1)}, bf16[2,512,256]{2,1,0:T(8,128)(2,1)}, u32[]{:S(2)}, u32[]{:S(2)}) collective-permute-start(bf16[2,512,256]{2,1,0:T(8,128)(2,1)} %get-tuple-element.45), channel_id=1, source_target_pairs={{0,8},{8,0},{16,24},{24,16},{32,40},{40,32},{48,56},{56,48},{64,72... | collective-permute-start | bytes 1572872 | tf_op jit(solution)/shard_map/ppermute | solution.py:33
  72.4 2.4 %collective-permute-start.11 = (bf16[2,512,256]{2,1,0:T(8,128)(2,1)S(1)}, bf16[2,512,256]{2,1,0:T(8,128)(2,1)S(1)}, u32[]{:S(2)}, u32[]{:S(2)}) collective-permute-start(bf16[2,512,256]{2,1,0:T(8,128)(2,1)S(1)} %get-tuple-element.49), channel_id=1, source_target_pairs={{0,8},{8,0},{16,24},{24,16},{32,40},{40,32},{48,56},{56,48},{64,72... | collective-permute-start | bytes 1572872 | tf_op jit(solution)/shard_map/ppermute | solution.py:33
  72.5 2.3 %collective-permute-start.12 = (bf16[1,512,256]{2,1,0:T(8,128)(2,1)S(1)}, bf16[1,512,256]{2,1,0:T(8,128)(2,1)S(1)}, u32[]{:S(2)}, u32[]{:S(2)}) collective-permute-start(bf16[1,512,256]{2,1,0:T(8,128)(2,1)S(1)} %get-tuple-element.51), channel_id=1, source_target_pairs={{0,8},{8,0},{16,24},{24,16},{32,40},{40,32},{48,56},{56,48},{64,72... | collective-permute-start | bytes 786440 | tf_op jit(solution)/shard_map/ppermute | solution.py:33
  76.4 36.0 %all-to-all-start = ((bf16[8,512,256]{2,1,0:T(8,128)(2,1)}), bf16[8,512,256]{2,1,0:T(8,128)(2,1)}, u32[]{:S(2)}, u32[]{:S(2)}) async-start(bf16[8,512,256]{2,1,0:T(8,128)(2,1)} %place.1), calls=%async_computation | async-start | bytes 4194304 | tf_op jit(solution)/shard_map/all_to_all | solution.py:425
  93.1 1.8 %collective-permute-start.13 = (bf16[1536,128]{1,0:T(8,128)(2,1)S(1)}, bf16[1536,128]{1,0:T(8,128)(2,1)S(1)}, u32[]{:S(2)}, u32[]{:S(2)}) collective-permute-start(bf16[1536,128]{1,0:T(8,128)(2,1)S(1)} %get-tuple-element.63), channel_id=1, source_target_pairs={{0,8},{8,0},{16,24},{24,16},{32,40},{40,32},{48,56},{56,48},{64,72... | collective-permute-start | bytes 1179656 | tf_op jit(solution)/shard_map/ppermute | solution.py:33
  95.0 23.3 %collective-permute-start.14 = (bf16[1536,128]{1,0:T(8,128)(2,1)S(1)}, bf16[1536,128]{1,0:T(8,128)(2,1)S(1)}, u32[]{:S(2)}, u32[]{:S(2)}) collective-permute-start(bf16[1536,128]{1,0:T(8,128)(2,1)S(1)} %send.1), channel_id=1, source_target_pairs={{16,0},{24,8},{32,16},{40,24},{48,32},{56,40},{64,48},{72,56},{80,... | collective-permute-start | bytes 1179656 | tf_op jit(solution)/shard_map/ppermute | solution.py:20

commit v8 on v7

--- a/solution.py
+++ b/solution.py
@@ -401,7 +401,7 @@
     )
     come_b = step_core(other_b)
     total, mine_d, other_d = project(
-        [((0, 0, 0, tok),)], False, real(1), where(places[7:]), weight, turned, (last,), (total,),
+        [((0, 0, 0, tok),)], False, 4 * real(1), where(places[7:]), weight, turned, (last,), (total,),
     )
     come_d = step_core(other_d)
     attention_gradient, mine_c, other_c, placed = project(

time: 120 us -> 118 us (0.983)
    ppermute x2, waiting for transfers between devices: 5.53 us -> 2.73 us  [step_y(): return lax.ppermute(value, 'tensor', [(t, t ^ 4) for t in range(8)])]
    ppermute x5, waiting for transfers between devices: 0.01 us -> 1.69 us  [step_x(): return lax.ppermute(value, 'tensor', pairs)]
  transfers between devices with their start and end apart: 16 -> 16, of which waited for: 7 -> 8; matrix products, arithmetic and copies ran while one was open for 3% -> 3% of each run, Pallas kernels for 36% -> 36%
where the time goes in v8:
time: 118 us
  Pallas kernels  50.7 us (43%)
  starting transfers between devices  30.1 us (26%)
  waiting for transfers between devices  26.4 us (22%)
  local copies, waits for them, and re-layouts  5.21 us (4%)
  other arithmetic  4.69 us (4%)
    pallas_call x4, Pallas kernels, project(): pl.pallas_call(lambda *refs: project_kernel(sources, shapes, groups, *ref...  18.6 us
    pallas_call x1, Pallas kernels, local(): pl.pallas_call(lambda *refs: forward_kernel(tok, span, heads, *refs), gri...  13.4 us
    ppermute x3, waiting for transfers between devices, shifted(): lax.ppermute(value, axis, [(source, source + steps) for source in range(i...  9.85 us
    pallas_call x1, Pallas kernels, local(): pl.pallas_call(lambda *refs: backward_past_kernel(tok, heads, *refs), gri...  9.24 us
    all_to_all x1, waiting for transfers between devices, local(): arrived = lax.all_to_all(placed, 'seq', 0, 0, axis_index_groups=groups)  8.75 us
    ppermute x5, starting transfers between devices, step_x(): return lax.ppermute(value, 'tensor', pairs)  8.63 us
    all_to_all x1, starting transfers between devices, local(): arrived = lax.all_to_all(placed, 'seq', 0, 0, axis_index_groups=groups)  7.43 us
    pallas_call x1, Pallas kernels, local(): pl.pallas_call(lambda *refs: backward_own_kernel(tok, heads, *refs), grid...  7.07 us
  transfers between devices with their start and end apart: 16, of which 8 were waited for; matrix products, arithmetic and copies ran while one was open for 3% of the time, Pallas kernels for 36%

profile of v8, /device:TPU:0, one launch (start us, length us, event | category | flops | bytes accessed | tf_op | source)
XLA Modules:
  0.0 118.0 jit_solution(1961428342856266137)
XLA Ops:
  1.3 1.0 fusion.1.refs_5_.refs_7_
  2.4 1.3 %collective-permute-start.1 = (bf16[1552,128]{1,0:T(8,128)(2,1)S(1)}, bf16[1552,128]{1,0:T(8,128)(2,1)S(1)}, u32[]{:S(2)}, u32[]{:S(2)}) collective-permute-start(bf16[1552,128]{1,0:T(8,128)(2,1)S(1)} %fusion.1.refs_5_.refs_7_), channel_id=1, source_target_pairs={{0,8},{8,16},{16,24},{24,32},{32,40},{40,48},{48,56},{56,64},{64,7... | collective-permute-start | bytes 1191944 | tf_op jit(solution)/shard_map/ppermute | solution.py:20
  3.7 4.2 %collective-permute-start = (bf16[1552,128]{1,0:T(8,128)(2,1)S(1)}, bf16[1552,128]{1,0:T(8,128)(2,1)S(1)}, u32[]{:S(2)}, u32[]{:S(2)}) collective-permute-start(bf16[1552,128]{1,0:T(8,128)(2,1)S(1)} %fusion.1.refs_5_.refs_7_), channel_id=1, source_target_pairs={{0,16},{8,24},{16,32},{24,40},{32,48},{40,56},{48,64},{56,72},{64,... | collective-permute-start | bytes 1191944 | tf_op jit(solution)/shard_map/ppermute | solution.py:20
  7.9 3.1 %collective-permute-start.3 = (bf16[768,512]{1,0:T(8,128)(2,1)}, bf16[768,512]{1,0:T(8,128)(2,1)}, u32[]{:S(2)}, u32[]{:S(2)}) collective-permute-start(bf16[768,512]{1,0:T(8,128)(2,1)} %refs_3_.1), channel_id=1, source_target_pairs={{0,2},{1,3},{2,0},{3,1},{4,6},{5,7},{6,4},{7,5},{8,10},{9,11},{10,... | collective-permute-start | bytes 2359304 | tf_op jit(solution)/shard_map/ppermute | solution.py:25
  11.0 6.5 %collective-permute-done.refs_3_.refs_5_ = bf16[1552,128]{1,0:T(8,128)(2,1)S(1)} collective-permute-done((bf16[1552,128]{1,0:T(8,128)(2,1)S(1)}, bf16[1552,128]{1,0:T(8,128)(2,1)S(1)}, u32[]{:S(2)}, u32[]{:S(2)}) %collective-permute-start) | collective-permute-done | bytes 397344 | tf_op jit(solution)/shard_map/ppermute | solution.py:20
  17.5 2.9 %collective-permute-start.2 = (bf16[768,512]{1,0:T(8,128)(2,1)}, bf16[768,512]{1,0:T(8,128)(2,1)}, u32[]{:S(2)}, u32[]{:S(2)}) collective-permute-start(bf16[768,512]{1,0:T(8,128)(2,1)} %refs_3_.1), channel_id=1, source_target_pairs={{0,4},{1,5},{2,6},{3,7},{4,0},{5,1},{6,2},{7,3},{8,12},{9,13},{10,... | collective-permute-start | bytes 2359304 | tf_op jit(solution)/shard_map/ppermute | solution.py:29
  20.4 2.8 %collective-permute-start.8 = (bf16[768,512]{1,0:T(8,128)(2,1)}, bf16[768,512]{1,0:T(8,128)(2,1)S(1)}, u32[]{:S(2)}, u32[]{:S(2)}) collective-permute-start(bf16[768,512]{1,0:T(8,128)(2,1)} %refs_3_.1), channel_id=1, source_target_pairs={{0,3},{1,0},{2,1},{3,2},{4,7},{5,4},{6,5},{7,6},{8,11},{9,8},{10,9... | collective-permute-start | bytes 2359304 | tf_op jit(solution)/shard_map/ppermute | solution.py:25
  23.2 0.8 broadcast_in_dim.10.refs_1_
  24.1 1.1 copy-done
  25.2 13.4 %forward.1 = (bf16[4,768,1792]{2,1,0:T(8,128)(2,1)}, bf16[768,512]{1,0:T(8,128)(2,1)}, bf16[512,768]{1,0:T(8,128)(2,1)}, f32[768,512]{1,0:T(8,128)}) custom-call(s32[1]{0:T(128)} %bitcast.10.refs_0_, s32[768,1]{1,0:T(8,128)S(1)} %broadcast_in_dim.10.refs_1_, bf16[768,512]{1,0:T(8,128)(2,1)S(1)} %copy-done, ...), custom_call_target="tpu_custom_call" | custom-call | flops 2818572288 | bytes 14680064 | tf_op jit(solution)/shard_map/forward/pallas_call | solution.py:357
  38.9 2.9 %collective-permute-start.10 = (bf16[768,512]{1,0:T(8,128)(2,1)}, bf16[768,512]{1,0:T(8,128)(2,1)}, u32[]{:S(2)}, u32[]{:S(2)}) collective-permute-start(bf16[768,512]{1,0:T(8,128)(2,1)} %collective-permute-done.3.refs_4_), channel_id=1, source_target_pairs={{0,4},{1,5},{2,6},{3,7},{4,0},{5,1},{6,2},{7,3},{8,12},{9,13},{10,... | collective-permute-start | bytes 2359304 | tf_op jit(solution)/shard_map/ppermute | solution.py:29
  41.9 2.8 %collective-permute-start.5 = (bf16[768,512]{1,0:T(8,128)(2,1)}, bf16[768,512]{1,0:T(8,128)(2,1)}, u32[]{:S(2)}, u32[]{:S(2)}) collective-permute-start(bf16[768,512]{1,0:T(8,128)(2,1)} %collective-permute-done.2.refs_5_), channel_id=1, source_target_pairs={{0,3},{1,0},{2,1},{3,2},{4,7},{5,4},{6,5},{7,6},{8,11},{9,8},{10,9... | collective-permute-start | bytes 2359304 | tf_op jit(solution)/shard_map/ppermute | solution.py:25
  44.7 5.1 %project.4 = (f32[768,512]{1,0:T(8,128)S(1)}, bf16[3,512,256]{2,1,0:T(8,128)(2,1)S(1)}, bf16[3,512,256]{2,1,0:T(8,128)(2,1)S(1)}) custom-call(s32[4]{0:T(128)S(1)} %pad_add_fusion.1.refs_0_, bf16[512,4096]{1,0:T(8,128)(2,1)} %refs_1_.7, bf16[512,768]{1,0:T(8,128)(2,1)} %get-tuple-element.38.refs_2_, bf16[768,512]{1,0:T(8,128)(2,1)} %refs_3_.1, ...), custom_call_target="tpu_custom_call" | custom-call | flops 2415919104 | bytes 1048576 | tf_op jit(solution)/shard_map/project/pallas_call | solution.py:289
  49.8 0.9 copy-done.1
  51.7 0.9 copy-done.4
  52.5 5.0 %project.5 = (f32[768,512]{1,0:T(8,128)S(1)}, bf16[2,512,256]{2,1,0:T(8,128)(2,1)S(1)}, bf16[2,512,256]{2,1,0:T(8,128)(2,1)}) custom-call(s32[3]{0:T(128)S(1)} %pad_add_fusion.2.refs_0_, bf16[512,4096]{1,0:T(8,128)(2,1)} %refs_1_.7, bf16[512,768]{1,0:T(8,128)(2,1)} %get-tuple-element.38.refs_2_, bf16[768,512]{1,0:T(8,128)(2,1)} %copy-done.4, ...), custom_call_target="tpu_custom_call" | custom-call | flops 1610612736 | bytes 1048576 | tf_op jit(solution)/shard_map/project/pallas_call | solution.py:289
  57.6 0.8 copy-done.2
  58.8 2.4 %collective-permute-done.10.refs_3_ = bf16[768,512]{1,0:T(8,128)(2,1)} collective-permute-done((bf16[768,512]{1,0:T(8,128)(2,1)}, bf16[768,512]{1,0:T(8,128)(2,1)}, u32[]{:S(2)}, u32[]{:S(2)}) %collective-permute-start.10) | collective-permute-done | bytes 786464 | tf_op jit(solution)/shard_map/ppermute | solution.py:29
  61.2 3.0 %project.6 = (f32[768,512]{1,0:T(8,128)S(1)}, bf16[1,512,256]{2,1,0:T(8,128)(2,1)S(1)}, bf16[1,512,256]{2,1,0:T(8,128)(2,1)S(1)}) custom-call(s32[2]{0:T(128)S(1)} %pad_add_fusion.3.refs_0_, bf16[512,4096]{1,0:T(8,128)(2,1)} %refs_1_.7, bf16[512,768]{1,0:T(8,128)(2,1)} %get-tuple-element.38.refs_2_, bf16[768,512]{1,0:T(8,128)(2,1)} %collective-permute-done.10.refs_3_, ...), custom_call_target="tpu_custom_call" | custom-call | flops 3221225472 | bytes 1048576 | tf_op jit(solution)/shard_map/project/pallas_call | solution.py:289
  64.2 1.7 %collective-permute-done.4.refs_3_ = bf16[768,512]{1,0:T(8,128)(2,1)} collective-permute-done((bf16[768,512]{1,0:T(8,128)(2,1)}, bf16[768,512]{1,0:T(8,128)(2,1)}, u32[]{:S(2)}, u32[]{:S(2)}) %collective-permute-start.4) | collective-permute-done | bytes 786464 | tf_op jit(solution)/shard_map/ppermute | solution.py:25
  65.9 5.4 %project.7 = (bf16[768,512]{1,0:T(8,128)(2,1)S(1)}, bf16[2,512,256]{2,1,0:T(8,128)(2,1)S(1)}, bf16[2,512,256]{2,1,0:T(8,128)(2,1)S(1)}, bf16[8,512,256]{2,1,0:T(8,128)(2,1)}) custom-call(s32[8]{0:T(128)S(1)} %stack.63.refs_0_, bf16[512,4096]{1,0:T(8,128)(2,1)} %refs_1_.7, bf16[512,768]{1,0:T(8,128)(2,1)} %get-tuple-element.38.refs_2_, ...), custom_call_target="tpu_custom_call" | custom-call | flops 1048576 | bytes 1048576 | tf_op jit(solution)/shard_map/project/pallas_call | solution.py:289
  72.0 1.7 %collective-permute-done.12.last_come_ref = bf16[1,512,256]{2,1,0:T(8,128)(2,1)S(1)} collective-permute-done((bf16[1,512,256]{2,1,0:T(8,128)(2,1)S(1)}, bf16[1,512,256]{2,1,0:T(8,128)(2,1)S(1)}, u32[]{:S(2)}, u32[]{:S(2)}) %collective-permute-start.12) | collective-permute-done | bytes 262176 | tf_op jit(solution)/shard_map/ppermute | solution.py:33
  73.7 1.5 %place.1 = bf16[8,512,256]{2,1,0:T(8,128)(2,1)} custom-call(s32[3]{0:T(128)S(1)} %pad_add_fusion.where_ref, bf16[2,512,256]{2,1,0:T(8,128)(2,1)S(1)} %get-tuple-element.48.mine_ref, bf16[2,512,256]{2,1,0:T(8,128)(2,1)S(1)} %collective-permute-done.11.come_ref, ...), custom_call_target="tpu_custom_call", output_to_operand_aliasing={{}: (5, {})} | custom-call | flops 1048576 | bytes 1048576 | tf_op jit(solution)/shard_map/place/pallas_call | solution.py:412
  75.2 7.4 %all-to-all-start = ((bf16[8,512,256]{2,1,0:T(8,128)(2,1)}), bf16[8,512,256]{2,1,0:T(8,128)(2,1)}, u32[]{:S(2)}, u32[]{:S(2)}) async-start(bf16[8,512,256]{2,1,0:T(8,128)(2,1)} %place.1), calls=%async_computation | async-start | bytes 4194304 | tf_op jit(solution)/shard_map/all_to_all | solution.py:425
  82.7 9.2 %backward_past.1 = (f32[768,512]{1,0:T(8,128)S(1)}, bf16[1536,128]{1,0:T(8,128)(2,1)S(1)}, bf16[1536,128]{1,0:T(8,128)(2,1)S(1)}) custom-call(bf16[768,512]{1,0:T(8,128)(2,1)} %refs_0_.3, bf16[768,512]{1,0:T(8,128)(2,1)S(1)} %get-tuple-element.54.refs_1_, bf16[768,512]{1,0:T(8,128)(2,1)} %get-tuple-element.55.refs_2_, f32[768,512]{1,0:T(8,128)} %get-tuple-element.56.refs_3_, ...), custom_call_target="tpu_custom_call" | custom-call | flops 1048576 | bytes 1048576 | tf_op jit(solution)/shard_map/backward_past/pallas_call | solution.py:430
  92.0 1.7 %collective-permute-done.13.crossed_ref = bf16[1536,128]{1,0:T(8,128)(2,1)S(1)} collective-permute-done((bf16[1536,128]{1,0:T(8,128)(2,1)S(1)}, bf16[1536,128]{1,0:T(8,128)(2,1)S(1)}, u32[]{:S(2)}, u32[]{:S(2)}) %collective-permute-start.13) | collective-permute-done | bytes 393248 | tf_op jit(solution)/shard_map/ppermute | solution.py:33
  93.8 1.5 %collective-permute-start.14 = (bf16[1536,128]{1,0:T(8,128)(2,1)S(1)}, bf16[1536,128]{1,0:T(8,128)(2,1)S(1)}, u32[]{:S(2)}, u32[]{:S(2)}) collective-permute-start(bf16[1536,128]{1,0:T(8,128)(2,1)S(1)} %send.1), channel_id=1, source_target_pairs={{16,0},{24,8},{32,16},{40,24},{48,32},{56,40},{64,48},{72,56},{80,... | collective-permute-start | bytes 1179656 | tf_op jit(solution)/shard_map/ppermute | solution.py:20
  95.3 7.1 %backward_own.1 = (bf16[768,512]{1,0:T(8,128)(2,1)}, f32[1536,128]{1,0:T(8,128)S(1)}) custom-call(bf16[768,512]{1,0:T(8,128)(2,1)} %refs_0_.3, bf16[768,512]{1,0:T(8,128)(2,1)S(1)} %get-tuple-element.54.refs_1_, bf16[768,512]{1,0:T(8,128)(2,1)} %get-tuple-element.55.refs_2_, f32[768,512]{1,0:T(8,128)} %get-tuple-element.56.refs_3_, ...), custom_call_target="tpu_custom_call" | custom-call | flops 1048576 | bytes 1048576 | tf_op jit(solution)/shard_map/backward_own/pallas_call | solution.py:445
  102.4 8.7 %all-to-all-done = bf16[8,512,256]{2,1,0:T(8,128)(2,1)} async-done(((bf16[8,512,256]{2,1,0:T(8,128)(2,1)}), bf16[8,512,256]{2,1,0:T(8,128)(2,1)}, u32[]{:S(2)}, u32[]{:S(2)}) %all-to-all-start) | async-done | bytes 2097184 | tf_op jit(solution)/shard_map/all_to_all | solution.py:425
  111.2 2.6 %reduce_sum.12 = bf16[512,256]{1,0:T(8,128)(2,1)} reduce(bf16[8,512,256]{2,1,0:T(8,128)(2,1)} %all-to-all-done, bf16[]{:T(256)} %constant.73.clone.1), dimensions={0}, to_apply=%region_0.1 | reduce | flops 917504 | bytes 2359298 | tf_op jit(solution)/shard_map/reduce_sum | solution.py:426
  113.8 3.3 %collective-permute-done.14.come_ref = bf16[1536,128]{1,0:T(8,128)(2,1)S(1)} collective-permute-done((bf16[1536,128]{1,0:T(8,128)(2,1)S(1)}, bf16[1536,128]{1,0:T(8,128)(2,1)S(1)}, u32[]{:S(2)}, u32[]{:S(2)}) %collective-permute-start.14) | collective-permute-done | bytes 393248 | tf_op jit(solution)/shard_map/ppermute | solution.py:20
  117.1 0.8 finish.1
  (29 shorter events, 3.3 us)
Async XLA Ops:
  2.4 8.6 %collective-permute-start.1 = (bf16[1552,128]{1,0:T(8,128)(2,1)S(1)}, bf16[1552,128]{1,0:T(8,128)(2,1)S(1)}, u32[]{:S(2)}, u32[]{:S(2)}) collective-permute-start(bf16[1552,128]{1,0:T(8,128)(2,1)S(1)} %fusion.1.refs_5_.refs_7_), channel_id=1, source_target_pairs={{0,8},{8,16},{16,24},{24,32},{32,40},{40,48},{48,56},{56,64},{64,7... | collective-permute-start | bytes 1191944 | tf_op jit(solution)/shard_map/ppermute | solution.py:20
  3.7 13.8 %collective-permute-start = (bf16[1552,128]{1,0:T(8,128)(2,1)S(1)}, bf16[1552,128]{1,0:T(8,128)(2,1)S(1)}, u32[]{:S(2)}, u32[]{:S(2)}) collective-permute-start(bf16[1552,128]{1,0:T(8,128)(2,1)S(1)} %fusion.1.refs_5_.refs_7_), channel_id=1, source_target_pairs={{0,16},{8,24},{16,32},{24,40},{32,48},{40,56},{48,64},{56,72},{64,... | collective-permute-start | bytes 1191944 | tf_op jit(solution)/shard_map/ppermute | solution.py:20
  7.9 30.7 %collective-permute-start.3 = (bf16[768,512]{1,0:T(8,128)(2,1)}, bf16[768,512]{1,0:T(8,128)(2,1)}, u32[]{:S(2)}, u32[]{:S(2)}) collective-permute-start(bf16[768,512]{1,0:T(8,128)(2,1)} %refs_3_.1), channel_id=1, source_target_pairs={{0,2},{1,3},{2,0},{3,1},{4,6},{5,7},{6,4},{7,5},{8,10},{9,11},{10,... | collective-permute-start | bytes 2359304 | tf_op jit(solution)/shard_map/ppermute | solution.py:25
  17.5 21.4 %collective-permute-start.2 = (bf16[768,512]{1,0:T(8,128)(2,1)}, bf16[768,512]{1,0:T(8,128)(2,1)}, u32[]{:S(2)}, u32[]{:S(2)}) collective-permute-start(bf16[768,512]{1,0:T(8,128)(2,1)} %refs_3_.1), channel_id=1, source_target_pairs={{0,4},{1,5},{2,6},{3,7},{4,0},{5,1},{6,2},{7,3},{8,12},{9,13},{10,... | collective-permute-start | bytes 2359304 | tf_op jit(solution)/shard_map/ppermute | solution.py:29
  20.4 30.3 %collective-permute-start.8 = (bf16[768,512]{1,0:T(8,128)(2,1)}, bf16[768,512]{1,0:T(8,128)(2,1)S(1)}, u32[]{:S(2)}, u32[]{:S(2)}) collective-permute-start(bf16[768,512]{1,0:T(8,128)(2,1)} %refs_3_.1), channel_id=1, source_target_pairs={{0,3},{1,0},{2,1},{3,2},{4,7},{5,4},{6,5},{7,6},{8,11},{9,8},{10,9... | collective-permute-start | bytes 2359304 | tf_op jit(solution)/shard_map/ppermute | solution.py:25
  23.2 27.9 %collective-permute-start.7 = (bf16[768,512]{1,0:T(8,128)(2,1)}, bf16[768,512]{1,0:T(8,128)(2,1)S(1)}, u32[]{:S(2)}, u32[]{:S(2)}) collective-permute-start(bf16[768,512]{1,0:T(8,128)(2,1)} %refs_3_.1), channel_id=1, source_target_pairs={{0,1},{1,2},{2,3},{3,0},{4,5},{5,6},{6,7},{7,4},{8,9},{9,10},{10,1... | collective-permute-start | bytes 2359304 | tf_op jit(solution)/shard_map/ppermute | solution.py:25
  24.1 1.1 copy-start
  38.9 22.2 %collective-permute-start.10 = (bf16[768,512]{1,0:T(8,128)(2,1)}, bf16[768,512]{1,0:T(8,128)(2,1)}, u32[]{:S(2)}, u32[]{:S(2)}) collective-permute-start(bf16[768,512]{1,0:T(8,128)(2,1)} %collective-permute-done.3.refs_4_), channel_id=1, source_target_pairs={{0,4},{1,5},{2,6},{3,7},{4,0},{5,1},{6,2},{7,3},{8,12},{9,13},{10,... | collective-permute-start | bytes 2359304 | tf_op jit(solution)/shard_map/ppermute | solution.py:29
  41.9 22.3 %collective-permute-start.5 = (bf16[768,512]{1,0:T(8,128)(2,1)}, bf16[768,512]{1,0:T(8,128)(2,1)}, u32[]{:S(2)}, u32[]{:S(2)}) collective-permute-start(bf16[768,512]{1,0:T(8,128)(2,1)} %collective-permute-done.2.refs_5_), channel_id=1, source_target_pairs={{0,3},{1,0},{2,1},{3,2},{4,7},{5,4},{6,5},{7,6},{8,11},{9,8},{10,9... | collective-permute-start | bytes 2359304 | tf_op jit(solution)/shard_map/ppermute | solution.py:25
  44.7 21.2 %collective-permute-start.4 = (bf16[768,512]{1,0:T(8,128)(2,1)}, bf16[768,512]{1,0:T(8,128)(2,1)}, u32[]{:S(2)}, u32[]{:S(2)}) collective-permute-start(bf16[768,512]{1,0:T(8,128)(2,1)} %collective-permute-done.2.refs_5_), channel_id=1, source_target_pairs={{0,1},{1,2},{2,3},{3,0},{4,5},{5,6},{6,7},{7,4},{8,9},{9,10},{10,1... | collective-permute-start | bytes 2359304 | tf_op jit(solution)/shard_map/ppermute | solution.py:25
  49.8 0.9 copy-start.1
  50.7 0.9 copy-start.3
  50.7 15.2 %collective-permute-start.6 = (bf16[3,512,256]{2,1,0:T(8,128)(2,1)S(1)}, bf16[3,512,256]{2,1,0:T(8,128)(2,1)}, u32[]{:S(2)}, u32[]{:S(2)}) collective-permute-start(bf16[3,512,256]{2,1,0:T(8,128)(2,1)S(1)} %get-tuple-element.42), channel_id=1, source_target_pairs={{0,8},{8,0},{16,24},{24,16},{32,40},{40,32},{48,56},{56,48},{64,72... | collective-permute-start | bytes 2359304 | tf_op jit(solution)/shard_map/ppermute | solution.py:33
  51.7 0.9 copy-start.4
  57.5 0.8 copy-start.2
  58.3 5.9 %collective-permute-start.9 = (bf16[2,512,256]{2,1,0:T(8,128)(2,1)}, bf16[2,512,256]{2,1,0:T(8,128)(2,1)}, u32[]{:S(2)}, u32[]{:S(2)}) collective-permute-start(bf16[2,512,256]{2,1,0:T(8,128)(2,1)} %get-tuple-element.45), channel_id=1, source_target_pairs={{0,8},{8,0},{16,24},{24,16},{32,40},{40,32},{48,56},{56,48},{64,72... | collective-permute-start | bytes 1572872 | tf_op jit(solution)/shard_map/ppermute | solution.py:33
  71.3 2.4 %collective-permute-start.11 = (bf16[2,512,256]{2,1,0:T(8,128)(2,1)S(1)}, bf16[2,512,256]{2,1,0:T(8,128)(2,1)S(1)}, u32[]{:S(2)}, u32[]{:S(2)}) collective-permute-start(bf16[2,512,256]{2,1,0:T(8,128)(2,1)S(1)} %get-tuple-element.49), channel_id=1, source_target_pairs={{0,8},{8,0},{16,24},{24,16},{32,40},{40,32},{48,56},{56,48},{64,72... | collective-permute-start | bytes 1572872 | tf_op jit(solution)/shard_map/ppermute | solution.py:33
  71.4 2.3 %collective-permute-start.12 = (bf16[1,512,256]{2,1,0:T(8,128)(2,1)S(1)}, bf16[1,512,256]{2,1,0:T(8,128)(2,1)S(1)}, u32[]{:S(2)}, u32[]{:S(2)}) collective-permute-start(bf16[1,512,256]{2,1,0:T(8,128)(2,1)S(1)} %get-tuple-element.51), channel_id=1, source_target_pairs={{0,8},{8,0},{16,24},{24,16},{32,40},{40,32},{48,56},{56,48},{64,72... | collective-permute-start | bytes 786440 | tf_op jit(solution)/shard_map/ppermute | solution.py:33
  75.2 35.9 %all-to-all-start = ((bf16[8,512,256]{2,1,0:T(8,128)(2,1)}), bf16[8,512,256]{2,1,0:T(8,128)(2,1)}, u32[]{:S(2)}, u32[]{:S(2)}) async-start(bf16[8,512,256]{2,1,0:T(8,128)(2,1)} %place.1), calls=%async_computation | async-start | bytes 4194304 | tf_op jit(solution)/shard_map/all_to_all | solution.py:425
  91.9 1.8 %collective-permute-start.13 = (bf16[1536,128]{1,0:T(8,128)(2,1)S(1)}, bf16[1536,128]{1,0:T(8,128)(2,1)S(1)}, u32[]{:S(2)}, u32[]{:S(2)}) collective-permute-start(bf16[1536,128]{1,0:T(8,128)(2,1)S(1)} %get-tuple-element.63), channel_id=1, source_target_pairs={{0,8},{8,0},{16,24},{24,16},{32,40},{40,32},{48,56},{56,48},{64,72... | collective-permute-start | bytes 1179656 | tf_op jit(solution)/shard_map/ppermute | solution.py:33
  93.8 23.3 %collective-permute-start.14 = (bf16[1536,128]{1,0:T(8,128)(2,1)S(1)}, bf16[1536,128]{1,0:T(8,128)(2,1)S(1)}, u32[]{:S(2)}, u32[]{:S(2)}) collective-permute-start(bf16[1536,128]{1,0:T(8,128)(2,1)S(1)} %send.1), channel_id=1, source_target_pairs={{16,0},{24,8},{32,16},{40,24},{48,32},{56,40},{64,48},{72,56},{80,... | collective-permute-start | bytes 1179656 | tf_op jit(solution)/shard_map/ppermute | solution.py:20

commit v9 on v8

--- a/solution.py
+++ b/solution.py
@@ -175,18 +175,21 @@
         own_out[pl.ds(tok, tok), :] = value_sum[...].T
 
 
-def project_kernel(sources, shapes, groups, where_ref, weight_ref, turned_ref, *refs):
+def project_kernel(sources, shapes, groups, with_total, with_parts, where_ref, weight_ref, turned_ref, *refs):
     count = len(shapes)
     pieces, refs = refs[:count], refs[count:]
     earlier, refs = refs[: 2 * len(groups)], refs[2 * len(groups) :]
     if groups:
         come, placed, placed_sems = refs[-3:]
         refs = refs[:-3]
-    sems, turned, weights, *buffers = refs[-3 - count :]
-    refs = refs[: -3 - count]
+    sems, turned, weights, total_sum, *buffers = refs[-4 - count :]
+    refs = refs[: -4 - count]
     if groups:
         placed_ref, refs = refs[-1], refs[:-1]
-    before, (total_ref, mine_ref, other_ref) = refs[:-3], refs[-3:]
+    if with_parts:
+        refs, (mine_ref, other_ref) = refs[:-2], refs[-2:]
+    if with_total:
+        before, total_ref = refs[:-1], refs[-1]
     width = weights.shape[1]
     cut = width // 2
     copies = []
@@ -200,11 +203,12 @@
     turned_copy = None
     for index, blocks in enumerate(sources):
         columns = pl.ds(pl.multiple_of(where_ref[1 + index] * width, width), width)
-        pending["weight", index] = fetch(weight_ref.at[:, columns], weights.at[index])
+        if with_total:
+            pending["weight", index] = fetch(weight_ref.at[:, columns], weights.at[index])
         for operand, _, _, _ in blocks:
             if ("piece", operand) not in pending:
                 pending["piece", operand] = fetch(pieces[operand], buffers[operand])
-        if turned_copy is None:
+        if with_parts and turned_copy is None:
             turned_copy = fetch(turned_ref, turned)
     pending["turned"] = turned_copy
     at, loads = 0, []
@@ -222,19 +226,24 @@
 
     mine = pl.multiple_of(where_ref[0] * cut, cut)
     other = pl.multiple_of((1 - where_ref[0]) * cut, cut)
-    total = before[0] if before else total_ref
     for index, blocks in enumerate(sources):
-        ready(("weight", index))
         for operand, _, _, _ in blocks:
             ready(("piece", operand))
-        weight = weights[index]
-        for operand, there, row, rows in blocks:
-            term = contract_last(buffers[operand][pl.ds(there, rows), :], weight)
-            at = pl.ds(row, rows)
-            if before or index:
-                term = total[at, :] + term
-            total_ref[at, :] = term.astype(total_ref.dtype)
-        total = total_ref
+        if with_total:
+            ready(("weight", index))
+            for operand, there, row, rows in blocks:
+                term = contract_last(buffers[operand][pl.ds(there, rows), :], weights[index])
+                at = pl.ds(row, rows)
+                if index:
+                    term = total_sum[at, :] + term
+                elif before:
+                    term = before[0][at, :] + term
+                if index == len(sources) - 1:
+                    total_ref[at, :] = term.astype(total_ref.dtype)
+                else:
+                    total_sum[at, :] = term
+        if not with_parts:
+            continue
         ready("turned")
         for out, begin in ((mine_ref, mine), (other_ref, other)):
             part = None
@@ -267,7 +276,7 @@
     return pl.BlockSpec(memory_space=pltpu.HBM)
 
 
-def project(sources, last, flops, where, weight, turned, pieces, before, earlier=()):
+def project(sources, last, flops, where, weight, turned, pieces, before, earlier=(), with_total=True, with_parts=True):
     width, tok = turned.shape
     count = len(sources)
     parts = jax.ShapeDtypeStruct((count, width, width // 2), jnp.bfloat16)
@@ -276,18 +285,19 @@
     shapes = [piece.shape for piece in pieces]
     groups = [part.shape[0] for part in earlier[::2]]
     slots = (sum(groups), width, width // 2)
-    out_specs = [whole()] * 3
-    out_shape = [jax.ShapeDtypeStruct((tok, width), jnp.bfloat16 if last else jnp.float32), parts, parts]
+    out_shape = [jax.ShapeDtypeStruct((tok, width), jnp.bfloat16 if last else jnp.float32)] * with_total
+    out_shape += [parts, parts] * with_parts
+    out_specs = [whole()] * len(out_shape)
     scratch = [
         pltpu.SemaphoreType.DMA((count + len(pieces) + 1,)), pltpu.VMEM((width, tok), jnp.bfloat16),
-        pltpu.VMEM((count, width, width), jnp.bfloat16),
+        pltpu.VMEM((count, width, width), jnp.bfloat16), pltpu.VMEM((tok, width), jnp.float32),
     ] + [pltpu.VMEM(shape, jnp.bfloat16) for shape in shapes]
     if groups:
         out_specs.append(hbm())
         out_shape.append(pltpu.HBM((8,) + slots[1:], jnp.bfloat16))
         scratch += [pltpu.VMEM(slots, jnp.bfloat16)] * 2 + [pltpu.SemaphoreType.DMA((2 * len(groups) + slots[0],))]
     return pl.pallas_call(
-        lambda *refs: project_kernel(sources, shapes, groups, *refs),
+        lambda *refs: project_kernel(sources, shapes, groups, with_total, with_parts, *refs),
         in_specs=[pl.BlockSpec(memory_space=pltpu.SMEM)] + [hbm()] * (2 + len(pieces) + len(earlier)) + [whole()] * len(before),
         out_specs=out_specs,
         scratch_shapes=scratch,
@@ -400,13 +410,18 @@
         where(places[3:5]), weight, turned, (near_up, near_down), (total,),
     )
     come_b = step_core(other_b)
-    total, mine_d, other_d = project(
-        [((0, 0, 0, tok),)], False, 4 * real(1), where(places[7:]), weight, turned, (last,), (total,),
+    mine_d, other_d = project(
+        [((0, 0, 0, tok),)], False, 4 * real(1), where(places[7:]), weight, turned, (last,), (), with_total=False,
     )
     come_d = step_core(other_d)
-    attention_gradient, mine_c, other_c, placed = project(
-        [((p, 0, 0, tok),) for p in range(2)], True, 1 << 20, where(places[5:7] + places[:5]), weight, turned,
-        (across_up, across_down), (total,), (mine_a, come_a, mine_b, come_b),
+    across_up, across_down, mine_d = lax.optimization_barrier((across_up, across_down, mine_d))
+    mine_c, other_c, placed = project(
+        [((p, 0, 0, tok),) for p in range(2)], False, 1 << 20, where(places[5:7] + places[:5]), weight, turned,
+        (across_up, across_down), (), (mine_a, come_a, mine_b, come_b), with_total=False,
+    )
+    (attention_gradient,) = project(
+        [((p, 0, 0, tok),) for p in range(3)], True, 1 << 20, where([places[7], *places[5:7]]), weight, turned,
+        (last, across_up, across_down), (total,), with_parts=False,
     )
     come_c = step_core(other_c)
     placed = pl.pallas_call(
@@ -420,7 +435,7 @@
         cost_estimate=pl.CostEstimate(flops=1 << 20, bytes_accessed=1 << 20, transcendentals=0),
         name="place",
     )(jnp.stack(places[5:]).astype(jnp.int32), mine_c, come_c, mine_d, come_d, placed)
-    placed, attention_gradient = lax.optimization_barrier((placed, attention_gradient))
+    placed, queries = lax.optimization_barrier((placed, queries))
     groups = [[2 * chip + c for chip in range(8)] for c in range(2)]
     arrived = lax.all_to_all(placed, "seq", 0, 0, axis_index_groups=groups)
     weight_grad = jnp.sum(arrived.astype(jnp.float32), axis=0).astype(jnp.bfloat16)

time: 118 us -> 115 us (0.975)
  waiting for transfers between devices: 26.4 us -> 21.3 us
  Pallas kernels: 50.7 us -> 53.2 us
  local copies, waits for them, and re-layouts: 5.21 us -> 3.78 us
    all_to_all x1, waiting for transfers between devices: 8.75 us -> 5.07 us  [local(): arrived = lax.all_to_all(placed, 'seq', 0, 0, axis_index_groups=groups)]
    ppermute x5, starting transfers between devices: 1.2 us -> 3.8 us  [step_core(): return lax.ppermute(value, 'seq', [(s, s ^ 1) for s in range(16)])]
    pallas_call x4 -> x5, Pallas kernels: 18.6 us -> 21 us  [project(): pl.pallas_call(lambda *refs: project_kernel(sources, shapes, groups, with...]
    ppermute x5, waiting for transfers between devices: 1.69 us -> 4.03 us  [step_x(): return lax.ppermute(value, 'tensor', pairs)]
    ppermute x2, waiting for transfers between devices: 2.73 us -> 0.47 us  [step_y(): return lax.ppermute(value, 'tensor', [(t, t ^ 4) for t in range(8)])]
    ppermute x2, starting transfers between devices: 5.8 us -> 3.61 us  [step_y(): return lax.ppermute(value, 'tensor', [(t, t ^ 4) for t in range(8)])]
    ppermute x3, waiting for transfers between devices: 9.85 us -> 8.31 us  [shifted(): lax.ppermute(value, axis, [(source, source + steps) for source in range(i...]
    unnamed x10 -> x8, local copies, waits for them, and re-layouts: 4.28 us -> 2.86 us
  transfers between devices with their start and end apart: 16 -> 16, of which waited for: 8 -> 7; matrix products, arithmetic and copies ran while one was open for 3% -> 3% of each run, Pallas kernels for 36% -> 40%
where the time goes in v9:
time: 115 us; the launch traced here: 114 us
  Pallas kernels  53.2 us (46%)
  starting transfers between devices  30.3 us (26%)
  waiting for transfers between devices  21.3 us (19%)
  other arithmetic  4.77 us (4%)
  local copies, waits for them, and re-layouts  3.78 us (3%)
    pallas_call x5, Pallas kernels, project(): pl.pallas_call(lambda *refs: project_kernel(sources, shapes, groups, with...  21 us
    pallas_call x1, Pallas kernels, local(): pl.pallas_call(lambda *refs: forward_kernel(tok, span, heads, *refs), gri...  13.4 us
    ppermute x5, starting transfers between devices, step_x(): return lax.ppermute(value, 'tensor', pairs)  9.58 us
    pallas_call x1, Pallas kernels, local(): pl.pallas_call(lambda *refs: backward_past_kernel(tok, heads, *refs), gri...  9.25 us
    ppermute x3, waiting for transfers between devices, shifted(): lax.ppermute(value, axis, [(source, source + steps) for source in range(i...  8.31 us
    pallas_call x1, Pallas kernels, local(): pl.pallas_call(lambda *refs: backward_own_kernel(tok, heads, *refs), grid...  7.07 us
    all_to_all x1, starting transfers between devices, local(): arrived = lax.all_to_all(placed, 'seq', 0, 0, axis_index_groups=groups)  6.75 us
    ppermute x3, starting transfers between devices, shifted(): lax.ppermute(value, axis, [(source, source + steps) for source in range(i...  6.58 us
  transfers between devices with their start and end apart: 16, of which 7 were waited for; matrix products, arithmetic and copies ran while one was open for 3% of the time, Pallas kernels for 40%

profile of v9, /device:TPU:0, one launch (start us, length us, event | category | flops | bytes accessed | tf_op | source)
XLA Modules:
  0.0 114.2 jit_solution(2470732723311878740)
XLA Ops:
  1.3 1.0 fusion.1.refs_5_.refs_7_
  2.4 3.6 %collective-permute-start = (bf16[1552,128]{1,0:T(8,128)(2,1)S(1)}, bf16[1552,128]{1,0:T(8,128)(2,1)S(1)}, u32[]{:S(2)}, u32[]{:S(2)}) collective-permute-start(bf16[1552,128]{1,0:T(8,128)(2,1)S(1)} %fusion.1.refs_5_.refs_7_), channel_id=1, source_target_pairs={{0,16},{8,24},{16,32},{24,40},{32,48},{40,56},{48,64},{56,72},{64,... | collective-permute-start | bytes 1191944 | tf_op jit(solution)/shard_map/ppermute | solution.py:20
  6.0 1.5 %collective-permute-start.1 = (bf16[1552,128]{1,0:T(8,128)(2,1)S(1)}, bf16[1552,128]{1,0:T(8,128)(2,1)S(1)}, u32[]{:S(2)}, u32[]{:S(2)}) collective-permute-start(bf16[1552,128]{1,0:T(8,128)(2,1)S(1)} %fusion.1.refs_5_.refs_7_), channel_id=1, source_target_pairs={{0,8},{8,16},{16,24},{24,32},{32,40},{40,48},{48,56},{56,64},{64,7... | collective-permute-start | bytes 1191944 | tf_op jit(solution)/shard_map/ppermute | solution.py:20
  7.5 3.1 %collective-permute-start.3 = (bf16[768,512]{1,0:T(8,128)(2,1)}, bf16[768,512]{1,0:T(8,128)(2,1)}, u32[]{:S(2)}, u32[]{:S(2)}) collective-permute-start(bf16[768,512]{1,0:T(8,128)(2,1)} %refs_3_.1), channel_id=1, source_target_pairs={{0,2},{1,3},{2,0},{3,1},{4,6},{5,7},{6,4},{7,5},{8,10},{9,11},{10,... | collective-permute-start | bytes 2359304 | tf_op jit(solution)/shard_map/ppermute | solution.py:25
  10.6 5.0 %collective-permute-done.refs_3_.refs_5_ = bf16[1552,128]{1,0:T(8,128)(2,1)S(1)} collective-permute-done((bf16[1552,128]{1,0:T(8,128)(2,1)S(1)}, bf16[1552,128]{1,0:T(8,128)(2,1)S(1)}, u32[]{:S(2)}, u32[]{:S(2)}) %collective-permute-start) | collective-permute-done | bytes 397344 | tf_op jit(solution)/shard_map/ppermute | solution.py:20
  15.5 2.9 %collective-permute-start.2 = (bf16[768,512]{1,0:T(8,128)(2,1)}, bf16[768,512]{1,0:T(8,128)(2,1)}, u32[]{:S(2)}, u32[]{:S(2)}) collective-permute-start(bf16[768,512]{1,0:T(8,128)(2,1)} %refs_3_.1), channel_id=1, source_target_pairs={{0,4},{1,5},{2,6},{3,7},{4,0},{5,1},{6,2},{7,3},{8,12},{9,13},{10,... | collective-permute-start | bytes 2359304 | tf_op jit(solution)/shard_map/ppermute | solution.py:29
  18.4 1.5 %collective-permute-start.8 = (bf16[768,512]{1,0:T(8,128)(2,1)}, bf16[768,512]{1,0:T(8,128)(2,1)S(1)}, u32[]{:S(2)}, u32[]{:S(2)}) collective-permute-start(bf16[768,512]{1,0:T(8,128)(2,1)} %refs_3_.1), channel_id=1, source_target_pairs={{0,1},{1,2},{2,3},{3,0},{4,5},{5,6},{6,7},{7,4},{8,9},{9,10},{10,1... | collective-permute-start | bytes 2359304 | tf_op jit(solution)/shard_map/ppermute | solution.py:25
  19.9 1.7 %collective-permute-start.9 = (bf16[768,512]{1,0:T(8,128)(2,1)}, bf16[768,512]{1,0:T(8,128)(2,1)}, u32[]{:S(2)}, u32[]{:S(2)}) collective-permute-start(bf16[768,512]{1,0:T(8,128)(2,1)} %refs_3_.1), channel_id=1, source_target_pairs={{0,3},{1,0},{2,1},{3,2},{4,7},{5,4},{6,5},{7,6},{8,11},{9,8},{10,9... | collective-permute-start | bytes 2359304 | tf_op jit(solution)/shard_map/ppermute | solution.py:25
  21.7 0.8 broadcast_in_dim.10.refs_1_
  22.6 1.1 copy-done
  23.7 13.4 %forward.1 = (bf16[4,768,1792]{2,1,0:T(8,128)(2,1)}, bf16[768,512]{1,0:T(8,128)(2,1)}, bf16[512,768]{1,0:T(8,128)(2,1)}, f32[768,512]{1,0:T(8,128)}) custom-call(s32[1]{0:T(128)} %bitcast.10.refs_0_, s32[768,1]{1,0:T(8,128)S(1)} %broadcast_in_dim.10.refs_1_, bf16[768,512]{1,0:T(8,128)(2,1)S(1)} %copy-done, ...), custom_call_target="tpu_custom_call" | custom-call | flops 2818572288 | bytes 14680064 | tf_op jit(solution)/shard_map/forward/pallas_call | solution.py:367
  37.9 0.9 collective-permute-start.4
  38.8 2.3 %collective-permute-start.5 = (bf16[768,512]{1,0:T(8,128)(2,1)}, bf16[768,512]{1,0:T(8,128)(2,1)}, u32[]{:S(2)}, u32[]{:S(2)}) collective-permute-start(bf16[768,512]{1,0:T(8,128)(2,1)} %collective-permute-done.2.refs_5_), channel_id=1, source_target_pairs={{0,3},{1,0},{2,1},{3,2},{4,7},{5,4},{6,5},{7,6},{8,11},{9,8},{10,9... | collective-permute-start | bytes 2359304 | tf_op jit(solution)/shard_map/ppermute | solution.py:25
  41.1 5.1 %project.6 = (f32[768,512]{1,0:T(8,128)S(1)}, bf16[3,512,256]{2,1,0:T(8,128)(2,1)S(1)}, bf16[3,512,256]{2,1,0:T(8,128)(2,1)S(1)}) custom-call(s32[4]{0:T(128)S(1)} %pad_add_fusion.2.refs_0_, bf16[512,4096]{1,0:T(8,128)(2,1)} %refs_1_.9, bf16[512,768]{1,0:T(8,128)(2,1)} %get-tuple-element.39.refs_2_, bf16[768,512]{1,0:T(8,128)(2,1)} %refs_3_.1, ...), custom_call_target="tpu_custom_call" | custom-call | flops 2415919104 | bytes 1048576 | tf_op jit(solution)/shard_map/project/pallas_call | solution.py:299
  46.3 0.9 copy-done.1
  47.2 2.3 %collective-permute-start.7 = (bf16[3,512,256]{2,1,0:T(8,128)(2,1)S(1)}, bf16[3,512,256]{2,1,0:T(8,128)(2,1)}, u32[]{:S(2)}, u32[]{:S(2)}) collective-permute-start(bf16[3,512,256]{2,1,0:T(8,128)(2,1)S(1)} %get-tuple-element.46), channel_id=1, source_target_pairs={{0,8},{8,0},{16,24},{24,16},{32,40},{40,32},{48,56},{56,48},{64,72... | collective-permute-start | bytes 2359304 | tf_op jit(solution)/shard_map/ppermute | solution.py:33
  49.6 5.0 %project.7 = (f32[768,512]{1,0:T(8,128)S(1)}, bf16[2,512,256]{2,1,0:T(8,128)(2,1)S(1)}, bf16[2,512,256]{2,1,0:T(8,128)(2,1)}) custom-call(s32[3]{0:T(128)S(1)} %pad_add_fusion.3.refs_0_, bf16[512,4096]{1,0:T(8,128)(2,1)} %refs_1_.9, bf16[512,768]{1,0:T(8,128)(2,1)} %get-tuple-element.39.refs_2_, bf16[768,512]{1,0:T(8,128)(2,1)} %copy-done.3, ...), custom_call_target="tpu_custom_call" | custom-call | flops 1610612736 | bytes 1048576 | tf_op jit(solution)/shard_map/project/pallas_call | solution.py:299
  56.8 2.5 %project.5 = (bf16[1,512,256]{2,1,0:T(8,128)(2,1)S(1)}, bf16[1,512,256]{2,1,0:T(8,128)(2,1)S(1)}) custom-call(s32[2]{0:T(128)S(1)} %pad_add_fusion.1.refs_0_, bf16[512,4096]{1,0:T(8,128)(2,1)} %refs_1_.9, bf16[512,768]{1,0:T(8,128)(2,1)} %get-tuple-element.39.refs_2_, bf16[768,512]{1,0:T(8,128)(2,1)} %collective-permute-done.6.refs_3_), custom_call_target="tpu_custom_call" | custom-call | flops 3221225472 | bytes 1048576 | tf_op jit(solution)/shard_map/project/pallas_call | solution.py:299
  59.4 4.0 %collective-permute-done.4.refs_3_.refs_4_ = bf16[768,512]{1,0:T(8,128)(2,1)} collective-permute-done((bf16[768,512]{1,0:T(8,128)(2,1)}, bf16[768,512]{1,0:T(8,128)(2,1)}, u32[]{:S(2)}, u32[]{:S(2)}) %collective-permute-start.4) | collective-permute-done | bytes 786464 | tf_op jit(solution)/shard_map/ppermute | solution.py:25
  63.4 4.8 %project.8 = (bf16[2,512,256]{2,1,0:T(8,128)(2,1)S(1)}, bf16[2,512,256]{2,1,0:T(8,128)(2,1)S(1)}, bf16[8,512,256]{2,1,0:T(8,128)(2,1)}) custom-call(s32[8]{0:T(128)S(1)} %stack.70.refs_0_, bf16[512,4096]{1,0:T(8,128)(2,1)} %refs_1_.9, bf16[512,768]{1,0:T(8,128)(2,1)} %get-tuple-element.39.refs_2_, bf16[768,512]{1,0:T(8,128)(2,1)} %collective-permute-done.4.refs_3_.refs_4_, ...), custom_call_target="tpu_custom_call" | custom-call | flops 1048576 | bytes 1048576 | tf_op jit(solution)/shard_map/project/pallas_call | solution.py:299
  68.9 1.7 %collective-permute-done.12.last_come_ref = bf16[1,512,256]{2,1,0:T(8,128)(2,1)S(1)} collective-permute-done((bf16[1,512,256]{2,1,0:T(8,128)(2,1)S(1)}, bf16[1,512,256]{2,1,0:T(8,128)(2,1)S(1)}, u32[]{:S(2)}, u32[]{:S(2)}) %collective-permute-start.12) | collective-permute-done | bytes 262176 | tf_op jit(solution)/shard_map/ppermute | solution.py:33
  70.6 1.5 %place.1 = bf16[8,512,256]{2,1,0:T(8,128)(2,1)} custom-call(s32[3]{0:T(128)S(1)} %pad_add_fusion.where_ref, bf16[2,512,256]{2,1,0:T(8,128)(2,1)S(1)} %get-tuple-element.50.mine_ref, bf16[2,512,256]{2,1,0:T(8,128)(2,1)S(1)} %collective-permute-done.11.come_ref, ...), custom_call_target="tpu_custom_call", output_to_operand_aliasing={{}: (5, {})} | custom-call | flops 1048576 | bytes 1048576 | tf_op jit(solution)/shard_map/place/pallas_call | solution.py:427
  72.1 6.7 %all-to-all-start = ((bf16[8,512,256]{2,1,0:T(8,128)(2,1)}), bf16[8,512,256]{2,1,0:T(8,128)(2,1)}, u32[]{:S(2)}, u32[]{:S(2)}) async-start(bf16[8,512,256]{2,1,0:T(8,128)(2,1)} %place.1), calls=%async_computation | async-start | bytes 4194304 | tf_op jit(solution)/shard_map/all_to_all | solution.py:440
  78.9 3.6 %project.9.refs_1_ = bf16[768,512]{1,0:T(8,128)(2,1)S(1)} custom-call(s32[4]{0:T(128)S(1)} %pad_add_fusion.4.refs_0_, bf16[512,4096]{1,0:T(8,128)(2,1)} %refs_1_.9, bf16[512,768]{1,0:T(8,128)(2,1)} %get-tuple-element.39.refs_2_, bf16[768,512]{1,0:T(8,128)(2,1)} %collective-permute-done.6.refs_3_, bf16[768,512]{1,0:T(8,128)(2,1)} %collective-permute-done.4.refs_3_.refs_4_, ...), custom_call_target="tpu_custom_call" | custom-call | flops 1048576 | bytes 1048576 | tf_op jit(solution)/shard_map/project/pallas_call | solution.py:299
  82.5 9.2 %backward_past.1 = (f32[768,512]{1,0:T(8,128)S(1)}, bf16[1536,128]{1,0:T(8,128)(2,1)S(1)}, bf16[1536,128]{1,0:T(8,128)(2,1)S(1)}) custom-call(bf16[768,512]{1,0:T(8,128)(2,1)} %refs_0_.1, bf16[768,512]{1,0:T(8,128)(2,1)S(1)} %project.9.refs_1_, bf16[768,512]{1,0:T(8,128)(2,1)} %get-tuple-element.57.refs_2_, f32[768,512]{1,0:T(8,128)} %get-tuple-element.58.refs_3_, ...), custom_call_target="tpu_custom_call" | custom-call | flops 1048576 | bytes 1048576 | tf_op jit(solution)/shard_map/backward_past/pallas_call | solution.py:445
  91.9 1.7 %collective-permute-done.13.crossed_ref = bf16[1536,128]{1,0:T(8,128)(2,1)S(1)} collective-permute-done((bf16[1536,128]{1,0:T(8,128)(2,1)S(1)}, bf16[1536,128]{1,0:T(8,128)(2,1)S(1)}, u32[]{:S(2)}, u32[]{:S(2)}) %collective-permute-start.13) | collective-permute-done | bytes 393248 | tf_op jit(solution)/shard_map/ppermute | solution.py:33
  93.7 1.5 %collective-permute-start.14 = (bf16[1536,128]{1,0:T(8,128)(2,1)S(1)}, bf16[1536,128]{1,0:T(8,128)(2,1)S(1)}, u32[]{:S(2)}, u32[]{:S(2)}) collective-permute-start(bf16[1536,128]{1,0:T(8,128)(2,1)S(1)} %send.1), channel_id=1, source_target_pairs={{16,0},{24,8},{32,16},{40,24},{48,32},{56,40},{64,48},{72,56},{80,... | collective-permute-start | bytes 1179656 | tf_op jit(solution)/shard_map/ppermute | solution.py:20
  95.2 7.1 %backward_own.1 = (bf16[768,512]{1,0:T(8,128)(2,1)}, f32[1536,128]{1,0:T(8,128)S(1)}) custom-call(bf16[768,512]{1,0:T(8,128)(2,1)} %refs_0_.1, bf16[768,512]{1,0:T(8,128)(2,1)S(1)} %project.9.refs_1_, bf16[768,512]{1,0:T(8,128)(2,1)} %get-tuple-element.57.refs_2_, f32[768,512]{1,0:T(8,128)} %get-tuple-element.58.refs_3_, ...), custom_call_target="tpu_custom_call" | custom-call | flops 1048576 | bytes 1048576 | tf_op jit(solution)/shard_map/backward_own/pallas_call | solution.py:460
  102.3 5.1 %all-to-all-done = bf16[8,512,256]{2,1,0:T(8,128)(2,1)} async-done(((bf16[8,512,256]{2,1,0:T(8,128)(2,1)}), bf16[8,512,256]{2,1,0:T(8,128)(2,1)}, u32[]{:S(2)}, u32[]{:S(2)}) %all-to-all-start) | async-done | bytes 2097184 | tf_op jit(solution)/shard_map/all_to_all | solution.py:440
  107.4 2.6 %reduce_sum.12 = bf16[512,256]{1,0:T(8,128)(2,1)} reduce(bf16[8,512,256]{2,1,0:T(8,128)(2,1)} %all-to-all-done, bf16[]{:T(256)} %constant.73.clone.1), dimensions={0}, to_apply=%region_0.1 | reduce | flops 917504 | bytes 2359298 | tf_op jit(solution)/shard_map/reduce_sum | solution.py:441
  110.0 3.3 %collective-permute-done.14.come_ref = bf16[1536,128]{1,0:T(8,128)(2,1)S(1)} collective-permute-done((bf16[1536,128]{1,0:T(8,128)(2,1)S(1)}, bf16[1536,128]{1,0:T(8,128)(2,1)S(1)}, u32[]{:S(2)}, u32[]{:S(2)}) %collective-permute-start.14) | collective-permute-done | bytes 393248 | tf_op jit(solution)/shard_map/ppermute | solution.py:20
  113.4 0.8 finish.1
  (29 shorter events, 4.8 us)
Async XLA Ops:
  2.4 13.2 %collective-permute-start = (bf16[1552,128]{1,0:T(8,128)(2,1)S(1)}, bf16[1552,128]{1,0:T(8,128)(2,1)S(1)}, u32[]{:S(2)}, u32[]{:S(2)}) collective-permute-start(bf16[1552,128]{1,0:T(8,128)(2,1)S(1)} %fusion.1.refs_5_.refs_7_), channel_id=1, source_target_pairs={{0,16},{8,24},{16,32},{24,40},{32,48},{40,56},{48,64},{56,72},{64,... | collective-permute-start | bytes 1191944 | tf_op jit(solution)/shard_map/ppermute | solution.py:20
  6.0 9.6 %collective-permute-start.1 = (bf16[1552,128]{1,0:T(8,128)(2,1)S(1)}, bf16[1552,128]{1,0:T(8,128)(2,1)S(1)}, u32[]{:S(2)}, u32[]{:S(2)}) collective-permute-start(bf16[1552,128]{1,0:T(8,128)(2,1)S(1)} %fusion.1.refs_5_.refs_7_), channel_id=1, source_target_pairs={{0,8},{8,16},{16,24},{24,32},{32,40},{40,48},{48,56},{56,64},{64,7... | collective-permute-start | bytes 1191944 | tf_op jit(solution)/shard_map/ppermute | solution.py:20
  7.5 29.6 %collective-permute-start.3 = (bf16[768,512]{1,0:T(8,128)(2,1)}, bf16[768,512]{1,0:T(8,128)(2,1)}, u32[]{:S(2)}, u32[]{:S(2)}) collective-permute-start(bf16[768,512]{1,0:T(8,128)(2,1)} %refs_3_.1), channel_id=1, source_target_pairs={{0,2},{1,3},{2,0},{3,1},{4,6},{5,7},{6,4},{7,5},{8,10},{9,11},{10,... | collective-permute-start | bytes 2359304 | tf_op jit(solution)/shard_map/ppermute | solution.py:25
  15.5 21.6 %collective-permute-start.2 = (bf16[768,512]{1,0:T(8,128)(2,1)}, bf16[768,512]{1,0:T(8,128)(2,1)}, u32[]{:S(2)}, u32[]{:S(2)}) collective-permute-start(bf16[768,512]{1,0:T(8,128)(2,1)} %refs_3_.1), channel_id=1, source_target_pairs={{0,4},{1,5},{2,6},{3,7},{4,0},{5,1},{6,2},{7,3},{8,12},{9,13},{10,... | collective-permute-start | bytes 2359304 | tf_op jit(solution)/shard_map/ppermute | solution.py:29
  18.4 28.7 %collective-permute-start.8 = (bf16[768,512]{1,0:T(8,128)(2,1)}, bf16[768,512]{1,0:T(8,128)(2,1)S(1)}, u32[]{:S(2)}, u32[]{:S(2)}) collective-permute-start(bf16[768,512]{1,0:T(8,128)(2,1)} %refs_3_.1), channel_id=1, source_target_pairs={{0,1},{1,2},{2,3},{3,0},{4,5},{5,6},{6,7},{7,4},{8,9},{9,10},{10,1... | collective-permute-start | bytes 2359304 | tf_op jit(solution)/shard_map/ppermute | solution.py:25
  19.9 29.6 %collective-permute-start.9 = (bf16[768,512]{1,0:T(8,128)(2,1)}, bf16[768,512]{1,0:T(8,128)(2,1)}, u32[]{:S(2)}, u32[]{:S(2)}) collective-permute-start(bf16[768,512]{1,0:T(8,128)(2,1)} %refs_3_.1), channel_id=1, source_target_pairs={{0,3},{1,0},{2,1},{3,2},{4,7},{5,4},{6,5},{7,6},{8,11},{9,8},{10,9... | collective-permute-start | bytes 2359304 | tf_op jit(solution)/shard_map/ppermute | solution.py:25
  22.6 1.1 copy-start
  37.1 19.7 %collective-permute-start.6 = (bf16[768,512]{1,0:T(8,128)(2,1)}, bf16[768,512]{1,0:T(8,128)(2,1)}, u32[]{:S(2)}, u32[]{:S(2)}) collective-permute-start(bf16[768,512]{1,0:T(8,128)(2,1)} %collective-permute-done.3.refs_4_), channel_id=1, source_target_pairs={{0,4},{1,5},{2,6},{3,7},{4,0},{5,1},{6,2},{7,3},{8,12},{9,13},{10,... | collective-permute-start | bytes 2359304 | tf_op jit(solution)/shard_map/ppermute | solution.py:29
  37.9 25.5 %collective-permute-start.4 = (bf16[768,512]{1,0:T(8,128)(2,1)}, bf16[768,512]{1,0:T(8,128)(2,1)}, u32[]{:S(2)}, u32[]{:S(2)}) collective-permute-start(bf16[768,512]{1,0:T(8,128)(2,1)} %collective-permute-done.2.refs_5_), channel_id=1, source_target_pairs={{0,1},{1,2},{2,3},{3,0},{4,5},{5,6},{6,7},{7,4},{8,9},{9,10},{10,1... | collective-permute-start | bytes 2359304 | tf_op jit(solution)/shard_map/ppermute | solution.py:25
  38.8 24.6 %collective-permute-start.5 = (bf16[768,512]{1,0:T(8,128)(2,1)}, bf16[768,512]{1,0:T(8,128)(2,1)}, u32[]{:S(2)}, u32[]{:S(2)}) collective-permute-start(bf16[768,512]{1,0:T(8,128)(2,1)} %collective-permute-done.2.refs_5_), channel_id=1, source_target_pairs={{0,3},{1,0},{2,1},{3,2},{4,7},{5,4},{6,5},{7,6},{8,11},{9,8},{10,9... | collective-permute-start | bytes 2359304 | tf_op jit(solution)/shard_map/ppermute | solution.py:25
  46.3 0.9 copy-start.1
  47.2 2.4 %copy-start.3 = (bf16[768,512]{1,0:T(8,128)(2,1)}, bf16[768,512]{1,0:T(8,128)(2,1)S(1)}, u32[]{:S(2)}) copy-start(bf16[768,512]{1,0:T(8,128)(2,1)S(1)} %collective-permute-done.8.refs_3_) | copy-start | bytes 2359300
  47.2 16.2 %collective-permute-start.7 = (bf16[3,512,256]{2,1,0:T(8,128)(2,1)S(1)}, bf16[3,512,256]{2,1,0:T(8,128)(2,1)}, u32[]{:S(2)}, u32[]{:S(2)}) collective-permute-start(bf16[3,512,256]{2,1,0:T(8,128)(2,1)S(1)} %get-tuple-element.46), channel_id=1, source_target_pairs={{0,8},{8,0},{16,24},{24,16},{32,40},{40,32},{48,56},{56,48},{64,72... | collective-permute-start | bytes 2359304 | tf_op jit(solution)/shard_map/ppermute | solution.py:33
  54.6 0.8 copy-start.2
  55.4 8.0 %collective-permute-start.10 = (bf16[2,512,256]{2,1,0:T(8,128)(2,1)}, bf16[2,512,256]{2,1,0:T(8,128)(2,1)}, u32[]{:S(2)}, u32[]{:S(2)}) collective-permute-start(bf16[2,512,256]{2,1,0:T(8,128)(2,1)} %get-tuple-element.49), channel_id=1, source_target_pairs={{0,8},{8,0},{16,24},{24,16},{32,40},{40,32},{48,56},{56,48},{64,72... | collective-permute-start | bytes 1572872 | tf_op jit(solution)/shard_map/ppermute | solution.py:33
  68.2 2.4 %collective-permute-start.11 = (bf16[2,512,256]{2,1,0:T(8,128)(2,1)S(1)}, bf16[2,512,256]{2,1,0:T(8,128)(2,1)S(1)}, u32[]{:S(2)}, u32[]{:S(2)}) collective-permute-start(bf16[2,512,256]{2,1,0:T(8,128)(2,1)S(1)} %get-tuple-element.51), channel_id=1, source_target_pairs={{0,8},{8,0},{16,24},{24,16},{32,40},{40,32},{48,56},{56,48},{64,72... | collective-permute-start | bytes 1572872 | tf_op jit(solution)/shard_map/ppermute | solution.py:33
  68.4 2.2 %collective-permute-start.12 = (bf16[1,512,256]{2,1,0:T(8,128)(2,1)S(1)}, bf16[1,512,256]{2,1,0:T(8,128)(2,1)S(1)}, u32[]{:S(2)}, u32[]{:S(2)}) collective-permute-start(bf16[1,512,256]{2,1,0:T(8,128)(2,1)S(1)} %get-tuple-element.53), channel_id=1, source_target_pairs={{0,8},{8,0},{16,24},{24,16},{32,40},{40,32},{48,56},{56,48},{64,72... | collective-permute-start | bytes 786440 | tf_op jit(solution)/shard_map/ppermute | solution.py:33
  72.1 35.3 %all-to-all-start = ((bf16[8,512,256]{2,1,0:T(8,128)(2,1)}), bf16[8,512,256]{2,1,0:T(8,128)(2,1)}, u32[]{:S(2)}, u32[]{:S(2)}) async-start(bf16[8,512,256]{2,1,0:T(8,128)(2,1)} %place.1), calls=%async_computation | async-start | bytes 4194304 | tf_op jit(solution)/shard_map/all_to_all | solution.py:440
  91.8 1.8 %collective-permute-start.13 = (bf16[1536,128]{1,0:T(8,128)(2,1)S(1)}, bf16[1536,128]{1,0:T(8,128)(2,1)S(1)}, u32[]{:S(2)}, u32[]{:S(2)}) collective-permute-start(bf16[1536,128]{1,0:T(8,128)(2,1)S(1)} %get-tuple-element.65), channel_id=1, source_target_pairs={{0,8},{8,0},{16,24},{24,16},{32,40},{40,32},{48,56},{56,48},{64,72... | collective-permute-start | bytes 1179656 | tf_op jit(solution)/shard_map/ppermute | solution.py:33
  93.7 19.6 %collective-permute-start.14 = (bf16[1536,128]{1,0:T(8,128)(2,1)S(1)}, bf16[1536,128]{1,0:T(8,128)(2,1)S(1)}, u32[]{:S(2)}, u32[]{:S(2)}) collective-permute-start(bf16[1536,128]{1,0:T(8,128)(2,1)S(1)} %send.1), channel_id=1, source_target_pairs={{16,0},{24,8},{32,16},{40,24},{48,32},{56,40},{64,48},{72,56},{80,... | collective-permute-start | bytes 1179656 | tf_op jit(solution)/shard_map/ppermute | solution.py:20
